TPU v7x, 256 devices: a whole 4x4x8 slice. The times are simulated.
256 devices in a mesh: row: 8 (over x, z_lo), col: 32 (over y, z_hi, core).
Axes of the slice: x: 4, y: 4, z: 8 (z_hi: 4, z_lo: 2; z = z_hi * 2 + z_lo), core: 2. Of those that a mesh axis runs over, the one named last changes fastest.
Arguments:
- queries: bfloat16 [32768, 1024], P(('row', 'col')), may hold values from -24 to 24
- query_exps: int32 [32768], P(('row', 'col')), may hold values from -1 to 3
- key_head: bfloat16 [32768, 128], P(('col', 'row')), may hold values from -5 to 5
- value_head: bfloat16 [32768, 128], P(('col', 'row')), may hold values from -6 to 6
- forward_out: bfloat16 [32768, 1024], P(('row', 'col')), may hold values from -6 to 6
- output_grad: bfloat16 [32768, 1024], P(('row', 'col')), may hold values from -6 to 6
- stripe_order: int32 [256], replicated, may hold values from 0 to 255, each once
- window_size: int32 [1], replicated, may hold values from 4096 to 8192
Outputs:
- query_grad: bfloat16 [32768, 1024], P(('row', 'col'))
- key_grad: bfloat16 [32768, 128], P(('col', 'row'))
- value_grad: bfloat16 [32768, 128], P(('col', 'row'))
Inputs may be any that keep to these rules, and one draw needn't show every extreme that they name: `stripe_order`: each stripe number appears once.
All inputs are finite; a program needn't handle non-finite values.
Results may differ from a plain program's by a relative error of at most 0.0095.
Values may be sent and summed in bfloat16 or wider, within the bound.
A program may use at most 128 MiB of HBM per device.

v0:
```python
import math

import jax
import jax.numpy as jnp
from jax import lax
from jax.sharding import PartitionSpec as P

STRIPE = 128


pair_block = 8
neg_big = -1e30


def from_everyone(value, axis):
    copies = jnp.broadcast_to(value, (lax.axis_size(axis), *value.shape))
    return lax.all_to_all(copies, axis, split_axis=0, concat_axis=0, tiled=True)


def in_order(parts, dim):
    lengths = list(parts.shape[1:])
    lengths[dim] *= parts.shape[0]
    return jnp.moveaxis(parts, 0, dim).reshape(lengths)


def collect(value, axis, dim):
    parts = from_everyone(value, axis)
    return in_order(parts, dim)


def side_by_side(arrays, axis, dim, along):
    widths = [a.shape[along] for a in arrays]
    both = jnp.concatenate(arrays, axis=along)
    whole = lax.all_gather(both, axis, axis=dim, tiled=True)
    return tuple(jnp.split(whole, [sum(widths[:k]) for k in range(1, len(widths))], axis=along))


def gathered_once(value, axis):
    leaves = jax.tree.leaves(value)
    turns = sorted(range(len(leaves)), key=lambda k: -leaves[k].size)
    width = (1, *leaves[turns[0]].shape)[-1]
    lines = [
        jnp.pad(leaves[k].reshape(-1), (0, -leaves[k].size % width)).reshape(-1, width)
        for k in turns
    ]
    both, at, found = (from_everyone(jnp.concatenate(lines), axis), 0, {})
    for k, line in zip(turns, lines):
        section = both[:, at : at + len(line)].reshape(len(both), -1)
        found[k] = section[:, : leaves[k].size].reshape(-1, *leaves[k].shape)
        at += len(line)
    numbers = iter(range(len(leaves)))
    return jax.tree.map(lambda _: found[next(numbers)], value)


def combined_pairwise(pieces, combine):
    while len(jax.tree.leaves(pieces)[0]) > 1:
        pieces = jax.vmap(combine)(
            *(jax.tree.map(lambda part: part[side::2], pieces) for side in (0, 1))
        )
    return jax.tree.map(lambda part: part[0], pieces)


def merged(value, axis, combine):
    pieces = gathered_once(value, axis)
    return combined_pairwise(pieces, combine)


def split_up(value, dim, devices):
    before, after = (value.shape[:dim], value.shape[dim + 1 :])
    return jnp.moveaxis(value.reshape(*before, devices, -1, *after), dim, 0)


def sent_and_summed(value, axis, dim):
    parts = split_up(value, dim, lax.axis_size(axis))
    arrived = lax.all_to_all(parts, axis, split_axis=0, concat_axis=0, tiled=True)
    return arrived.astype(jnp.float32).sum(axis=0)


def in_one_piece(arrays, axis, dim, along):
    ends, at = ([], 0)
    for a in arrays[:-1]:
        at += a.shape[along]
        ends.append(at)
    both = jnp.concatenate(arrays, axis=along)
    return tuple(
        jnp.split(lax.psum_scatter(both, axis, scatter_dimension=dim, tiled=True), ends, axis=along)
    )


def pair_list(q_start, k_start, window_len):
    distance = q_start[:, None] - k_start[None, :]
    usable = ((distance >= 0) & (distance - (STRIPE - 1) < window_len)).reshape(-1)
    padded_len = -(-usable.shape[0] // pair_block) * pair_block
    live_count = jnp.sum(usable.astype(jnp.int32))
    pair_order = jnp.nonzero(usable, size=padded_len, fill_value=0)[0].astype(jnp.int32)
    turn_count = (live_count + pair_block - 1) // pair_block
    return (pair_order, live_count, turn_count)


def pick_batch(pair_order, live_count, offset, k_stripes):
    pair_ids = lax.dynamic_slice_in_dim(pair_order, offset, pair_block)
    in_range = offset + jnp.arange(pair_block, dtype=jnp.int32) < live_count
    return (pair_ids // k_stripes, pair_ids % k_stripes, in_range)


def tile_keep(q_first, k_first, in_range, window_len):
    offsets = jnp.arange(STRIPE, dtype=jnp.int32)
    distance = (
        q_first[:, None, None]
        + offsets[None, :, None]
        - (k_first[:, None, None] + offsets[None, None, :])
    )
    visible = (distance >= 0) & (distance < window_len) & in_range[:, None, None]
    return visible[:, None, :, :]


def merge_stats(first_pair, second_pair):
    highest = jnp.maximum(first_pair[0], second_pair[0])
    summed = first_pair[1] * jnp.exp(first_pair[0] - highest) + second_pair[1] * jnp.exp(
        second_pair[0] - highest
    )
    return (highest, summed)


def head_sums(grads, outputs, head_count):
    row_count, feat_width = grads.shape
    product = grads.astype(jnp.float32) * outputs.astype(jnp.float32)
    return (
        product.reshape(row_count, head_count, feat_width // head_count)
        .sum(-1)
        .astype(jnp.bfloat16)
    )


def per_device(
    queries, query_exps, key_head, value_head, forward_out, output_grad, stripe_order, window_size
):
    head_dim = key_head.shape[1]
    feat_width = queries.shape[1]
    head_count = feat_width // head_dim
    inv_scale = 1.0 / math.sqrt(head_dim)
    window_len = window_size[0]
    row_count = lax.axis_size("row")
    col_count = lax.axis_size("col")
    own_stripes = queries.shape[0] // STRIPE
    scaled = (
        queries.astype(jnp.float32) * jnp.exp2(query_exps.astype(jnp.float32))[:, None]
    ).astype(jnp.bfloat16)
    delta_own = head_sums(output_grad, forward_out, head_count)
    q_panel = collect(scaled, "row", 0)
    k_panel, v_panel = side_by_side((key_head, value_head), "col", 0, 1)
    q_stripes = q_panel.shape[0] // STRIPE
    k_stripes = k_panel.shape[0] // STRIPE
    query_tiles = q_panel.reshape(q_stripes, STRIPE, feat_width)
    key_tiles = k_panel.reshape(k_stripes, STRIPE, head_dim)
    value_tiles = v_panel.reshape(k_stripes, STRIPE, head_dim)
    order_by_row = stripe_order.reshape(row_count, col_count, own_stripes)
    q_start = (
        lax.dynamic_index_in_dim(order_by_row, lax.axis_index("col"), 1, keepdims=False).reshape(-1)
        * STRIPE
    )
    order_by_col = stripe_order.reshape(col_count, row_count, own_stripes)
    k_start = (
        lax.dynamic_index_in_dim(order_by_col, lax.axis_index("row"), 1, keepdims=False).reshape(-1)
        * STRIPE
    )
    pair_order, live_count, turn_count = pair_list(q_start, k_start, window_len)

    def visible_scores(offset, first_stripe, order_now, count_now):
        q_local, k_index, in_range = pick_batch(order_now, count_now, offset, k_stripes)
        q_index = first_stripe + q_local
        query_rows = query_tiles[q_index]
        key_rows = key_tiles[k_index]
        batch_size = query_rows.shape[0]
        query_split = query_rows.reshape(batch_size, STRIPE, head_count, head_dim)
        scores = (
            jnp.einsum("bihd,bjd->bhij", query_split, key_rows, preferred_element_type=jnp.float32)
            * inv_scale
        )
        visible = tile_keep(q_start[q_index], k_start[k_index], in_range, window_len)
        return (q_local, q_index, k_index, query_split, key_rows, scores, visible)

    def add_stats(turn, state):
        highest, normaliser = state
        parts = visible_scores(turn * pair_block, 0, pair_order, live_count)
        q_index, scores, visible = (parts[1], parts[5], parts[6])
        tile_max = jnp.max(jnp.where(visible, scores, neg_big), axis=3)
        raised = highest.at[q_index].max(tile_max)
        normaliser = normaliser * jnp.exp(highest - raised)
        shifted = jnp.where(visible, scores - raised[q_index][..., None], neg_big)
        return (raised, normaliser.at[q_index].add(jnp.sum(jnp.exp(shifted), axis=3)))

    start_max = jnp.full((q_stripes, head_count, STRIPE), neg_big, jnp.float32)
    highest, normaliser = lax.fori_loop(
        0, turn_count, add_stats, (start_max, jnp.zeros_like(start_max))
    )
    highest, normaliser = merged((highest, normaliser), "row", merge_stats)
    log_norm = highest + jnp.log(normaliser)
    start_sums = (
        jnp.zeros((q_stripes, STRIPE, feat_width), jnp.float32),
        jnp.zeros((k_stripes, STRIPE, head_dim), jnp.float32),
        jnp.zeros((k_stripes, STRIPE, head_dim), jnp.float32),
    )
    pieces = side_by_side((output_grad, delta_own), "row", 0, 1)
    grad_piece = pieces[0]
    piece_stripes = grad_piece.shape[0] // STRIPE
    first_stripe = jnp.int32(0) // STRIPE
    delta_tiles = pieces[1].reshape(piece_stripes, STRIPE, head_count)
    grad_tiles = grad_piece.reshape(piece_stripes, STRIPE, feat_width)
    order_now, count_now, turns_now = pair_list(q_start, k_start, window_len)

    def add_grads(turn, sums):
        query_sum, key_sum, value_sum = sums
        q_local, q_index, k_index, query_split, key_rows, scores, visible = visible_scores(
            turn * pair_block, first_stripe, order_now, count_now
        )
        weights = jnp.exp(jnp.where(visible, scores - log_norm[q_index][..., None], neg_big))
        rounded_weights = weights.astype(jnp.bfloat16)
        grad_rows = grad_tiles[q_local]
        batch_size = grad_rows.shape[0]
        grad_split = grad_rows.reshape(batch_size, STRIPE, head_count, head_dim)
        weight_grad = jnp.einsum(
            "bihd,bjd->bhij", grad_split, value_tiles[k_index], preferred_element_type=jnp.float32
        )
        delta_now = jnp.transpose(delta_tiles[q_local].astype(jnp.float32), (0, 2, 1))[..., None]
        score_grad = (weights * (weight_grad - delta_now)).astype(jnp.bfloat16)
        query_part = (
            jnp.einsum("bhij,bjd->bihd", score_grad, key_rows, preferred_element_type=jnp.float32)
            * inv_scale
        )
        key_part = (
            jnp.einsum(
                "bhij,bihd->bjd", score_grad, query_split, preferred_element_type=jnp.float32
            )
            * inv_scale
        )
        value_part = jnp.einsum(
            "bhij,bihd->bjd", rounded_weights, grad_split, preferred_element_type=jnp.float32
        )
        query_sum = query_sum.at[q_index].add(query_part.reshape(batch_size, STRIPE, feat_width))
        return (query_sum, key_sum.at[k_index].add(key_part), value_sum.at[k_index].add(value_part))

    sums = lax.fori_loop(0, turns_now, add_grads, start_sums)
    query_sum, key_sum, value_sum = sums
    query_grad = sent_and_summed(
        query_sum.reshape(-1, feat_width).astype(jnp.bfloat16), "row", 0
    ).astype(jnp.bfloat16)
    key_grad, value_grad = in_one_piece(
        (key_sum.reshape(-1, head_dim), value_sum.reshape(-1, head_dim)), "col", 0, 1
    )
    return (query_grad, key_grad.astype(jnp.bfloat16), value_grad.astype(jnp.bfloat16))


def solution(mesh):
    return jax.shard_map(
        per_device,
        mesh=mesh,
        in_specs=(
            P(("row", "col"), None),
            P(("row", "col")),
            P(("col", "row"), None),
            P(("col", "row"), None),
            P(("row", "col"), None),
            P(("row", "col"), None),
            P(),
            P(),
        ),
        out_specs=(P(("row", "col"), None), P(("col", "row"), None), P(("col", "row"), None)),
        check_vma=False,
    )
```

profile of v0, /device:TPU:4, one launch (start us, length us, event | category | flops | bytes accessed | tf_op | source)
XLA Modules:
  0.0 755.1 jit_solution(9260675178856520706)
XLA Ops:
  11.9 6.3 all-to-all-start
  26.8 42.5 %all-gather.3.cloned.1.call-done = bf16[4096,256]{1,0:T(8,128)(2,1)} async-done(((bf16[128,256]{1,0:T(8,128)(2,1)}), bf16[4096,256]{1,0:T(8,128)(2,1)}) %all-gather.3.cloned.1.call-update) | async-done | bytes 2097168 | tf_op jit(solution)/shard_map/all_gather | solution.py:34
  69.3 3.0 fusion.59
  72.3 102.1 %while.30 = (s32[]{:T(128)}, f32[8,8,128]{2,1,0:T(8,128)S(1)}, f32[8,8,128]{2,1,0:T(8,128)S(1)}, s32[]{:T(128)}, s32[256]{0:T(256)S(1)}, /*index=5*/s32[8]{0:T(1...) while((s32[]{:T(128)}, f32[8,8,128]{2,1,0:T(8,128)S(1)}, ...), condition=%wide.region_11.12_spmd, body=%wide.region_6.11_spmd.sunk | while | flops 276451584 | bytes 16507775 | solution.py:194
  79.2 4.5 fusion.93
  85.1 3.4 fusion.94
  96.3 4.5 fusion.93
  102.2 3.4 fusion.94
  113.4 4.5 fusion.93
  119.2 3.4 fusion.94
  130.4 4.5 fusion.93
  136.2 3.4 fusion.94
  147.4 4.5 fusion.93
  153.2 3.4 fusion.94
  164.4 4.5 fusion.93
  170.2 3.4 fusion.94
  175.3 37.9 %all-to-all-start.1 = ((f32[8,128,128]{2,1,0:T(8,128)}), f32[8,128,128]{2,1,0:T(8,128)S(1)}, u32[]{:S(2)}, u32[]{:S(2)}) async-start(f32[8,128,128]{2,1,0:T(8,128)} %broadcast_in_dim.134), calls=%async_computation.1 | async-start | bytes 1048576 | tf_op jit(solution)/shard_map/all_to_all | solution.py:17
  213.2 3.1 split.28
  216.3 3.9 copy.81
  226.8 268.0 %while.31 = (s32[]{:T(128)}, f32[8,128,1024]{2,1,0:T(8,128)}, f32[32,128,128]{2,1,0:T(8,128)}, f32[32,128,128]{2,1,0:T(8,128)}, s32[]{:T(128)}, /*index=5*/s32[2...) while((s32[]{:T(128)}, f32[8,128,1024]{2,1,0:T(8,128)}, ...), condition=%wide.region_17.18_spmd, body=%wide.region_13.17_spmd.sunk | while | flops 1355821312 | bytes 92677248 | solution.py:243
  234.7 3.6 gather_fusion.12
  253.1 4.3 convolution_multiply_fusion.2
  257.5 5.3 copy.125
  262.8 8.6 %scatter_fusion.2 = f32[8,128,1024]{2,1,0:T(8,128)} fusion(f32[8,128,1024]{2,1,0:T(8,128)} %get-tuple-element.771, s32[8]{0:T(128)S(1)} %compare_select_fusion.23, f32[8,128,1024]{2,1,0:T(8,128)} %copy.125), kind=kCustom, calls=%fused_computation.15.clone.1 | custom fusion | flops 1048576 | bytes 12582944 | tf_op jit(solution)/shard_map/while/body/scatter-add | solution.py:240
  279.3 3.6 gather_fusion.12
  297.7 4.3 convolution_multiply_fusion.2
  302.0 5.3 copy.125
  307.3 8.5 %scatter_fusion.2 = f32[8,128,1024]{2,1,0:T(8,128)} fusion(f32[8,128,1024]{2,1,0:T(8,128)} %get-tuple-element.771, s32[8]{0:T(128)S(1)} %compare_select_fusion.23, f32[8,128,1024]{2,1,0:T(8,128)} %copy.125), kind=kCustom, calls=%fused_computation.15.clone.1 | custom fusion | flops 1048576 | bytes 12582944 | tf_op jit(solution)/shard_map/while/body/scatter-add | solution.py:240
  323.7 3.6 gather_fusion.12
  342.1 4.3 convolution_multiply_fusion.2
  346.5 5.3 copy.125
  351.8 8.7 %scatter_fusion.2 = f32[8,128,1024]{2,1,0:T(8,128)} fusion(f32[8,128,1024]{2,1,0:T(8,128)} %get-tuple-element.771, s32[8]{0:T(128)S(1)} %compare_select_fusion.23, f32[8,128,1024]{2,1,0:T(8,128)} %copy.125), kind=kCustom, calls=%fused_computation.15.clone.1 | custom fusion | flops 1048576 | bytes 12582944 | tf_op jit(solution)/shard_map/while/body/scatter-add | solution.py:240
  368.4 3.6 gather_fusion.12
  386.8 4.3 convolution_multiply_fusion.2
  391.1 5.3 copy.125
  396.5 8.8 %scatter_fusion.2 = f32[8,128,1024]{2,1,0:T(8,128)} fusion(f32[8,128,1024]{2,1,0:T(8,128)} %get-tuple-element.771, s32[8]{0:T(128)S(1)} %compare_select_fusion.23, f32[8,128,1024]{2,1,0:T(8,128)} %copy.125), kind=kCustom, calls=%fused_computation.15.clone.1 | custom fusion | flops 1048576 | bytes 12582944 | tf_op jit(solution)/shard_map/while/body/scatter-add | solution.py:240
  413.1 3.6 gather_fusion.12
  431.5 4.3 convolution_multiply_fusion.2
  435.9 5.3 copy.125
  441.2 9.0 %scatter_fusion.2 = f32[8,128,1024]{2,1,0:T(8,128)} fusion(f32[8,128,1024]{2,1,0:T(8,128)} %get-tuple-element.771, s32[8]{0:T(128)S(1)} %compare_select_fusion.23, f32[8,128,1024]{2,1,0:T(8,128)} %copy.125), kind=kCustom, calls=%fused_computation.15.clone.1 | custom fusion | flops 1048576 | bytes 12582944 | tf_op jit(solution)/shard_map/while/body/scatter-add | solution.py:240
  458.1 3.6 gather_fusion.12
  476.5 4.3 convolution_multiply_fusion.2
  480.8 5.3 copy.125
  486.1 8.7 %scatter_fusion.2 = f32[8,128,1024]{2,1,0:T(8,128)} fusion(f32[8,128,1024]{2,1,0:T(8,128)} %get-tuple-element.771, s32[8]{0:T(128)S(1)} %compare_select_fusion.23, f32[8,128,1024]{2,1,0:T(8,128)} %copy.125), kind=kCustom, calls=%fused_computation.15.clone.1 | custom fusion | flops 1048576 | bytes 12582944 | tf_op jit(solution)/shard_map/while/body/scatter-add | solution.py:240
  494.9 4.4 pad_maximum_fusion
  501.8 107.9 %all_to_all.15 = bf16[8,128,1024]{2,1,0:T(8,128)(2,1)} all-to-all(bf16[8,128,1024]{2,1,0:T(8,128)(2,1)S(1)} %convert_element_type.69), channel_id=1, replica_groups=mesh['row'=8,'col'=32] {'row'}, dimensions={0} | all-to-all | bytes 4194304 | tf_op jit(solution)/shard_map/all_to_all | solution.py:75
  609.7 2.7 reduce_sum.56
  612.4 134.6 %reduce-scatter.2.cloned.1.call-done = f32[128,256]{1,0:T(8,128)} async-done(((f32[4096,256]{1,0:T(8,128)}), f32[128,256]{1,0:T(8,128)}) %reduce-scatter.2.cloned.1.call-update) | async-done | bytes 131088 | tf_op jit(solution)/shard_map/reduce_scatter | solution.py:86
  (328 shorter events, 213.2 us)
Async XLA Ops:
  7.2 62.1 %all-gather.3.cloned.1.call-start = ((), (), s32[]{:S(2)}) async-start(), calls=%async_computation.4 | async-start | bytes 2162688 | tf_op jit(solution)/shard_map/all_gather | solution.py:34
  11.9 6.3 copy-start.3
  11.9 6.5 copy-start.4
  11.9 60.3 %all-to-all-start = ((bf16[8,128,1024]{2,1,0:T(8,128)(2,1)}), bf16[8,128,1024]{2,1,0:T(8,128)(2,1)S(1)}, u32[]{:S(2)}, u32[]{:S(2)}) async-start(bf16[8,128,1024]{2,1,0:T(8,128)(2,1)} %broadcast_in_dim.131), calls=%async_computation | async-start | bytes 4194304 | tf_op jit(solution)/shard_map/all_to_all | solution.py:17
  18.2 1.5 copy-start.5
  18.2 195.0 %all-gather.5.cloned.1.call-start = ((), (), s32[]{:S(2)}) async-start(), calls=%async_computation.5 | async-start | bytes 2377728 | tf_op jit(solution)/shard_map/all_gather | solution.py:34
  175.3 45.7 %all-to-all-start.1 = ((f32[8,128,128]{2,1,0:T(8,128)}), f32[8,128,128]{2,1,0:T(8,128)S(1)}, u32[]{:S(2)}, u32[]{:S(2)}) async-start(f32[8,128,128]{2,1,0:T(8,128)} %broadcast_in_dim.134), calls=%async_computation.1 | async-start | bytes 1048576 | tf_op jit(solution)/shard_map/all_to_all | solution.py:17
  213.2 533.8 %reduce-scatter.2.cloned.1.call-start = ((), (), s32[]{:S(2)}) async-start(), calls=%async_computation.6 | async-start | bytes 4325376 | tf_op jit(solution)/shard_map/reduce_scatter | solution.py:86
  240.3 2.5 copy-start.2
  244.0 3.0 copy-start
  245.7 1.4 copy-start.1
  284.9 2.5 copy-start.2
  288.6 3.0 copy-start
  290.3 1.4 copy-start.1
  329.3 2.5 copy-start.2
  333.0 3.0 copy-start
  334.7 1.4 copy-start.1
  374.0 2.5 copy-start.2
  377.7 3.0 copy-start
  379.4 1.4 copy-start.1
  418.7 2.5 copy-start.2
  422.4 3.0 copy-start
  424.1 1.4 copy-start.1
  463.7 2.5 copy-start.2
  467.4 3.0 copy-start
  469.1 1.4 copy-start.1
Sparse Core Ops, SparseCore 0:
  11.1 58.1 all-gather.2
  71.0 50.7 all-gather.4
  499.4 247.5 reduce-scatter.1
where the time goes:
time: 760 us; the launch traced here: 755 us
  waiting for transfers between devices  177 us (23%)
  local copies, waits for them, and re-layouts  165 us (22%)
  other arithmetic  155 us (20%)
  blocking collectives  108 us (14%)
  matrix products  89 us (12%)
  starting transfers between devices  44.3 us (6%)
  between operations  15.2 us (2%)
    reduce_scatter x1, waiting for transfers between devices, in_one_piece(): lax.psum_scatter(both, axis, scatter_dimension=dim, tiled=True)  135 us
    all_to_all x1, blocking collectives, sent_and_summed(): lax.all_to_all(parts, axis, split_axis=0, concat_axis=0, tiled=True)  108 us
    scatter-add x6, other arithmetic, add_grads(): query_sum.at[q_index]  52.3 us
    all_to_all x2, starting transfers between devices, from_everyone(): return lax.all_to_all(copies, axis, split_axis=0, concat_axis=0, tiled=True)  44.2 us
    all_gather x2, waiting for transfers between devices, side_by_side(): whole = lax.all_gather(both, axis, axis=dim, tiled=True)  42.5 us
    dot_general x12, matrix products, visible_scores(): jnp.einsum('bihd,bjd->bhij', query_split, key_rows, preferred_element_typ...  41.7 us
    reshape x6, local copies, waits for them, and re-layouts, add_grads(): query_part.reshape(batch_size, STRIPE, feat_width)  32.1 us
    dot_general x6, matrix products, add_grads(): jnp.einsum('bhij,bjd->bihd', score_grad, key_rows, preferred_element_type...  25.9 us
  transfers between devices with their start and end apart: 5, of which 2 were waited for; matrix products, arithmetic and copies ran while one was open for 17% of the time, Pallas kernels for 0%

commit v1 on v0

v1 whole, which is shorter than its diff:
```python
import functools
import math

import jax
import jax.numpy as jnp
from jax import lax
from jax.experimental import pallas as pl
from jax.experimental.pallas import tpu as pltpu
from jax.sharding import PartitionSpec as P

STRIPE = 128
HEADS = 8
DIM = 128
WIDE = HEADS * STRIPE
NEG = -1e30
FAR = -(1 << 20)
SCALE = 1.0 / math.sqrt(DIM)
SCALE2 = math.log2(math.e) / math.sqrt(DIM)


def build_list(j, nk, q_pos, k_pos, window, idx, gap):
    q_at = q_pos[j] * STRIPE

    def one(k, n):
        distance = q_at - k_pos[k] * STRIPE
        seen = (distance >= 0) & (distance - (STRIPE - 1) < window)
        idx[n] = k
        gap[n] = distance
        return n + seen.astype(jnp.int32)

    n = lax.fori_loop(0, nk, one, jnp.int32(0), unroll=8)
    idx[n] = 0
    gap[n] = FAR
    return (n + 1) // 2


def pair_mask(g0, g1, window):
    delta = lax.broadcasted_iota(jnp.int32, (STRIPE, STRIPE), 1) - lax.broadcasted_iota(
        jnp.int32, (STRIPE, STRIPE), 0
    )
    parts = []
    for g in (g0, g1):
        distance = delta + g
        parts.append((distance >= 0) & (distance < window))
    both = jnp.concatenate(parts, axis=0)
    return jnp.concatenate([both, both], axis=1)


def dot_nt(a, b):
    return lax.dot_general(a, b, (((1,), (1,)), ((), ())), preferred_element_type=jnp.float32)


def dot_nn(a, b):
    return lax.dot_general(a, b, (((1,), (0,)), ((), ())), preferred_element_type=jnp.float32)


def stats_kernel(nq, nk, q_pos, k_pos, win, q_ref, k_ref, out_ref, idx, gap, m_ref, l_ref):
    window = win[0]

    def per_query(j, carry):
        steps = build_list(j, nk, q_pos, k_pos, window, idx, gap)
        m_ref[...] = jnp.full_like(m_ref, NEG)
        l_ref[...] = jnp.zeros_like(l_ref)

        def step(t, c):
            i0, i1 = idx[2 * t], idx[2 * t + 1]
            keys = jnp.concatenate([k_ref[i0], k_ref[i1]], axis=0)
            mask = pair_mask(gap[2 * t], gap[2 * t + 1], window)
            for b in range(HEADS // 2):
                cols = pl.ds(b * 256, 256)
                s = dot_nt(keys, q_ref[j, cols, :])
                s = jnp.where(mask, s, NEG).reshape(32, 8, 256)
                m_old = m_ref[:, cols]
                m_new = jnp.maximum(m_old, jnp.max(s, axis=0))
                e = jnp.exp2((s - m_new[None]) * SCALE2)
                l_ref[:, cols] = l_ref[:, cols] * jnp.exp2((m_old - m_new) * SCALE2) + jnp.sum(e, axis=0)
                m_ref[:, cols] = m_new
            return c

        lax.fori_loop(0, steps, step, 0)
        m_all = m_ref[...]
        top = jnp.max(m_all, axis=0, keepdims=True)
        total = jnp.sum(l_ref[...] * jnp.exp2((m_all - top) * SCALE2), axis=0, keepdims=True)
        out_ref[j, 0:1, :] = top
        out_ref[j, 1:2, :] = total
        return carry

    lax.fori_loop(0, nq, per_query, 0)


def grads_kernel(
    nq, nk, q_pos, k_pos, win, q_ref, g_ref, k_ref, v_ref, stat_ref, dq_ref, dkv_ref, idx, gap, kt_ref, acc_ref, dq_acc
):
    window = win[0]

    def clear(k, c):
        acc_ref[k] = jnp.zeros((STRIPE, 2 * DIM), jnp.float32)
        kt_ref[k] = jnp.transpose(k_ref[k].astype(jnp.float32)).astype(jnp.bfloat16)
        return c

    lax.fori_loop(0, nk, clear, 0)

    def per_query(j, carry):
        steps = build_list(j, nk, q_pos, k_pos, window, idx, gap)
        dq_acc[...] = jnp.zeros_like(dq_acc)

        def step(t, c):
            i0, i1 = idx[2 * t], idx[2 * t + 1]
            keys = jnp.concatenate([k_ref[i0], k_ref[i1]], axis=0)
            vals = jnp.concatenate([v_ref[i0], v_ref[i1]], axis=0)
            keys_t = jnp.concatenate([kt_ref[i0], kt_ref[i1]], axis=1)
            mask = pair_mask(gap[2 * t], gap[2 * t + 1], window)
            dk = jnp.zeros((2 * STRIPE, DIM), jnp.float32)
            dv = jnp.zeros((2 * STRIPE, DIM), jnp.float32)
            for b in range(HEADS // 2):
                cols = pl.ds(b * 256, 256)
                q = q_ref[j, cols, :]
                g = g_ref[j, cols, :]
                s = dot_nt(keys, q)
                p = jnp.where(mask, jnp.exp2(s * SCALE2 - stat_ref[j, 0:1, cols]), 0.0)
                w = dot_nt(vals, g)
                ds = (p * (w - stat_ref[j, 1:2, cols])).astype(jnp.bfloat16)
                dv += dot_nn(p.astype(jnp.bfloat16), g)
                dk += dot_nn(ds, q)
                dq_acc[:, cols] += dot_nn(keys_t, ds)
            for n, i in enumerate((i0, i1)):
                rows = slice(n * STRIPE, (n + 1) * STRIPE)
                acc_ref[i, :, 0:DIM] += dk[rows]
                acc_ref[i, :, DIM:] += dv[rows]
            return c

        lax.fori_loop(0, steps, step, 0)
        dq_ref[j] = (dq_acc[...] * SCALE).astype(jnp.bfloat16)
        return carry

    lax.fori_loop(0, nq, per_query, 0)

    def finish(k, c):
        dkv_ref[k, :, 0:DIM] = (acc_ref[k, :, 0:DIM] * SCALE).astype(jnp.bfloat16)
        dkv_ref[k, :, DIM:] = acc_ref[k, :, DIM:].astype(jnp.bfloat16)
        return c

    lax.fori_loop(0, nk, finish, 0)


def smem():
    return pl.BlockSpec(memory_space=pltpu.SMEM)


def vmem():
    return pl.BlockSpec(memory_space=pltpu.VMEM)


def stats_call(nq, nk, q_pos, k_pos, win, q, k):
    return pl.pallas_call(
        functools.partial(stats_kernel, nq, nk),
        out_shape=jax.ShapeDtypeStruct((nq, 2, WIDE), jnp.float32),
        in_specs=[smem()] * 3 + [vmem()] * 2,
        out_specs=vmem(),
        scratch_shapes=[
            pltpu.SMEM((nk + 1,), jnp.int32),
            pltpu.SMEM((nk + 1,), jnp.int32),
            pltpu.VMEM((8, WIDE), jnp.float32),
            pltpu.VMEM((8, WIDE), jnp.float32),
        ],
        compiler_params=pltpu.CompilerParams(vmem_limit_bytes=48 << 20),
        name="stats",
    )(q_pos, k_pos, win, q, k)


def grads_call(nq, nk, q_pos, k_pos, win, q, g, k, v, stats):
    return pl.pallas_call(
        functools.partial(grads_kernel, nq, nk),
        out_shape=(
            jax.ShapeDtypeStruct((nq, DIM, WIDE), jnp.bfloat16),
            jax.ShapeDtypeStruct((nk, STRIPE, 2 * DIM), jnp.bfloat16),
        ),
        in_specs=[smem()] * 3 + [vmem()] * 5,
        out_specs=(vmem(), vmem()),
        scratch_shapes=[
            pltpu.SMEM((nk + 1,), jnp.int32),
            pltpu.SMEM((nk + 1,), jnp.int32),
            pltpu.VMEM((nk, DIM, STRIPE), jnp.bfloat16),
            pltpu.VMEM((nk, STRIPE, 2 * DIM), jnp.float32),
            pltpu.VMEM((DIM, WIDE), jnp.float32),
        ],
        compiler_params=pltpu.CompilerParams(vmem_limit_bytes=48 << 20),
        name="grads",
    )(q_pos, k_pos, win, q, g, k, v, stats)


def from_everyone(value, axis):
    copies = jnp.broadcast_to(value, (lax.axis_size(axis), *value.shape))
    return lax.all_to_all(copies, axis, split_axis=0, concat_axis=0, tiled=True)


def per_device(
    queries, query_exps, key_head, value_head, forward_out, output_grad, stripe_order, window_size
):
    nq = lax.axis_size("row")
    nk = lax.axis_size("col")
    q_pos = lax.dynamic_index_in_dim(stripe_order.reshape(nq, nk), lax.axis_index("col"), 1, keepdims=False)
    k_pos = lax.dynamic_index_in_dim(stripe_order.reshape(nk, nq), lax.axis_index("row"), 1, keepdims=False)

    scaled = (
        queries.astype(jnp.float32) * jnp.exp2(query_exps.astype(jnp.float32))[:, None]
    ).astype(jnp.bfloat16)

    def by_head(a):
        return a.reshape(STRIPE, HEADS, DIM).transpose(1, 0, 2).reshape(WIDE, DIM)

    product = output_grad.astype(jnp.float32) * forward_out.astype(jnp.float32)
    delta = product.reshape(STRIPE, HEADS, DIM).sum(-1).astype(jnp.bfloat16)
    delta = delta.T.reshape(1, WIDE).astype(jnp.float32)

    k_all = from_everyone(key_head, "col").reshape(nk, STRIPE, DIM)
    q_all = from_everyone(by_head(scaled), "row").reshape(nq, WIDE, DIM)
    v_all = from_everyone(value_head, "col").reshape(nk, STRIPE, DIM)
    g_all = from_everyone(by_head(output_grad), "row").reshape(nq, WIDE, DIM)

    part = stats_call(nq, nk, q_pos, k_pos, window_size, q_all, k_all)
    mine = lax.all_to_all(part, "row", split_axis=0, concat_axis=0, tiled=True)
    top = jnp.max(mine[:, 0], axis=0)
    total = jnp.sum(mine[:, 1] * jnp.exp2((mine[:, 0] - top) * SCALE2), axis=0)
    log_norm = (top * SCALE2 + jnp.log2(total))[None]
    stats = from_everyone(jnp.concatenate([log_norm, delta], axis=0)[None], "row").reshape(nq, 2, WIDE)

    dq, dkv = grads_call(nq, nk, q_pos, k_pos, window_size, q_all, g_all, k_all, v_all, stats)
    dq = lax.all_to_all(dq, "row", split_axis=0, concat_axis=0, tiled=True)
    dkv = lax.all_to_all(dkv, "col", split_axis=0, concat_axis=0, tiled=True)
    dq = dq.astype(jnp.float32).sum(0).astype(jnp.bfloat16)
    dq = dq.reshape(DIM, HEADS, STRIPE).transpose(2, 1, 0).reshape(STRIPE, WIDE)
    dkv = dkv.astype(jnp.float32).sum(0).astype(jnp.bfloat16)
    return dq, dkv[:, :DIM], dkv[:, DIM:]


def solution(mesh):
    return jax.shard_map(
        per_device,
        mesh=mesh,
        in_specs=(
            P(("row", "col"), None),
            P(("row", "col")),
            P(("col", "row"), None),
            P(("col", "row"), None),
            P(("row", "col"), None),
            P(("row", "col"), None),
            P(),
            P(),
        ),
        out_specs=(P(("row", "col"), None), P(("col", "row"), None), P(("col", "row"), None)),
        check_vma=False,
    )
```

time: 760 us -> 299 us (0.39)
  local copies, waits for them, and re-layouts: 165 us -> 8.79 us
  other arithmetic: 155 us -> 4.78 us
  matrix products: 89 us -> 0 us
  Pallas kernels: 0 us -> 63.5 us
  waiting for transfers between devices: 177 us -> 115 us
  blocking collectives: 108 us -> 67.8 us
  between operations: 15.2 us -> 1.51 us
  starting transfers between devices: 44.3 us -> 34.7 us
    reduce_scatter x1 -> x0, waiting for transfers between devices: 135 us -> none  [in_one_piece(): lax.psum_scatter(both, axis, scatter_dimension=dim, tiled=True)]
    gather x78 -> x0, local copies, waits for them, and re-layouts: 104 us -> none  [the longest x12 24 us: visible_scores(): query_rows = query_tiles[q_index]]
    scatter-add x25 -> x0, other arithmetic: 91.6 us -> none  [the longest x6 52.3 us: add_grads(): query_sum.at[q_index]]
    dot_general x36 -> x0, matrix products: 89 us -> none  [the longest x12 41.7 us: visible_scores(): jnp.einsum('bihd,bjd->bhij', query_split, key_rows, preferred_element_typ...]
    pallas_call x0 -> x2, Pallas kernels: none -> 63.5 us  [the longest x1 45.8 us: grads_call(): pl.pallas_call(functools.partial(grads_kernel, nq, nk), out_shape=(jax.Sh...]
    all_to_all x2 -> x3, waiting for transfers between devices: 0.01 us -> 60.3 us  [from_everyone(): return lax.all_to_all(copies, axis, split_axis=0, concat_axis=0, tiled=True)]
    all_to_all x0 -> x2, waiting for transfers between devices: none -> 54.8 us  [the longest x1 50.8 us: per_device(): dkv = lax.all_to_all(dkv, 'col', split_axis=0, concat_axis=0, tiled=True)]
    all_gather x2 -> x0, waiting for transfers between devices: 42.5 us -> none  [side_by_side(): whole = lax.all_gather(both, axis, axis=dim, tiled=True)]
  transfers between devices with their start and end apart: 5 -> 5, of which waited for: 2 -> 5; matrix products, arithmetic and copies ran while one was open for 17% -> 2% of each run, Pallas kernels for 0% -> 6%
where the time goes in v1:
time: 299 us; the launch traced here: 296 us
  waiting for transfers between devices  115 us (38%)
  blocking collectives  67.8 us (23%)
  Pallas kernels  63.5 us (21%)
  starting transfers between devices  34.7 us (12%)
  local copies, waits for them, and re-layouts  8.79 us (3%)
  other arithmetic  4.78 us (2%)
    all_to_all x3, waiting for transfers between devices, from_everyone(): return lax.all_to_all(copies, axis, split_axis=0, concat_axis=0, tiled=True)  60.3 us
    all_to_all x1, waiting for transfers between devices, per_device(): dkv = lax.all_to_all(dkv, 'col', split_axis=0, concat_axis=0, tiled=True)  50.8 us
    pallas_call x1, Pallas kernels, grads_call(): pl.pallas_call(functools.partial(grads_kernel, nq, nk), out_shape=(jax.Sh...  45.8 us
    all_to_all x2, blocking collectives, from_everyone(): return lax.all_to_all(copies, axis, split_axis=0, concat_axis=0, tiled=True)  38.2 us
    all_to_all x1, blocking collectives, per_device(): dq = lax.all_to_all(dq, 'row', split_axis=0, concat_axis=0, tiled=True)  29.6 us
    all_to_all x3, starting transfers between devices, from_everyone(): return lax.all_to_all(copies, axis, split_axis=0, concat_axis=0, tiled=True)  22 us
    pallas_call x1, Pallas kernels, stats_call(): pl.pallas_call(functools.partial(stats_kernel, nq, nk), out_shape=jax.Sha...  17.7 us
    all_to_all x1, starting transfers between devices, per_device(): dkv = lax.all_to_all(dkv, 'col', split_axis=0, concat_axis=0, tiled=True)  6.71 us
  transfers between devices with their start and end apart: 5, of which 5 were waited for; matrix products, arithmetic and copies ran while one was open for 2% of the time, Pallas kernels for 6%

profile of v1, /device:TPU:4, one launch (start us, length us, event | category | flops | bytes accessed | tf_op | source)
XLA Modules:
  0.0 296.2 jit_solution(17946762200731127779)
XLA Ops:
  0.6 0.0 copy-start.6
  0.6 0.0 copy-start.3
  0.7 2.0 broadcast_in_dim.21
  2.7 11.5 %all-to-all-start.2 = ((bf16[32,128,128]{2,1,0:T(8,128)(2,1)}), bf16[32,128,128]{2,1,0:T(8,128)(2,1)S(1)}, u32[]{:S(2)}, u32[]{:S(2)}) async-start(bf16[32,128,128]{2,1,0:T(8,128)(2,1)} %broadcast_in_dim.21), calls=%async_computation.2 | async-start | bytes 2097152 | tf_op jit(solution)/shard_map/all_to_all | solution.py:194
  14.2 0.0 copy-done.6
  14.2 0.0 copy-done.3
  14.2 0.1 fusion
  14.4 30.1 %all-to-all-done.2.k_ref = bf16[32,128,128]{2,1,0:T(8,128)(2,1)S(1)} async-done(((bf16[32,128,128]{2,1,0:T(8,128)(2,1)}), bf16[32,128,128]{2,1,0:T(8,128)(2,1)S(1)}, u32[]{:S(2)}, u32[]{:S(2)}) %all-to-all-start.2) | async-done | bytes 1048608 | tf_op jit(solution)/shard_map/all_to_all | solution.py:194
  44.5 0.3 broadcast_in_dim.19
  44.8 0.0 copy-start.4
  44.8 28.9 %all_to_all.40.q_ref = bf16[8,1024,128]{2,1,0:T(8,128)(2,1)S(1)} all-to-all(bf16[8,1024,128]{2,1,0:T(8,128)(2,1)S(1)} %broadcast_in_dim.19), channel_id=1, replica_groups=mesh['row'=8,'col'=32] {'row'}, dimensions={0} | all-to-all | bytes 4194304 | tf_op jit(solution)/shard_map/all_to_all | solution.py:194
  73.7 0.0 copy-done.4
  73.7 0.0 copy-start
  73.7 0.0 copy-start.5
  73.7 1.4 broadcast_in_dim.22
  75.2 4.8 %all-to-all-start.3 = ((bf16[32,128,128]{2,1,0:T(8,128)(2,1)}), bf16[32,128,128]{2,1,0:T(8,128)(2,1)}, u32[]{:S(2)}, u32[]{:S(2)}) async-start(bf16[32,128,128]{2,1,0:T(8,128)(2,1)} %broadcast_in_dim.22), calls=%async_computation.3 | async-start | bytes 2097152 | tf_op jit(solution)/shard_map/all_to_all | solution.py:194
  80.0 0.0 copy-start.2
  80.0 0.0 copy-done.5
  80.0 0.1 reshape.79
  80.1 0.1 reshape.80
  80.8 0.2 dynamic-slice_reduce_fusion.1.q_pos
  81.0 0.2 dynamic-slice_reduce_fusion.k_pos
  81.2 17.7 %stats.1 = f32[8,2,1024]{2,1,0:T(2,128)} custom-call(s32[8]{0:T(128)S(1)} %dynamic-slice_reduce_fusion.1.q_pos, s32[32]{0:T(128)S(1)} %dynamic-slice_reduce_fusion.k_pos, s32[1]{0:T(128)S(6)} %copy.53.win, bf16[8,1024,128]{2,1,0:T(8,128)(2,1)S(1)} %all_to_all.40.q_ref, bf16[32,128,128]{2,1,0:T(8,128)(2,1)S(1)} %all-to-all-done.2.k_ref), custom_call_target="tpu_custom_call" | custom-call | tf_op jit(solution)/shard_map/stats/pallas_call | solution.py:155
  98.8 0.0 copy-done
  98.8 11.2 %all-to-all-done.3.v_ref = bf16[32,128,128]{2,1,0:T(8,128)(2,1)} async-done(((bf16[32,128,128]{2,1,0:T(8,128)(2,1)}), bf16[32,128,128]{2,1,0:T(8,128)(2,1)}, u32[]{:S(2)}, u32[]{:S(2)}) %all-to-all-start.3) | async-done | bytes 1048608 | tf_op jit(solution)/shard_map/all_to_all | solution.py:194
  110.0 5.9 %all-to-all-start.4 = ((f32[8,2,1024]{2,1,0:T(2,128)}), f32[8,2,1024]{2,1,0:T(2,128)S(1)}, u32[]{:S(2)}, u32[]{:S(2)}) async-start(f32[8,2,1024]{2,1,0:T(2,128)} %stats.1), calls=%async_computation.4 | async-start | bytes 131072 | tf_op jit(solution)/shard_map/all_to_all | solution.py:222
  116.0 0.0 copy-done.2
  116.0 4.0 %all-to-all-done.4 = f32[8,2,1024]{2,1,0:T(2,128)S(1)} async-done(((f32[8,2,1024]{2,1,0:T(2,128)}), f32[8,2,1024]{2,1,0:T(2,128)S(1)}, u32[]{:S(2)}, u32[]{:S(2)}) %all-to-all-start.4) | async-done | bytes 65568 | tf_op jit(solution)/shard_map/all_to_all | solution.py:222
  120.0 1.6 broadcast_in_dim.20
  121.6 5.8 %all-to-all-start.1 = ((bf16[8,1024,128]{2,1,0:T(8,128)(2,1)}), bf16[8,1024,128]{2,1,0:T(8,128)(2,1)S(1)}, u32[]{:S(2)}, u32[]{:S(2)}) async-start(bf16[8,1024,128]{2,1,0:T(8,128)(2,1)} %broadcast_in_dim.20), calls=%async_computation.1 | async-start | bytes 4194304 | tf_op jit(solution)/shard_map/all_to_all | solution.py:194
  127.4 1.0 multiply_bitcast_fusion
  128.4 0.9 copy.40
  129.3 1.3 reduce_sum.43
  130.6 0.1 slice_reduce_fusion
  130.8 19.0 %all-to-all-done.1.g_ref = bf16[8,1024,128]{2,1,0:T(8,128)(2,1)S(1)} async-done(((bf16[8,1024,128]{2,1,0:T(8,128)(2,1)}), bf16[8,1024,128]{2,1,0:T(8,128)(2,1)S(1)}, u32[]{:S(2)}, u32[]{:S(2)}) %all-to-all-start.1) | async-done | bytes 2097184 | tf_op jit(solution)/shard_map/all_to_all | solution.py:194
  149.8 0.0 copy-start.1
  149.8 9.3 %all_to_all.41 = f32[8,1,2,1024]{3,2,1,0:T(2,128)S(1)} all-to-all(f32[8,1,2,1024]{3,2,1,0:T(2,128)S(1)} %broadcast_in_dim.23), channel_id=1, replica_groups=mesh['row'=8,'col'=32] {'row'}, dimensions={0} | all-to-all | bytes 131072 | tf_op jit(solution)/shard_map/all_to_all | solution.py:194
  159.1 0.0 copy-done.1
  159.1 45.8 %grads.1 = (bf16[8,128,1024]{2,1,0:T(8,128)(2,1)S(1)}, bf16[32,128,256]{2,1,0:T(8,128)(2,1)}) custom-call(s32[8]{0:T(128)S(1)} %dynamic-slice_reduce_fusion.1.q_pos, s32[32]{0:T(128)S(1)} %dynamic-slice_reduce_fusion.k_pos, s32[1]{0:T(128)S(6)} %copy.53.win, bf16[8,1024,128]{2,1,0:T(8,128)(2,1)} %copy-done, bf16[8,1024,128]{2,1,0:T(8,128)(2,1)} %copy-done.1, ...), custom_call_target="tpu_custom_call" | custom-call | tf_op jit(solution)/shard_map/grads/pallas_call | solution.py:172
  204.9 29.6 %all_to_all.42 = bf16[8,128,1024]{2,1,0:T(8,128)(2,1)S(1)} all-to-all(bf16[8,128,1024]{2,1,0:T(8,128)(2,1)S(1)} %get-tuple-element.5), channel_id=1, replica_groups=mesh['row'=8,'col'=32] {'row'}, dimensions={0} | all-to-all | bytes 4194304 | tf_op jit(solution)/shard_map/all_to_all | solution.py:229
  234.5 6.7 %all-to-all-start.7 = ((bf16[32,128,256]{2,1,0:T(8,128)(2,1)}), bf16[32,128,256]{2,1,0:T(8,128)(2,1)}, u32[]{:S(2)}, u32[]{:S(2)}) async-start(bf16[32,128,256]{2,1,0:T(8,128)(2,1)} %get-tuple-element.6), calls=%async_computation.7 | async-start | bytes 4194304 | tf_op jit(solution)/shard_map/all_to_all | solution.py:230
  241.2 0.4 reduce_sum.44
  241.6 0.2 copy.32
  241.8 0.2 copy.33
  242.0 0.9 copy.34
  242.8 50.8 %all-to-all-done.7 = bf16[32,128,256]{2,1,0:T(8,128)(2,1)} async-done(((bf16[32,128,256]{2,1,0:T(8,128)(2,1)}), bf16[32,128,256]{2,1,0:T(8,128)(2,1)}, u32[]{:S(2)}, u32[]{:S(2)}) %all-to-all-start.7) | async-done | bytes 2097184 | tf_op jit(solution)/shard_map/all_to_all | solution.py:230
  293.7 1.9 reduce_sum.45
  295.5 0.6 fusion.6
  (11 shorter events, 0.3 us)
Async XLA Ops:
  0.6 13.5 %copy-start.6 = (s32[128]{0:T(128)S(1)}, s32[128]{0:T(128)}, u32[]{:S(2)}) copy-start(s32[128]{0:T(128)} %param.9) | copy-start | bytes 1540
  0.6 13.6 %copy-start.3 = (bf16[128,1024]{1,0:T(8,128)(2,1)S(1)}, bf16[128,1024]{1,0:T(8,128)(2,1)}, u32[]{:S(2)}) copy-start(bf16[128,1024]{1,0:T(8,128)(2,1)} %param.8) | copy-start | bytes 786436
  2.7 41.9 %all-to-all-start.2 = ((bf16[32,128,128]{2,1,0:T(8,128)(2,1)}), bf16[32,128,128]{2,1,0:T(8,128)(2,1)S(1)}, u32[]{:S(2)}, u32[]{:S(2)}) async-start(bf16[32,128,128]{2,1,0:T(8,128)(2,1)} %broadcast_in_dim.21), calls=%async_computation.2 | async-start | bytes 2097152 | tf_op jit(solution)/shard_map/all_to_all | solution.py:194
  44.8 28.9 %copy-start.4 = (bf16[128,128]{1,0:T(8,128)(2,1)S(1)}, bf16[128,128]{1,0:T(8,128)(2,1)}, u32[]{:S(2)}) copy-start(bf16[128,128]{1,0:T(8,128)(2,1)} %param.11) | copy-start | bytes 98308
  73.7 25.1 %copy-start = (bf16[8,1024,128]{2,1,0:T(8,128)(2,1)}, bf16[8,1024,128]{2,1,0:T(8,128)(2,1)S(1)}, u32[]{:S(2)}) copy-start(bf16[8,1024,128]{2,1,0:T(8,128)(2,1)S(1)} %all_to_all.40.q_ref) | copy-start | bytes 6291460
  73.7 6.2 %copy-start.5 = (s32[256]{0:T(256)S(1)}, s32[256]{0:T(256)}, u32[]{:S(2)}) copy-start(s32[256]{0:T(256)} %param.14) | copy-start | bytes 3076
  75.2 34.8 %all-to-all-start.3 = ((bf16[32,128,128]{2,1,0:T(8,128)(2,1)}), bf16[32,128,128]{2,1,0:T(8,128)(2,1)}, u32[]{:S(2)}, u32[]{:S(2)}) async-start(bf16[32,128,128]{2,1,0:T(8,128)(2,1)} %broadcast_in_dim.22), calls=%async_computation.3 | async-start | bytes 2097152 | tf_op jit(solution)/shard_map/all_to_all | solution.py:194
  80.0 36.0 %copy-start.2 = (bf16[128,1024]{1,0:T(8,128)(2,1)S(1)}, bf16[128,1024]{1,0:T(8,128)(2,1)}, u32[]{:S(2)}) copy-start(bf16[128,1024]{1,0:T(8,128)(2,1)} %param.13) | copy-start | bytes 786436
  110.0 10.0 %all-to-all-start.4 = ((f32[8,2,1024]{2,1,0:T(2,128)}), f32[8,2,1024]{2,1,0:T(2,128)S(1)}, u32[]{:S(2)}, u32[]{:S(2)}) async-start(f32[8,2,1024]{2,1,0:T(2,128)} %stats.1), calls=%async_computation.4 | async-start | bytes 131072 | tf_op jit(solution)/shard_map/all_to_all | solution.py:222
  121.6 28.2 %all-to-all-start.1 = ((bf16[8,1024,128]{2,1,0:T(8,128)(2,1)}), bf16[8,1024,128]{2,1,0:T(8,128)(2,1)S(1)}, u32[]{:S(2)}, u32[]{:S(2)}) async-start(bf16[8,1024,128]{2,1,0:T(8,128)(2,1)} %broadcast_in_dim.20), calls=%async_computation.1 | async-start | bytes 4194304 | tf_op jit(solution)/shard_map/all_to_all | solution.py:194
  149.8 9.3 %copy-start.1 = (bf16[8,1024,128]{2,1,0:T(8,128)(2,1)}, bf16[8,1024,128]{2,1,0:T(8,128)(2,1)S(1)}, u32[]{:S(2)}) copy-start(bf16[8,1024,128]{2,1,0:T(8,128)(2,1)S(1)} %all-to-all-done.1.g_ref) | copy-start | bytes 6291460
  234.5 59.2 %all-to-all-start.7 = ((bf16[32,128,256]{2,1,0:T(8,128)(2,1)}), bf16[32,128,256]{2,1,0:T(8,128)(2,1)}, u32[]{:S(2)}, u32[]{:S(2)}) async-start(bf16[32,128,256]{2,1,0:T(8,128)(2,1)} %get-tuple-element.6), calls=%async_computation.7 | async-start | bytes 4194304 | tf_op jit(solution)/shard_map/all_to_all | solution.py:230

commit v2 on v1

v2 whole, which is shorter than its diff:
```python
import functools
import math

import jax
import jax.numpy as jnp
from jax import lax
from jax.experimental import pallas as pl
from jax.experimental.pallas import tpu as pltpu
from jax.sharding import PartitionSpec as P

STRIPE = 128
HEADS = 8
DIM = 128
WIDE = HEADS * STRIPE
NQ = 4
NK = 64
MESH = pl.DeviceIdType.MESH
NEG = -1e30
FAR = -(1 << 20)
SCALE = 1.0 / math.sqrt(DIM)
SCALE2 = math.log2(math.e) / math.sqrt(DIM)


def coords():
    row, col = lax.axis_index("row"), lax.axis_index("col")
    x, y, core = row // 2, col // 8, col % 2
    z = ((col // 2) % 4) * 2 + row % 2
    return x, y, z, core


def device(x, y, z, core):
    return (x * 2 + z % 2, y * 8 + (z // 2) * 2 + core)


def slot_of(y, z, core):
    return core * 32 + y * 8 + z


def key_positions(order, k_pos):
    row = lax.axis_index("row")

    def one(s, c):
        y, z, core = (s // 8) % 4, s % 8, s // 32
        stored = (y * 8 + (z // 2) * 2 + core) * 8 + (row // 2) * 2 + z % 2
        k_pos[s] = order[stored] * STRIPE
        return c

    lax.fori_loop(0, NK, one, 0, unroll=8)


def query_position(order, j):
    row, col = lax.axis_index("row"), lax.axis_index("col")
    return order[(j * 2 + row % 2) * 32 + col] * STRIPE


def build_list(q_at, k_pos, window, idx, gap):
    def one(k, n):
        distance = q_at - k_pos[k]
        seen = (distance >= 0) & (distance - (STRIPE - 1) < window)
        idx[n] = k
        gap[n] = distance
        return n + seen.astype(jnp.int32)

    n = lax.fori_loop(0, NK, one, jnp.int32(0), unroll=8)
    idx[n] = 0
    gap[n] = FAR
    return (n + 1) // 2


def pair_mask(g0, g1, window):
    delta = lax.broadcasted_iota(jnp.int32, (STRIPE, STRIPE), 1) - lax.broadcasted_iota(
        jnp.int32, (STRIPE, STRIPE), 0
    )
    parts = []
    for g in (g0, g1):
        distance = delta + g
        parts.append((distance >= 0) & (distance < window))
    both = jnp.concatenate(parts, axis=0)
    return jnp.concatenate([both, both], axis=1)


def dot_nt(a, b):
    return lax.dot_general(a, b, (((1,), (1,)), ((), ())), preferred_element_type=jnp.float32)


def dot_nn(a, b):
    return lax.dot_general(a, b, (((1,), (0,)), ((), ())), preferred_element_type=jnp.float32)


def stats_kernel(order, win, q_ref, k_ref, out_ref, k_pos, idx, gap, m_ref, l_ref):
    window = win[0]
    key_positions(order, k_pos)

    def per_query(j, carry):
        steps = build_list(query_position(order, j), k_pos, window, idx, gap)
        m_ref[...] = jnp.full_like(m_ref, NEG)
        l_ref[...] = jnp.zeros_like(l_ref)

        def step(t, c):
            i0, i1 = idx[2 * t], idx[2 * t + 1]
            keys = jnp.concatenate([k_ref[i0, 0], k_ref[i1, 0]], axis=0)
            mask = pair_mask(gap[2 * t], gap[2 * t + 1], window)
            for b in range(HEADS // 2):
                cols = pl.ds(b * 256, 256)
                s = dot_nt(keys, q_ref[j, 0, cols, :])
                s = jnp.where(mask, s, NEG).reshape(32, 8, 256)
                m_old = m_ref[:, cols]
                m_new = jnp.maximum(m_old, jnp.max(s, axis=0))
                e = jnp.exp2((s - m_new[None]) * SCALE2)
                l_ref[:, cols] = l_ref[:, cols] * jnp.exp2((m_old - m_new) * SCALE2) + jnp.sum(e, axis=0)
                m_ref[:, cols] = m_new
            return c

        lax.fori_loop(0, steps, step, 0)
        m_all = m_ref[...]
        top = jnp.max(m_all, axis=0, keepdims=True)
        total = jnp.sum(l_ref[...] * jnp.exp2((m_all - top) * SCALE2), axis=0, keepdims=True)
        out_ref[0, pl.ds(j, 1), :] = top
        out_ref[1, pl.ds(j, 1), :] = total
        return carry

    lax.fori_loop(0, NQ, per_query, 0)


def grads_kernel(
    order, win, qg_ref, kv_ref, norm_ref, delta_ref, dq_ref, dkv_ref, k_pos, idx, gap, kt_ref, acc_ref, dq_acc, stat_ref
):
    window = win[0]
    key_positions(order, k_pos)

    def clear(k, c):
        acc_ref[k] = jnp.zeros((STRIPE, 2 * DIM), jnp.float32)
        kt_ref[k] = jnp.transpose(kv_ref[k, 0].astype(jnp.float32)).astype(jnp.bfloat16)
        return c

    lax.fori_loop(0, NK, clear, 0)

    def per_query(j, carry):
        steps = build_list(query_position(order, j), k_pos, window, idx, gap)
        dq_acc[...] = jnp.zeros_like(dq_acc)
        stat_ref[0:1, :] = norm_ref[pl.ds(j, 1), :]
        for h in range(HEADS):
            stat_ref[1:2, h * DIM : (h + 1) * DIM] = delta_ref[j, h : h + 1, :]

        def step(t, c):
            i0, i1 = idx[2 * t], idx[2 * t + 1]
            keys = jnp.concatenate([kv_ref[i0, 0], kv_ref[i1, 0]], axis=0)
            vals = jnp.concatenate([kv_ref[i0, 1], kv_ref[i1, 1]], axis=0)
            keys_t = jnp.concatenate([kt_ref[i0], kt_ref[i1]], axis=1)
            mask = pair_mask(gap[2 * t], gap[2 * t + 1], window)
            dk = jnp.zeros((2 * STRIPE, DIM), jnp.float32)
            dv = jnp.zeros((2 * STRIPE, DIM), jnp.float32)
            for b in range(HEADS // 2):
                cols = pl.ds(b * 256, 256)
                q = qg_ref[j, 0, cols, :]
                g = qg_ref[j, 1, cols, :]
                s = dot_nt(keys, q)
                p = jnp.where(mask, jnp.exp2(s * SCALE2 - stat_ref[0:1, cols]), 0.0)
                w = dot_nt(vals, g)
                ds = (p * (w - stat_ref[1:2, cols])).astype(jnp.bfloat16)
                dv += dot_nn(p.astype(jnp.bfloat16), g)
                dk += dot_nn(ds, q)
                dq_acc[:, cols] += dot_nn(keys_t, ds)
            for n, i in enumerate((i0, i1)):
                rows = slice(n * STRIPE, (n + 1) * STRIPE)
                acc_ref[i, :, 0:DIM] += dk[rows]
                acc_ref[i, :, DIM:] += dv[rows]
            return c

        lax.fori_loop(0, steps, step, 0)
        dq_ref[j] = (dq_acc[...] * SCALE).astype(jnp.bfloat16)
        return carry

    lax.fori_loop(0, NQ, per_query, 0)

    def finish(k, c):
        dkv_ref[k, :, 0:DIM] = (acc_ref[k, :, 0:DIM] * SCALE).astype(jnp.bfloat16)
        dkv_ref[k, :, DIM:] = acc_ref[k, :, DIM:].astype(jnp.bfloat16)
        return c

    lax.fori_loop(0, NK, finish, 0)


def remote(src, dst, send_sem, recv_sem, to):
    return pltpu.make_async_remote_copy(
        src_ref=src, dst_ref=dst, send_sem=send_sem, recv_sem=recv_sem, device_id=to, device_id_type=MESH
    )


def greet(peers):
    barrier = pltpu.get_barrier_semaphore()
    for peer in peers:
        pl.semaphore_signal(barrier, inc=1, device_id=peer, device_id_type=MESH)
    pl.semaphore_wait(barrier, len(peers))


def plane_peers(x, y, z, core):
    peers = [device(x, y, z, 1 - core)]
    peers += [device((x + d) % 4, y, z, core) for d in (1, 3)]
    peers += [device(x, (y + d) % 4, z, core) for d in (1, 3)]
    peers += [device(x, y, (z + d) % 8, core) for d in range(1, 8)]
    return peers


def gather_kernel(
    q_ref, exp_ref, k_ref, v_ref, o_ref, g_ref, qg_out, kv_out, delta_out,
    kv_own, qg_own, delta_own, kv_recv, z_send, y_send, y_pass, sib_send, x_send, x_pass, x_recv, d_send, d_recv, local,
):
    x, y, z, core = coords()
    mine = slot_of(y, z, core)
    sibling = device(x, y, z, 1 - core)
    y_up, y_down = (y + 1) % 4, (y + 3) % 4
    sign = 1 - 2 * core
    x_to, x_from = (x + sign + 4) % 4, (x - sign + 4) % 4

    greet(plane_peers(x, y, z, core) + [device((x + 2) % 4, y, z, core)])

    kv_own[0] = k_ref[...]
    kv_own[1] = v_ref[...]

    def z_copy(d):
        return remote(
            kv_own, kv_out.at[mine], z_send.at[d], kv_recv.at[mine], device(x, y, (z + d) % 8, core)
        )

    for d in (1, 7, 2, 6, 3, 5, 4):
        z_copy(d).start()

    scale = jnp.transpose(jnp.broadcast_to(jnp.exp2(exp_ref[...].astype(jnp.float32)), (STRIPE, STRIPE)))

    def x_copy(p, n):
        return remote(
            qg_own.at[p], qg_out.at[x, p], x_send.at[p, n], x_recv.at[x, p], device((x + 1 + 2 * n) % 4, y, z, core)
        )

    for h in range(HEADS):
        cols = slice(h * DIM, (h + 1) * DIM)
        qg_own[0, cols, :] = (q_ref[:, cols].astype(jnp.float32) * scale).astype(jnp.bfloat16)
    for n in range(2):
        x_copy(0, n).start()
    for h in range(HEADS):
        cols = slice(h * DIM, (h + 1) * DIM)
        qg_own[1, cols, :] = g_ref[:, cols]
    for n in range(2):
        x_copy(1, n).start()

    own_kv = pltpu.make_async_copy(kv_own, kv_out.at[mine], local.at[0])
    own_qg = pltpu.make_async_copy(qg_own, qg_out.at[x], local.at[1])
    own_kv.start()
    own_qg.start()

    def y_copy(s, src, d, up):
        to = y_up if up else y_down
        return remote(src, kv_out.at[s], y_send.at[d, 0 if up else 1], kv_recv.at[s], device(x, to, z, core))

    def sib_copy(s, src):
        return remote(src, kv_out.at[s], sib_send.at[s % 32], kv_recv.at[s], sibling)

    def arrived(s):
        remote(kv_own, kv_out.at[s], local.at[0], kv_recv.at[s], sibling).wait_recv()

    y_copy(mine, kv_own, 0, True).start()
    y_copy(mine, kv_own, 0, False).start()
    sib_copy(mine, kv_own).start()

    for h in range(HEADS):
        cols = slice(h * DIM, (h + 1) * DIM)
        product = g_ref[:, cols].astype(jnp.float32) * o_ref[:, cols].astype(jnp.float32)
        sums = jnp.sum(jnp.transpose(product), axis=0, keepdims=True)
        delta_own[h : h + 1, :] = sums.astype(jnp.bfloat16).astype(jnp.float32)

    def d_copy(n):
        return remote(delta_own, delta_out.at[x], d_send.at[n], d_recv.at[x], device((x + 1 + n) % 4, y, z, core))

    for n in range(3):
        d_copy(n).start()
    own_delta = pltpu.make_async_copy(delta_own, delta_out.at[x], local.at[2])
    own_delta.start()

    def from_z(d, c):
        s = slot_of(y, (z + d) % 8, core)
        arrived(s)
        y_copy(s, kv_out.at[s], d, True).start()
        y_copy(s, kv_out.at[s], d, False).start()
        sib_copy(s, kv_out.at[s]).start()
        return c

    def x_arrived(who, p):
        remote(qg_own.at[p], qg_out.at[who, p], local.at[0], x_recv.at[who, p], sibling).wait_recv()

    def x_forward(p):
        return remote(
            qg_out.at[x_from, p], qg_out.at[x_from, p], x_pass.at[p], x_recv.at[x_from, p], device(x_to, y, z, core)
        )

    def from_y(lower, upper):
        def body(d, c):
            zz = (z + d) % 8
            below, above = slot_of(y_down, zz, core), slot_of(y_up, zz, core)
            arrived(below)
            if lower:
                y_onward(below, d, True).start()
            sib_copy(below, kv_out.at[below]).start()
            arrived(above)
            if upper:
                y_onward(above, d, False).start()
            sib_copy(above, kv_out.at[above]).start()
            return c

        return body

    def y_onward(s, d, up):
        to = y_up if up else y_down
        return remote(kv_out.at[s], kv_out.at[s], y_pass.at[d], kv_recv.at[s], device(x, to, z, core))

    for d in (1, 7, 2, 6, 3, 5, 4):
        from_z(d, 0)
    x_arrived(x_from, 0)
    x_forward(0).start()
    lax.fori_loop(0, 4, from_y(True, False), 0)
    x_arrived(x_from, 1)
    x_forward(1).start()
    lax.fori_loop(4, 8, from_y(False, True), 0)

    def from_far(d, c):
        s = slot_of((y + 2) % 4, (z + d) % 8, core)
        arrived(s)
        sib_copy(s, kv_out.at[s]).start()
        return c

    lax.fori_loop(0, 8, from_far, 0)

    for p in range(2):
        x_arrived(x_to, p)
        x_arrived((x + 2) % 4, p)
    for n in range(1, 4):
        who = (x + n) % 4
        remote(delta_own, delta_out.at[who], local.at[0], d_recv.at[who], sibling).wait_recv()

    def from_sibling(s, c):
        arrived((1 - core) * 32 + s)
        return c

    lax.fori_loop(0, 32, from_sibling, 0)

    def sent(d, c):
        y_copy(mine, kv_own, d, True).wait_send()
        y_copy(mine, kv_own, d, False).wait_send()
        y_onward(mine, d, True).wait_send()
        return c

    lax.fori_loop(0, 8, sent, 0)

    def sib_sent(s, c):
        sib_copy(s, kv_own).wait_send()
        return c

    lax.fori_loop(0, 32, sib_sent, 0)
    for d in range(1, 8):
        z_copy(d).wait_send()
    for p in range(2):
        for n in range(2):
            x_copy(p, n).wait_send()
        x_forward(p).wait_send()
    for n in range(3):
        d_copy(n).wait_send()
    own_kv.wait()
    own_qg.wait()
    own_delta.wait()


def norm_kernel(part_ref, out_ref, got, send, recv):
    x, y, z, core = coords()
    peers = [device((x + d) % 4, y, z, core) for d in (1, 3, 2)]
    greet(peers)

    def copy(n):
        return remote(part_ref, got.at[x], send.at[n], recv.at[x], peers[n])

    for n in range(3):
        copy(n).start()
    for n in range(1, 4):
        who = (x + n) % 4
        remote(part_ref, got.at[who], send.at[0], recv.at[who], peers[0]).wait_recv()
    tops = [part_ref[0]] + [got[(x + n) % 4, 0] for n in range(1, 4)]
    sums = [part_ref[1]] + [got[(x + n) % 4, 1] for n in range(1, 4)]
    top = functools.reduce(jnp.maximum, tops)
    total = functools.reduce(jnp.add, [s * jnp.exp2((t - top) * SCALE2) for t, s in zip(tops, sums)])
    out_ref[...] = top * SCALE2 + jnp.log2(total)
    for n in range(3):
        copy(n).wait_send()


def reduce_kernel(
    dq_ref, kv_ref, dq_out, dk_out, dv_out,
    sib_got, kv_sum, opp_got, near_got, far_got, z_got, x_opp, x_near, x_far, x_sum,
    sib_send, sib_recv, a_send, a_recv, b_send, b_recv, c_send, c_recv, z_send, z_recv, x_send, x_recv,
):
    x, y, z, core = coords()
    sign = 1 - 2 * core
    sibling = device(x, y, z, 1 - core)
    y_to, y_back, y_opp = (y + sign + 4) % 4, (y - sign + 4) % 4, (y + 2) % 4
    x_to, x_back, x_over = (x + sign + 4) % 4, (x - sign + 4) % 4, (x + 2) % 4
    to_next, to_back = device(x, y_to, z, core), device(x, y_back, z, core)
    dev_to, dev_back = device(x_to, y, z, core), device(x_back, y, z, core)

    greet(plane_peers(x, y, z, core))

    def add(*parts):
        return functools.reduce(jnp.add, [p.astype(jnp.float32) for p in parts])

    def sib_copy(s):
        return remote(kv_ref.at[(1 - core) * 32 + s], sib_got.at[s], sib_send.at[s], sib_recv.at[s], sibling)

    def sib_start(yy):
        def body(d, c):
            sib_copy(yy * 8 + (z + d) % 8).start()
            return c

        lax.fori_loop(0, 8, body, 0)

    sib_start(y_opp)
    x_a = remote(dq_ref.at[x_over], x_opp, x_send.at[0], x_recv.at[0], dev_to)
    x_b = remote(dq_ref.at[x_back], x_near, x_send.at[1], x_recv.at[1], dev_back)
    x_c = remote(x_sum, x_far, x_send.at[2], x_recv.at[2], dev_to)
    x_a.start()
    sib_start(y_back)
    x_b.start()
    sib_start(y_to)
    sib_start(y)

    def with_sibling(s):
        sib_copy(s).wait_recv()
        return add(kv_ref[core * 32 + s], sib_got[s])

    def a_copy(zz):
        return remote(kv_sum.at[y_opp * 8 + zz], opp_got.at[zz], a_send.at[zz], a_recv.at[zz], to_next)

    def b_copy(zz):
        return remote(kv_sum.at[y_back * 8 + zz], near_got.at[zz], b_send.at[zz], b_recv.at[zz], to_back)

    def c_copy(zz):
        return remote(kv_sum.at[y_to * 8 + zz], far_got.at[zz], c_send.at[zz], c_recv.at[zz], to_next)

    def z_copy(zz):
        return remote(kv_sum.at[y * 8 + zz], z_got.at[z], z_send.at[zz], z_recv.at[z], device(x, y, zz, core))

    def step_a(d, c):
        zz = (z + d) % 8
        s = y_opp * 8 + zz
        kv_sum[s] = with_sibling(s).astype(jnp.bfloat16)
        a_copy(zz).start()
        return c

    def step_b(d, c):
        zz = (z + d) % 8
        s = y_back * 8 + zz
        kv_sum[s] = with_sibling(s).astype(jnp.bfloat16)
        b_copy(zz).start()
        return c

    def step_c(d, c):
        zz = (z + d) % 8
        s = y_to * 8 + zz
        total = with_sibling(s)
        a_copy(zz).wait_recv()
        kv_sum[s] = add(total, opp_got[zz]).astype(jnp.bfloat16)
        c_copy(zz).start()
        return c

    def total_here(zz):
        s = y * 8 + zz
        total = with_sibling(s)
        b_copy(zz).wait_recv()
        c_copy(zz).wait_recv()
        return add(total, near_got[zz], far_got[zz])

    def step_z(d, c):
        zz = (z + d) % 8
        kv_sum[y * 8 + zz] = total_here(zz).astype(jnp.bfloat16)
        z_copy(zz).start()
        return c

    lax.fori_loop(1, 9, step_a, 0)
    lax.fori_loop(1, 9, step_b, 0)

    x_a.wait_recv()
    def sum_x(h, c):
        rows = pl.ds(pl.multiple_of(h * 16, 16), 16)
        x_sum[rows, :] = add(dq_ref[x_to, rows, :], x_opp[rows, :]).astype(jnp.bfloat16)
        return c

    lax.fori_loop(0, 8, sum_x, 0)
    x_c.start()

    lax.fori_loop(1, 9, step_c, 0)
    lax.fori_loop(1, 8, step_z, 0)

    x_b.wait_recv()
    x_c.wait_recv()
    for h in range(HEADS):
        cols = slice(h * DIM, (h + 1) * DIM)
        total = add(dq_ref[x, :, cols], x_near[:, cols], x_far[:, cols])
        dq_out[:, cols] = jnp.transpose(total).astype(jnp.bfloat16)

    total = total_here(z)
    for d in range(1, 8):
        who = (z + d) % 8
        remote(kv_sum.at[0], z_got.at[who], z_send.at[0], z_recv.at[who], sibling).wait_recv()
        total = add(total, z_got[who])
    dk_out[...] = total[:, 0:DIM].astype(jnp.bfloat16)
    dv_out[...] = total[:, DIM:].astype(jnp.bfloat16)

    def sib_sent(s, c):
        sib_copy(s).wait_send()
        return c

    lax.fori_loop(0, 32, sib_sent, 0)

    def sent(d, c):
        zz = (z + d) % 8
        a_copy(zz).wait_send()
        b_copy(zz).wait_send()
        c_copy(zz).wait_send()
        return c

    lax.fori_loop(0, 8, sent, 0)

    def z_sent(d, c):
        z_copy((z + d) % 8).wait_send()
        return c

    lax.fori_loop(1, 8, z_sent, 0)
    x_a.wait_send()
    x_b.wait_send()
    x_c.wait_send()


def smem():
    return pl.BlockSpec(memory_space=pltpu.SMEM)


def vmem():
    return pl.BlockSpec(memory_space=pltpu.VMEM)


def hbm():
    return pl.BlockSpec(memory_space=pl.ANY)


def bf16(*shape):
    return jax.ShapeDtypeStruct(shape, jnp.bfloat16)


def f32(*shape):
    return jax.ShapeDtypeStruct(shape, jnp.float32)


def dma(*shape):
    return pltpu.SemaphoreType.DMA(shape)


def params(collective_id=None, vmem_mib=48):
    return pltpu.CompilerParams(
        collective_id=collective_id, has_side_effects=collective_id is not None, vmem_limit_bytes=vmem_mib << 20
    )


def gather_call(queries, exps, keys, values, outs, grads):
    return pl.pallas_call(
        gather_kernel,
        out_shape=(bf16(NQ, 2, WIDE, DIM), bf16(NK, 2, STRIPE, DIM), f32(NQ, HEADS, STRIPE)),
        in_specs=[vmem()] * 6,
        out_specs=(hbm(), hbm(), hbm()),
        scratch_shapes=[
            pltpu.VMEM((2, STRIPE, DIM), jnp.bfloat16),
            pltpu.VMEM((2, WIDE, DIM), jnp.bfloat16),
            pltpu.VMEM((HEADS, STRIPE), jnp.float32),
            dma(NK), dma(8), dma(8, 2), dma(8), dma(32), dma(2, 2), dma(2), dma(NQ, 2), dma(3), dma(NQ), dma(3),
        ],
        compiler_params=params(0),
        name="gather",
    )(queries, exps, keys, values, outs, grads)


def stats_call(order, win, qg, kv):
    return pl.pallas_call(
        stats_kernel,
        grid=(1,),
        out_shape=f32(2, NQ, WIDE),
        in_specs=[
            smem(),
            smem(),
            pl.BlockSpec((NQ, 1, WIDE, DIM), lambda i: (0, 0, 0, 0)),
            pl.BlockSpec((NK, 1, STRIPE, DIM), lambda i: (0, 0, 0, 0)),
        ],
        out_specs=pl.BlockSpec((2, NQ, WIDE), lambda i: (0, 0, 0)),
        scratch_shapes=[
            pltpu.SMEM((NK,), jnp.int32),
            pltpu.SMEM((NK + 1,), jnp.int32),
            pltpu.SMEM((NK + 1,), jnp.int32),
            pltpu.VMEM((8, WIDE), jnp.float32),
            pltpu.VMEM((8, WIDE), jnp.float32),
        ],
        compiler_params=params(),
        name="stats",
    )(order, win, qg, kv)


def norm_call(part):
    return pl.pallas_call(
        norm_kernel,
        out_shape=f32(NQ, WIDE),
        in_specs=[vmem()],
        out_specs=vmem(),
        scratch_shapes=[pltpu.VMEM((NQ, 2, NQ, WIDE), jnp.float32), dma(3), dma(NQ)],
        compiler_params=params(1),
        name="norm",
    )(part)


def grads_call(order, win, qg, kv, norm, delta):
    return pl.pallas_call(
        grads_kernel,
        out_shape=(bf16(NQ, DIM, WIDE), bf16(NK, STRIPE, 2 * DIM)),
        in_specs=[smem()] * 2 + [vmem()] * 4,
        out_specs=(vmem(), vmem()),
        scratch_shapes=[
            pltpu.SMEM((NK,), jnp.int32),
            pltpu.SMEM((NK + 1,), jnp.int32),
            pltpu.SMEM((NK + 1,), jnp.int32),
            pltpu.VMEM((NK, DIM, STRIPE), jnp.bfloat16),
            pltpu.VMEM((NK, STRIPE, 2 * DIM), jnp.float32),
            pltpu.VMEM((DIM, WIDE), jnp.float32),
            pltpu.VMEM((2, WIDE), jnp.float32),
        ],
        compiler_params=params(),
        name="grads",
    )(order, win, qg, kv, norm, delta)


def reduce_call(dq, dkv):
    tile = (STRIPE, 2 * DIM)
    return pl.pallas_call(
        reduce_kernel,
        out_shape=(bf16(STRIPE, WIDE), bf16(STRIPE, DIM), bf16(STRIPE, DIM)),
        in_specs=[vmem()] * 2,
        out_specs=(vmem(), vmem(), vmem()),
        scratch_shapes=[
            pltpu.VMEM((32, *tile), jnp.bfloat16),
            pltpu.VMEM((32, *tile), jnp.bfloat16),
            pltpu.VMEM((8, *tile), jnp.bfloat16),
            pltpu.VMEM((8, *tile), jnp.bfloat16),
            pltpu.VMEM((8, *tile), jnp.bfloat16),
            pltpu.VMEM((8, *tile), jnp.bfloat16),
            pltpu.VMEM((DIM, WIDE), jnp.bfloat16),
            pltpu.VMEM((DIM, WIDE), jnp.bfloat16),
            pltpu.VMEM((DIM, WIDE), jnp.bfloat16),
            pltpu.VMEM((DIM, WIDE), jnp.bfloat16),
            dma(32), dma(32), dma(8), dma(8), dma(8), dma(8), dma(8), dma(8), dma(8), dma(8), dma(3), dma(3),
        ],
        compiler_params=params(2),
        name="reduce",
    )(dq, dkv)


def per_device(
    queries, query_exps, key_head, value_head, forward_out, output_grad, stripe_order, window_size
):
    qg, kv, delta = gather_call(
        queries, query_exps.reshape(1, STRIPE), key_head, value_head, forward_out, output_grad
    )
    part = stats_call(stripe_order, window_size, qg, kv)
    norm = norm_call(part)
    dq, dkv = grads_call(stripe_order, window_size, qg, kv, norm, delta)
    return reduce_call(dq, dkv)


def solution(mesh):
    return jax.shard_map(
        per_device,
        mesh=mesh,
        in_specs=(
            P(("row", "col"), None),
            P(("row", "col")),
            P(("col", "row"), None),
            P(("col", "row"), None),
            P(("row", "col"), None),
            P(("row", "col"), None),
            P(),
            P(),
        ),
        out_specs=(P(("row", "col"), None), P(("col", "row"), None), P(("col", "row"), None)),
        check_vma=False,
    )
```

time: 299 us -> 170 us (0.57)
  waiting for transfers between devices: 115 us -> 0 us
  Pallas kernels: 63.5 us -> 157 us
  blocking collectives: 67.8 us -> 0 us
  starting transfers between devices: 34.7 us -> 0 us
  other arithmetic: 4.78 us -> 0 us
    all_to_all x5 -> x0, waiting for transfers between devices: 115 us -> none  [the longest x3 60.3 us: from_everyone(): return lax.all_to_all(copies, axis, split_axis=0, concat_axis=0, tiled=True)]
    pallas_call x2 -> x5, Pallas kernels: 63.5 us -> 157 us  [the longest x1 59.1 us: reduce_call(): pl.pallas_call(reduce_kernel, out_shape=(bf16(STRIPE, WIDE), bf16(STRIPE,...]
    all_to_all x3 -> x0, blocking collectives: 67.8 us -> none  [the longest x2 38.2 us: from_everyone(): return lax.all_to_all(copies, axis, split_axis=0, concat_axis=0, tiled=True)]
    all_to_all x5 -> x0, starting transfers between devices: 34.7 us -> none  [the longest x3 22 us: from_everyone(): return lax.all_to_all(copies, axis, split_axis=0, concat_axis=0, tiled=True)]
    unnamed x18 -> x21, local copies, waits for them, and re-layouts: 1.86 us -> 9.81 us
    broadcast_in_dim x5 -> x0, local copies, waits for them, and re-layouts: 5.31 us -> none  [from_everyone(): copies = jnp.broadcast_to(value, (lax.axis_size(axis), *value.shape))]
    reduce_sum x4 -> x0, other arithmetic: 3.53 us -> none  [the longest x1 1.88 us: per_device(): dkv = dkv.astype(jnp.float32).sum(0).astype(jnp.bfloat16)]
  transfers between devices with their start and end apart: 5 -> 0, of which waited for: 5 -> 0; matrix products, arithmetic and copies ran while one was open for 2% -> 0% of each run, Pallas kernels for 6% -> 0%
where the time goes in v2:
time: 170 us; the launch traced here: 169 us
  Pallas kernels  157 us (92%)
  local copies, waits for them, and re-layouts  9.81 us (6%)
    pallas_call x1, Pallas kernels, reduce_call(): pl.pallas_call(reduce_kernel, out_shape=(bf16(STRIPE, WIDE), bf16(STRIPE,...  59.1 us
    pallas_call x1, Pallas kernels, grads_call(): pl.pallas_call(grads_kernel, out_shape=(bf16(NQ, DIM, WIDE), bf16(NK, STR...  41.1 us
    pallas_call x1, Pallas kernels, gather_call(): pl.pallas_call(gather_kernel, out_shape=(bf16(NQ, 2, WIDE, DIM), bf16(NK,...  34.7 us
    pallas_call x1, Pallas kernels, stats_call(): pl.pallas_call(stats_kernel, grid=(1,), out_shape=f32(2, NQ, WIDE), in_sp...  14.9 us
    unnamed x21, local copies, waits for them, and re-layouts  9.81 us
    pallas_call x1, Pallas kernels, norm_call(): pl.pallas_call(norm_kernel, out_shape=f32(NQ, WIDE), in_specs=[vmem()], o...  7.58 us

profile of v2, /device:TPU:4, one launch (start us, length us, event | category | flops | bytes accessed | tf_op | source)
XLA Modules:
  0.0 168.6 jit_solution(13942560264283064168)
XLA Ops:
  0.6 0.0 copy-start.7
  1.3 0.0 copy-start.1
  1.3 0.9 copy-done.1
  2.3 0.0 copy-start.2
  2.3 0.9 copy-done.2
  3.2 0.0 copy-start.3
  3.2 0.9 copy-done.3
  4.2 0.0 copy-start.4
  4.2 0.8 copy-done.4
  4.9 0.0 copy-start.5
  4.9 0.8 copy-done.5
  5.7 0.0 copy-start.8
  5.7 0.7 copy-done.8
  6.3 34.7 %gather.1 = (bf16[4,2,1024,128]{3,2,1,0:T(8,128)(2,1)S(1)}, bf16[64,2,128,128]{3,2,1,0:T(8,128)(2,1)}, f32[4,8,128]{2,1,0:T(8,128)S(1)}) custom-call(bf16[128,1024]{1,0:T(8,128)(2,1)S(1)} %copy-done.1, s32[1,128]{1,0:T(1,128)S(1)} %bitcast.1, bf16[128,128]{1,0:T(8,128)(2,1)S(1)} %copy-done.4, bf16[128,128]{1,0:T(8,128)(2,1)S(1)} %copy-done.5, ...), custom_call_target="tpu_custom_call" | custom-call | tf_op jit(solution)/shard_map/gather/pallas_call | solution.py:570
  41.1 0.0 copy-start.6
  41.1 0.7 copy-done.6
  41.8 14.9 %stats.1.part_ref = f32[2,4,1024]{2,1,0:T(4,128)S(1)} custom-call(s32[256]{0:T(256)S(1)} %copy-done.6, s32[1]{0:T(128)S(6)} %copy.14.win, bf16[4,2,1024,128]{3,2,1,0:T(8,128)(2,1)S(1)} %get-tuple-element.8.q_ref.qg_ref, bf16[64,2,128,128]{3,2,1,0:T(8,128)(2,1)} %get-tuple-element.9.k_ref.kv_ref), custom_call_target="tpu_custom_call" | custom-call | tf_op jit(solution)/shard_map/stats/pallas_call | solution.py:587
  56.7 7.6 %norm.1.norm_ref = f32[4,1024]{1,0:T(4,128)S(1)} custom-call(f32[2,4,1024]{2,1,0:T(4,128)S(1)} %stats.1.part_ref), custom_call_target="tpu_custom_call" | custom-call | tf_op jit(solution)/shard_map/norm/pallas_call | solution.py:611
  64.3 0.0 copy-done.7
  64.3 41.1 %grads.1 = (bf16[4,128,1024]{2,1,0:T(8,128)(2,1)S(1)}, bf16[64,128,256]{2,1,0:T(8,128)(2,1)}) custom-call(s32[256]{0:T(256)S(1)} %copy-done.7, s32[1]{0:T(128)S(6)} %copy.14.win, bf16[4,2,1024,128]{3,2,1,0:T(8,128)(2,1)S(1)} %get-tuple-element.8.q_ref.qg_ref, bf16[64,2,128,128]{3,2,1,0:T(8,128)(2,1)} %get-tuple-element.9.k_ref.kv_ref, ...), custom_call_target="tpu_custom_call" | custom-call | tf_op jit(solution)/shard_map/grads/pallas_call | solution.py:623
  105.4 0.0 copy-start
  105.4 2.2 %copy-done = bf16[64,128,256]{2,1,0:T(8,128)(2,1)S(1)} copy-done((bf16[64,128,256]{2,1,0:T(8,128)(2,1)S(1)}, bf16[64,128,256]{2,1,0:T(8,128)(2,1)}, u32[]{:S(2)}) %copy-start) | copy-done | bytes 4194328
  107.6 59.1 %reduce.1 = (bf16[128,1024]{1,0:T(8,128)(2,1)S(1)}, bf16[128,128]{1,0:T(8,128)(2,1)S(1)}, bf16[128,128]{1,0:T(8,128)(2,1)S(1)}) custom-call(bf16[4,128,1024]{2,1,0:T(8,128)(2,1)S(1)} %get-tuple-element.11.dq_ref, bf16[64,128,256]{2,1,0:T(8,128)(2,1)S(1)} %copy-done), custom_call_target="tpu_custom_call" | custom-call | tf_op jit(solution)/shard_map/reduce/pallas_call | solution.py:644
  166.7 0.7 copy.15
  167.4 0.6 copy.16
  168.0 0.6 copy.17
Async XLA Ops:
  0.6 63.7 %copy-start.7 = (s32[256]{0:T(256)S(1)}, s32[256]{0:T(256)}, u32[]{:S(2)}) copy-start(s32[256]{0:T(256)} %order.3) | copy-start | bytes 3076
  1.3 1.0 copy-start.1
  2.3 0.9 copy-start.2
  3.2 0.9 copy-start.3
  4.2 0.8 copy-start.4
  4.9 0.8 copy-start.5
  5.7 0.7 copy-start.8
  41.1 0.7 copy-start.6
  105.4 2.2 %copy-start = (bf16[64,128,256]{2,1,0:T(8,128)(2,1)S(1)}, bf16[64,128,256]{2,1,0:T(8,128)(2,1)}, u32[]{:S(2)}) copy-start(bf16[64,128,256]{2,1,0:T(8,128)(2,1)} %get-tuple-element.12.kv_ref) | copy-start | bytes 12582916

commit v3 on v2

--- a/solution.py
+++ b/solution.py
@@ -64,19 +64,25 @@
     n = lax.fori_loop(0, NK, one, jnp.int32(0), unroll=8)
     idx[n] = 0
     gap[n] = FAR
-    return (n + 1) // 2
-
-
-def pair_mask(g0, g1, window):
+    return n
+
+
+def over_list(n, step):
+    fours = n // 4
+    lax.fori_loop(0, fours, lambda t, c: step(4, 4 * t, c), 0)
+    lax.fori_loop(2 * fours, (n + 1) // 2, lambda t, c: step(2, 2 * t, c), 0)
+
+
+def tile_mask(gaps, window):
     delta = lax.broadcasted_iota(jnp.int32, (STRIPE, STRIPE), 1) - lax.broadcasted_iota(
         jnp.int32, (STRIPE, STRIPE), 0
     )
     parts = []
-    for g in (g0, g1):
+    for g in gaps:
         distance = delta + g
         parts.append((distance >= 0) & (distance < window))
-    both = jnp.concatenate(parts, axis=0)
-    return jnp.concatenate([both, both], axis=1)
+    rows = jnp.concatenate(parts, axis=0)
+    return jnp.concatenate([rows, rows], axis=1)
 
 
 def dot_nt(a, b):
@@ -87,23 +93,22 @@
     return lax.dot_general(a, b, (((1,), (0,)), ((), ())), preferred_element_type=jnp.float32)
 
 
-def stats_kernel(order, win, q_ref, k_ref, out_ref, k_pos, idx, gap, m_ref, l_ref):
+def stats_kernel(order, win, qg_ref, kv_ref, out_ref, k_pos, idx, gap, m_ref, l_ref):
     window = win[0]
     key_positions(order, k_pos)
 
     def per_query(j, carry):
-        steps = build_list(query_position(order, j), k_pos, window, idx, gap)
+        n = build_list(query_position(order, j), k_pos, window, idx, gap)
         m_ref[...] = jnp.full_like(m_ref, NEG)
         l_ref[...] = jnp.zeros_like(l_ref)
 
-        def step(t, c):
-            i0, i1 = idx[2 * t], idx[2 * t + 1]
-            keys = jnp.concatenate([k_ref[i0, 0], k_ref[i1, 0]], axis=0)
-            mask = pair_mask(gap[2 * t], gap[2 * t + 1], window)
+        def step(group, first, c):
+            keys = jnp.concatenate([kv_ref[idx[first + i], 0] for i in range(group)], axis=0)
+            mask = tile_mask([gap[first + i] for i in range(group)], window)
             for b in range(HEADS // 2):
                 cols = pl.ds(b * 256, 256)
-                s = dot_nt(keys, q_ref[j, 0, cols, :])
-                s = jnp.where(mask, s, NEG).reshape(32, 8, 256)
+                s = dot_nt(keys, qg_ref[j, 0, cols, :])
+                s = jnp.where(mask, s, NEG).reshape(group * 16, 8, 256)
                 m_old = m_ref[:, cols]
                 m_new = jnp.maximum(m_old, jnp.max(s, axis=0))
                 e = jnp.exp2((s - m_new[None]) * SCALE2)
@@ -111,7 +116,7 @@
                 m_ref[:, cols] = m_new
             return c
 
-        lax.fori_loop(0, steps, step, 0)
+        over_list(n, step)
         m_all = m_ref[...]
         top = jnp.max(m_all, axis=0, keepdims=True)
         total = jnp.sum(l_ref[...] * jnp.exp2((m_all - top) * SCALE2), axis=0, keepdims=True)
@@ -123,51 +128,50 @@
 
 
 def grads_kernel(
-    order, win, qg_ref, kv_ref, norm_ref, delta_ref, dq_ref, dkv_ref, k_pos, idx, gap, kt_ref, acc_ref, dq_acc, stat_ref
+    order, win, qg_ref, kv_ref, norm_ref, delta_ref, dq_ref, dkv_ref, k_pos, idx, gap, acc_ref, dq_acc, stat_ref
 ):
     window = win[0]
     key_positions(order, k_pos)
 
     def clear(k, c):
         acc_ref[k] = jnp.zeros((STRIPE, 2 * DIM), jnp.float32)
-        kt_ref[k] = jnp.transpose(kv_ref[k, 0].astype(jnp.float32)).astype(jnp.bfloat16)
         return c
 
     lax.fori_loop(0, NK, clear, 0)
 
     def per_query(j, carry):
-        steps = build_list(query_position(order, j), k_pos, window, idx, gap)
+        n = build_list(query_position(order, j), k_pos, window, idx, gap)
         dq_acc[...] = jnp.zeros_like(dq_acc)
         stat_ref[0:1, :] = norm_ref[pl.ds(j, 1), :]
         for h in range(HEADS):
             stat_ref[1:2, h * DIM : (h + 1) * DIM] = delta_ref[j, h : h + 1, :]
 
-        def step(t, c):
-            i0, i1 = idx[2 * t], idx[2 * t + 1]
-            keys = jnp.concatenate([kv_ref[i0, 0], kv_ref[i1, 0]], axis=0)
-            vals = jnp.concatenate([kv_ref[i0, 1], kv_ref[i1, 1]], axis=0)
-            keys_t = jnp.concatenate([kt_ref[i0], kt_ref[i1]], axis=1)
-            mask = pair_mask(gap[2 * t], gap[2 * t + 1], window)
-            dk = jnp.zeros((2 * STRIPE, DIM), jnp.float32)
-            dv = jnp.zeros((2 * STRIPE, DIM), jnp.float32)
+        def step(group, first, c):
+            at = [idx[first + i] for i in range(group)]
+            keys = jnp.concatenate([kv_ref[i, 0] for i in at], axis=0)
+            vals = jnp.concatenate([kv_ref[i, 1] for i in at], axis=0)
+            keys_t = jnp.transpose(keys)
+            mask = tile_mask([gap[first + i] for i in range(group)], window)
+            weights, score_grads = [], []
             for b in range(HEADS // 2):
                 cols = pl.ds(b * 256, 256)
-                q = qg_ref[j, 0, cols, :]
-                g = qg_ref[j, 1, cols, :]
-                s = dot_nt(keys, q)
+                s = dot_nt(keys, qg_ref[j, 0, cols, :])
                 p = jnp.where(mask, jnp.exp2(s * SCALE2 - stat_ref[0:1, cols]), 0.0)
-                w = dot_nt(vals, g)
-                ds = (p * (w - stat_ref[1:2, cols])).astype(jnp.bfloat16)
-                dv += dot_nn(p.astype(jnp.bfloat16), g)
-                dk += dot_nn(ds, q)
-                dq_acc[:, cols] += dot_nn(keys_t, ds)
-            for n, i in enumerate((i0, i1)):
-                rows = slice(n * STRIPE, (n + 1) * STRIPE)
-                acc_ref[i, :, 0:DIM] += dk[rows]
-                acc_ref[i, :, DIM:] += dv[rows]
+                w = dot_nt(vals, qg_ref[j, 1, cols, :])
+                score_grads.append((p * (w - stat_ref[1:2, cols])).astype(jnp.bfloat16))
+                weights.append(p.astype(jnp.bfloat16))
+            weights = jnp.concatenate(weights, axis=1)
+            score_grads = jnp.concatenate(score_grads, axis=1)
+            dv = dot_nn(weights, qg_ref[j, 1])
+            dk = dot_nn(score_grads, qg_ref[j, 0])
+            dq_acc[...] += dot_nn(keys_t, score_grads)
+            for i, k in enumerate(at):
+                rows = slice(i * STRIPE, (i + 1) * STRIPE)
+                acc_ref[k, :, 0:DIM] += dk[rows]
+                acc_ref[k, :, DIM:] += dv[rows]
             return c
 
-        lax.fori_loop(0, steps, step, 0)
+        over_list(n, step)
         dq_ref[j] = (dq_acc[...] * SCALE).astype(jnp.bfloat16)
         return carry
 
@@ -203,9 +207,19 @@
 
 
 def gather_kernel(
-    q_ref, exp_ref, k_ref, v_ref, o_ref, g_ref, qg_out, kv_out, delta_out,
-    kv_own, qg_own, delta_own, kv_recv, z_send, y_send, y_pass, sib_send, x_send, x_pass, x_recv, d_send, d_recv, local,
+    q_in, exp_in, k_in, v_in, o_in, g_in, qg_out, kv_out, delta_out,
+    q_ref, exp_ref, o_ref, g_ref, kv_own, qg_own, delta_own,
+    kv_recv, z_send, y_send, y_pass, sib_send, x_send, x_pass, x_recv, d_send, d_recv, local, load,
 ):
+    loads = [
+        pltpu.make_async_copy(src, dst, load.at[n])
+        for n, (src, dst) in enumerate(
+            ((k_in, kv_own.at[0]), (v_in, kv_own.at[1]), (exp_in, exp_ref), (q_in, q_ref), (g_in, g_ref), (o_in, o_ref))
+        )
+    ]
+    for copy in loads:
+        copy.start()
+
     x, y, z, core = coords()
     mine = slot_of(y, z, core)
     sibling = device(x, y, z, 1 - core)
@@ -213,56 +227,120 @@
     sign = 1 - 2 * core
     x_to, x_from = (x + sign + 4) % 4, (x - sign + 4) % 4
 
-    greet(plane_peers(x, y, z, core) + [device((x + 2) % 4, y, z, core)])
-
-    kv_own[0] = k_ref[...]
-    kv_own[1] = v_ref[...]
-
-    def z_copy(d):
-        return remote(
-            kv_own, kv_out.at[mine], z_send.at[d], kv_recv.at[mine], device(x, y, (z + d) % 8, core)
-        )
-
-    for d in (1, 7, 2, 6, 3, 5, 4):
-        z_copy(d).start()
-
+    greet(
+        [device(x, y, z, 1 - core)]
+        + [device((x + d) % 4, y, z, core) for d in (1, 3, 2)]
+        + [device(x, (y + d) % 4, z, core) for d in (1, 3)]
+        + [device(x, y, (z + d) % 8, core) for d in (1, 7)]
+    )
+
+    def slot_copy(s, src, send, to):
+        return remote(src, kv_out.at[s], send, kv_recv.at[s], to)
+
+    def arrived(s):
+        slot_copy(s, kv_own, local.at[0], sibling).wait_recv()
+
+    def z_copy(d, src, up):
+        to = device(x, y, (z + (1 if up else 7)) % 8, core)
+        return slot_copy(slot_of(y, (z + d) % 8, core), src, z_send.at[d, 0 if up else 1], to)
+
+    def y_copy(d, src, up):
+        to = device(x, y_up if up else y_down, z, core)
+        return slot_copy(slot_of(y, (z + d) % 8, core), src, y_send.at[d, 0 if up else 1], to)
+
+    def y_onward(d, up):
+        s = slot_of(y_down if up else y_up, (z + d) % 8, core)
+        return slot_copy(s, kv_out.at[s], y_pass.at[d], device(x, y_up if up else y_down, z, core))
+
+    def sib_copy(s, src):
+        return slot_copy(s, src, sib_send.at[s % 32], sibling)
+
+    def spread(d, src):
+        y_copy(d, src, True).start()
+        y_copy(d, src, False).start()
+        sib_copy(slot_of(y, (z + d) % 8, core), src).start()
+
+    loads[0].wait()
+    loads[1].wait()
+    z_copy(0, kv_own, True).start()
+    z_copy(0, kv_own, False).start()
+    spread(0, kv_own)
+
+    loads[2].wait()
+    loads[3].wait()
     scale = jnp.transpose(jnp.broadcast_to(jnp.exp2(exp_ref[...].astype(jnp.float32)), (STRIPE, STRIPE)))
 
     def x_copy(p, n):
-        return remote(
-            qg_own.at[p], qg_out.at[x, p], x_send.at[p, n], x_recv.at[x, p], device((x + 1 + 2 * n) % 4, y, z, core)
-        )
+        to = device((x + 1 + 2 * n) % 4, y, z, core)
+        return remote(qg_own.at[p], qg_out.at[x, p], x_send.at[p, n], x_recv.at[x, p], to)
 
     for h in range(HEADS):
         cols = slice(h * DIM, (h + 1) * DIM)
         qg_own[0, cols, :] = (q_ref[:, cols].astype(jnp.float32) * scale).astype(jnp.bfloat16)
-    for n in range(2):
-        x_copy(0, n).start()
+    x_copy(0, 0).start()
+    x_copy(0, 1).start()
+
+    def x_arrived(who, p):
+        remote(qg_own.at[p], qg_out.at[who, p], local.at[0], x_recv.at[who, p], sibling).wait_recv()
+
+    def x_forward(p):
+        block = qg_out.at[x_from, p]
+        return remote(block, block, x_pass.at[p], x_recv.at[x_from, p], device(x_to, y, z, core))
+
+    def from_z(d, up, onward):
+        s = slot_of(y, (z + d) % 8, core)
+        arrived(s)
+        if onward is True:
+            z_copy(d, kv_out.at[s], up).start()
+        elif onward is not None:
+            @pl.when(onward)
+            def _():
+                z_copy(d, kv_out.at[s], up).start()
+        spread(d, kv_out.at[s])
+
+    def from_y(d):
+        zz = (z + d) % 8
+        below, above = slot_of(y_down, zz, core), slot_of(y_up, zz, core)
+        arrived(below)
+        if d < 4:
+            y_onward(d, True).start()
+        sib_copy(below, kv_out.at[below]).start()
+        arrived(above)
+        if d >= 4:
+            y_onward(d, False).start()
+        sib_copy(above, kv_out.at[above]).start()
+
+    loads[4].wait()
     for h in range(HEADS):
         cols = slice(h * DIM, (h + 1) * DIM)
         qg_own[1, cols, :] = g_ref[:, cols]
-    for n in range(2):
-        x_copy(1, n).start()
+
+    from_z(7, True, True)
+    from_z(1, False, True)
 
     own_kv = pltpu.make_async_copy(kv_own, kv_out.at[mine], local.at[0])
     own_qg = pltpu.make_async_copy(qg_own, qg_out.at[x], local.at[1])
     own_kv.start()
     own_qg.start()
 
-    def y_copy(s, src, d, up):
-        to = y_up if up else y_down
-        return remote(src, kv_out.at[s], y_send.at[d, 0 if up else 1], kv_recv.at[s], device(x, to, z, core))
-
-    def sib_copy(s, src):
-        return remote(src, kv_out.at[s], sib_send.at[s % 32], kv_recv.at[s], sibling)
-
-    def arrived(s):
-        remote(kv_own, kv_out.at[s], local.at[0], kv_recv.at[s], sibling).wait_recv()
-
-    y_copy(mine, kv_own, 0, True).start()
-    y_copy(mine, kv_own, 0, False).start()
-    sib_copy(mine, kv_own).start()
-
+    from_z(6, True, True)
+    from_z(2, False, True)
+    from_y(0)
+
+    x_arrived(x_from, 0)
+    x_forward(0).start()
+    x_copy(1, 0).start()
+    x_copy(1, 1).start()
+
+    from_z(5, True, core == 0)
+    from_z(3, False, core == 1)
+    from_y(1)
+    from_y(7)
+    from_z(4, True, None)
+    from_y(2)
+    from_y(6)
+
+    loads[5].wait()
     for h in range(HEADS):
         cols = slice(h * DIM, (h + 1) * DIM)
         product = g_ref[:, cols].astype(jnp.float32) * o_ref[:, cols].astype(jnp.float32)
@@ -277,58 +355,16 @@
     own_delta = pltpu.make_async_copy(delta_own, delta_out.at[x], local.at[2])
     own_delta.start()
 
-    def from_z(d, c):
-        s = slot_of(y, (z + d) % 8, core)
-        arrived(s)
-        y_copy(s, kv_out.at[s], d, True).start()
-        y_copy(s, kv_out.at[s], d, False).start()
-        sib_copy(s, kv_out.at[s]).start()
-        return c
-
-    def x_arrived(who, p):
-        remote(qg_own.at[p], qg_out.at[who, p], local.at[0], x_recv.at[who, p], sibling).wait_recv()
-
-    def x_forward(p):
-        return remote(
-            qg_out.at[x_from, p], qg_out.at[x_from, p], x_pass.at[p], x_recv.at[x_from, p], device(x_to, y, z, core)
-        )
-
-    def from_y(lower, upper):
-        def body(d, c):
-            zz = (z + d) % 8
-            below, above = slot_of(y_down, zz, core), slot_of(y_up, zz, core)
-            arrived(below)
-            if lower:
-                y_onward(below, d, True).start()
-            sib_copy(below, kv_out.at[below]).start()
-            arrived(above)
-            if upper:
-                y_onward(above, d, False).start()
-            sib_copy(above, kv_out.at[above]).start()
-            return c
-
-        return body
-
-    def y_onward(s, d, up):
-        to = y_up if up else y_down
-        return remote(kv_out.at[s], kv_out.at[s], y_pass.at[d], kv_recv.at[s], device(x, to, z, core))
-
-    for d in (1, 7, 2, 6, 3, 5, 4):
-        from_z(d, 0)
-    x_arrived(x_from, 0)
-    x_forward(0).start()
-    lax.fori_loop(0, 4, from_y(True, False), 0)
+    from_y(3)
+    from_y(5)
+    from_y(4)
     x_arrived(x_from, 1)
     x_forward(1).start()
-    lax.fori_loop(4, 8, from_y(False, True), 0)
-
-    def from_far(d, c):
+
+    for d in (0, 1, 7, 2, 6, 3, 5, 4):
         s = slot_of((y + 2) % 4, (z + d) % 8, core)
         arrived(s)
         sib_copy(s, kv_out.at[s]).start()
-        return c
-
-    lax.fori_loop(0, 8, from_far, 0)
 
     for p in range(2):
         x_arrived(x_to, p)
@@ -344,9 +380,9 @@
     lax.fori_loop(0, 32, from_sibling, 0)
 
     def sent(d, c):
-        y_copy(mine, kv_own, d, True).wait_send()
-        y_copy(mine, kv_own, d, False).wait_send()
-        y_onward(mine, d, True).wait_send()
+        y_copy(d, kv_own, True).wait_send()
+        y_copy(d, kv_own, False).wait_send()
+        slot_copy(mine, kv_own, y_pass.at[d], sibling).wait_send()
         return c
 
     lax.fori_loop(0, 8, sent, 0)
@@ -356,11 +392,20 @@
         return c
 
     lax.fori_loop(0, 32, sib_sent, 0)
-    for d in range(1, 8):
-        z_copy(d).wait_send()
+    for d, up in ((0, True), (0, False), (7, True), (1, False), (6, True), (2, False)):
+        z_copy(d, kv_own, up).wait_send()
+
+    @pl.when(core == 0)
+    def _():
+        z_copy(5, kv_own, True).wait_send()
+
+    @pl.when(core == 1)
+    def _():
+        z_copy(3, kv_own, False).wait_send()
+
     for p in range(2):
-        for n in range(2):
-            x_copy(p, n).wait_send()
+        x_copy(p, 0).wait_send()
+        x_copy(p, 1).wait_send()
         x_forward(p).wait_send()
     for n in range(3):
         d_copy(n).wait_send()
@@ -412,22 +457,18 @@
     def sib_copy(s):
         return remote(kv_ref.at[(1 - core) * 32 + s], sib_got.at[s], sib_send.at[s], sib_recv.at[s], sibling)
 
-    def sib_start(yy):
-        def body(d, c):
-            sib_copy(yy * 8 + (z + d) % 8).start()
-            return c
-
-        lax.fori_loop(0, 8, body, 0)
-
-    sib_start(y_opp)
+    far_first = (4, 3, 5, 2, 6, 1, 7, 0)
+
     x_a = remote(dq_ref.at[x_over], x_opp, x_send.at[0], x_recv.at[0], dev_to)
     x_b = remote(dq_ref.at[x_back], x_near, x_send.at[1], x_recv.at[1], dev_back)
     x_c = remote(x_sum, x_far, x_send.at[2], x_recv.at[2], dev_to)
-    x_a.start()
-    sib_start(y_back)
-    x_b.start()
-    sib_start(y_to)
-    sib_start(y)
+    for d in far_first:
+        zz = (z + d) % 8
+        for yy in (y_opp, y_back, y_to, y):
+            sib_copy(yy * 8 + zz).start()
+        if d == 3:
+            x_a.start()
+            x_b.start()
 
     def with_sibling(s):
         sib_copy(s).wait_recv()
@@ -445,28 +486,25 @@
     def z_copy(zz):
         return remote(kv_sum.at[y * 8 + zz], z_got.at[z], z_send.at[zz], z_recv.at[z], device(x, y, zz, core))
 
-    def step_a(d, c):
+    def step_a(d):
         zz = (z + d) % 8
         s = y_opp * 8 + zz
         kv_sum[s] = with_sibling(s).astype(jnp.bfloat16)
         a_copy(zz).start()
-        return c
-
-    def step_b(d, c):
+
+    def step_b(d):
         zz = (z + d) % 8
         s = y_back * 8 + zz
         kv_sum[s] = with_sibling(s).astype(jnp.bfloat16)
         b_copy(zz).start()
-        return c
-
-    def step_c(d, c):
+
+    def step_c(d):
         zz = (z + d) % 8
         s = y_to * 8 + zz
         total = with_sibling(s)
         a_copy(zz).wait_recv()
         kv_sum[s] = add(total, opp_got[zz]).astype(jnp.bfloat16)
         c_copy(zz).start()
-        return c
 
     def total_here(zz):
         s = y * 8 + zz
@@ -475,26 +513,28 @@
         c_copy(zz).wait_recv()
         return add(total, near_got[zz], far_got[zz])
 
-    def step_z(d, c):
+    def step_z(d):
         zz = (z + d) % 8
         kv_sum[y * 8 + zz] = total_here(zz).astype(jnp.bfloat16)
         z_copy(zz).start()
-        return c
-
-    lax.fori_loop(1, 9, step_a, 0)
-    lax.fori_loop(1, 9, step_b, 0)
-
-    x_a.wait_recv()
+
     def sum_x(h, c):
         rows = pl.ds(pl.multiple_of(h * 16, 16), 16)
         x_sum[rows, :] = add(dq_ref[x_to, rows, :], x_opp[rows, :]).astype(jnp.bfloat16)
         return c
 
-    lax.fori_loop(0, 8, sum_x, 0)
-    x_c.start()
-
-    lax.fori_loop(1, 9, step_c, 0)
-    lax.fori_loop(1, 8, step_z, 0)
+    for n in range(11):
+        if n < 8:
+            step_a(far_first[n])
+            step_b(far_first[n])
+        if 0 <= n - 1 < 8:
+            step_c(far_first[n - 1])
+        if 0 <= n - 3 < 7:
+            step_z(far_first[n - 3])
+        if n == 6:
+            x_a.wait_recv()
+            lax.fori_loop(0, 8, sum_x, 0)
+            x_c.start()
 
     x_b.wait_recv()
     x_c.wait_recv()
@@ -570,15 +610,19 @@
     return pl.pallas_call(
         gather_kernel,
         out_shape=(bf16(NQ, 2, WIDE, DIM), bf16(NK, 2, STRIPE, DIM), f32(NQ, HEADS, STRIPE)),
-        in_specs=[vmem()] * 6,
+        in_specs=[hbm()] * 6,
         out_specs=(hbm(), hbm(), hbm()),
         scratch_shapes=[
+            pltpu.VMEM((STRIPE, WIDE), jnp.bfloat16),
+            pltpu.VMEM((1, STRIPE), jnp.int32),
+            pltpu.VMEM((STRIPE, WIDE), jnp.bfloat16),
+            pltpu.VMEM((STRIPE, WIDE), jnp.bfloat16),
             pltpu.VMEM((2, STRIPE, DIM), jnp.bfloat16),
             pltpu.VMEM((2, WIDE, DIM), jnp.bfloat16),
             pltpu.VMEM((HEADS, STRIPE), jnp.float32),
-            dma(NK), dma(8), dma(8, 2), dma(8), dma(32), dma(2, 2), dma(2), dma(NQ, 2), dma(3), dma(NQ), dma(3),
+            dma(NK), dma(8, 2), dma(8, 2), dma(8), dma(32), dma(2, 2), dma(2), dma(NQ, 2), dma(3), dma(NQ), dma(3), dma(6),
         ],
-        compiler_params=params(0),
+        compiler_params=params(0, 8),
         name="gather",
     )(queries, exps, keys, values, outs, grads)
 
@@ -586,15 +630,9 @@
 def stats_call(order, win, qg, kv):
     return pl.pallas_call(
         stats_kernel,
-        grid=(1,),
         out_shape=f32(2, NQ, WIDE),
-        in_specs=[
-            smem(),
-            smem(),
-            pl.BlockSpec((NQ, 1, WIDE, DIM), lambda i: (0, 0, 0, 0)),
-            pl.BlockSpec((NK, 1, STRIPE, DIM), lambda i: (0, 0, 0, 0)),
-        ],
-        out_specs=pl.BlockSpec((2, NQ, WIDE), lambda i: (0, 0, 0)),
+        in_specs=[smem()] * 2 + [vmem()] * 2,
+        out_specs=vmem(),
         scratch_shapes=[
             pltpu.SMEM((NK,), jnp.int32),
             pltpu.SMEM((NK + 1,), jnp.int32),
@@ -602,7 +640,7 @@
             pltpu.VMEM((8, WIDE), jnp.float32),
             pltpu.VMEM((8, WIDE), jnp.float32),
         ],
-        compiler_params=params(),
+        compiler_params=params(None, 16),
         name="stats",
     )(order, win, qg, kv)
 
@@ -614,7 +652,7 @@
         in_specs=[vmem()],
         out_specs=vmem(),
         scratch_shapes=[pltpu.VMEM((NQ, 2, NQ, WIDE), jnp.float32), dma(3), dma(NQ)],
-        compiler_params=params(1),
+        compiler_params=params(1, 4),
         name="norm",
     )(part)
 
@@ -629,12 +667,11 @@
             pltpu.SMEM((NK,), jnp.int32),
             pltpu.SMEM((NK + 1,), jnp.int32),
             pltpu.SMEM((NK + 1,), jnp.int32),
-            pltpu.VMEM((NK, DIM, STRIPE), jnp.bfloat16),
             pltpu.VMEM((NK, STRIPE, 2 * DIM), jnp.float32),
             pltpu.VMEM((DIM, WIDE), jnp.float32),
             pltpu.VMEM((2, WIDE), jnp.float32),
         ],
-        compiler_params=params(),
+        compiler_params=params(None, 32),
         name="grads",
     )(order, win, qg, kv, norm, delta)
 
@@ -659,7 +696,7 @@
             pltpu.VMEM((DIM, WIDE), jnp.bfloat16),
             dma(32), dma(32), dma(8), dma(8), dma(8), dma(8), dma(8), dma(8), dma(8), dma(8), dma(3), dma(3),
         ],
-        compiler_params=params(2),
+        compiler_params=params(2, 20),
         name="reduce",
     )(dq, dkv)
 

time: 170 us -> 131 us (0.77)
  the two profiles are of different devices: /device:TPU:4 before, /device:TPU:6 now
where the time goes in v3:
time: 131 us; the launch traced here: 130 us
  Pallas kernels  121 us (92%)
  local copies, waits for them, and re-layouts  7.62 us (6%)
  between operations  1.34 us (1%)
    pallas_call x1, Pallas kernels, reduce_call(): pl.pallas_call(reduce_kernel, out_shape=(bf16(STRIPE, WIDE), bf16(STRIPE,...  38.8 us
    pallas_call x1, Pallas kernels, gather_call(): pl.pallas_call(gather_kernel, out_shape=(bf16(NQ, 2, WIDE, DIM), bf16(NK,...  34.1 us
    pallas_call x1, Pallas kernels, grads_call(): pl.pallas_call(grads_kernel, out_shape=(bf16(NQ, DIM, WIDE), bf16(NK, STR...  27.4 us
    pallas_call x1, Pallas kernels, stats_call(): pl.pallas_call(stats_kernel, out_shape=f32(2, NQ, WIDE), in_specs=[smem()...  14.8 us
    unnamed x17, local copies, waits for them, and re-layouts  7.62 us
    pallas_call x1, Pallas kernels, norm_call(): pl.pallas_call(norm_kernel, out_shape=f32(NQ, WIDE), in_specs=[vmem()], o...  6.45 us

profile of v3, /device:TPU:6, one launch (start us, length us, event | category | flops | bytes accessed | tf_op | source)
XLA Modules:
  0.0 130.4 jit_solution(12005864127049451203)
XLA Ops:
  1.3 0.0 copy-start
  1.3 0.9 copy-done
  2.2 0.0 copy-start.1
  2.2 0.9 copy-done.1
  3.2 0.0 copy-start.2
  3.2 0.9 copy-done.2
  4.1 0.0 copy-start.3
  4.1 0.8 copy-done.3
  4.9 0.0 copy-start.4
  4.9 0.8 copy-done.4
  5.6 0.0 copy-start.6
  5.7 0.7 copy-done.6
  6.3 34.1 %gather.1 = (bf16[4,2,1024,128]{3,2,1,0:T(8,128)(2,1)S(1)}, bf16[64,2,128,128]{3,2,1,0:T(8,128)(2,1)S(1)}, f32[4,8,128]{2,1,0:T(8,128)S(1)}) custom-call(bf16[128,1024]{1,0:T(8,128)(2,1)S(1)} %copy-done, s32[1,128]{1,0:T(1,128)S(1)} %bitcast.1, bf16[128,128]{1,0:T(8,128)(2,1)S(1)} %copy-done.3, bf16[128,128]{1,0:T(8,128)(2,1)S(1)} %copy-done.4, ...), custom_call_target="tpu_custom_call" | custom-call | tf_op jit(solution)/shard_map/gather/pallas_call | solution.py:610
  40.4 0.0 copy-start.5
  40.4 0.7 copy-done.5
  41.1 14.8 %stats.1.part_ref = f32[2,4,1024]{2,1,0:T(4,128)S(1)} custom-call(s32[256]{0:T(256)S(1)} %copy-done.5, s32[1]{0:T(128)S(6)} %copy.14.win, bf16[4,2,1024,128]{3,2,1,0:T(8,128)(2,1)S(1)} %get-tuple-element.8.qg_ref, bf16[64,2,128,128]{3,2,1,0:T(8,128)(2,1)S(1)} %get-tuple-element.9.kv_ref), custom_call_target="tpu_custom_call" | custom-call | tf_op jit(solution)/shard_map/stats/pallas_call | solution.py:631
  55.9 6.4 %norm.1.norm_ref = f32[4,1024]{1,0:T(4,128)S(1)} custom-call(f32[2,4,1024]{2,1,0:T(4,128)S(1)} %stats.1.part_ref), custom_call_target="tpu_custom_call" | custom-call | tf_op jit(solution)/shard_map/norm/pallas_call | solution.py:649
  62.3 27.4 %grads.1 = (bf16[4,128,1024]{2,1,0:T(8,128)(2,1)S(1)}, bf16[64,128,256]{2,1,0:T(8,128)(2,1)S(1)}) custom-call(s32[256]{0:T(256)S(1)} %copy-done.5, s32[1]{0:T(128)S(6)} %copy.14.win, bf16[4,2,1024,128]{3,2,1,0:T(8,128)(2,1)S(1)} %get-tuple-element.8.qg_ref, bf16[64,2,128,128]{3,2,1,0:T(8,128)(2,1)S(1)} %get-tuple-element.9.kv_ref, ...), custom_call_target="tpu_custom_call" | custom-call | tf_op jit(solution)/shard_map/grads/pallas_call | solution.py:661
  89.7 38.8 %reduce.1 = (bf16[128,1024]{1,0:T(8,128)(2,1)S(1)}, bf16[128,128]{1,0:T(8,128)(2,1)S(1)}, bf16[128,128]{1,0:T(8,128)(2,1)S(1)}) custom-call(bf16[4,128,1024]{2,1,0:T(8,128)(2,1)S(1)} %get-tuple-element.11.dq_ref, bf16[64,128,256]{2,1,0:T(8,128)(2,1)S(1)} %get-tuple-element.12.kv_ref), custom_call_target="tpu_custom_call" | custom-call | tf_op jit(solution)/shard_map/reduce/pallas_call | solution.py:681
  128.5 0.7 copy.15
  129.2 0.6 copy.16
  129.8 0.6 copy.17
Async XLA Ops:
  1.3 1.0 copy-start
  2.2 0.9 copy-start.1
  3.2 0.9 copy-start.2
  4.1 0.8 copy-start.3
  4.9 0.8 copy-start.4
  5.6 0.7 copy-start.6
  40.4 0.7 copy-start.5

commit v4 on v3

--- a/solution.py
+++ b/solution.py
@@ -36,13 +36,21 @@
     return core * 32 + y * 8 + z
 
 
+def key_slot(y, z, core):
+    return core * 32 + z * 4 + y
+
+
+def slot_of_key(k):
+    return slot_of(k % 4, (k // 4) % 8, k // 32)
+
+
 def key_positions(order, k_pos):
     row = lax.axis_index("row")
 
-    def one(s, c):
-        y, z, core = (s // 8) % 4, s % 8, s // 32
+    def one(k, c):
+        y, z, core = k % 4, (k // 4) % 8, k // 32
         stored = (y * 8 + (z // 2) * 2 + core) * 8 + (row // 2) * 2 + z % 2
-        k_pos[s] = order[stored] * STRIPE
+        k_pos[k] = order[stored] * STRIPE
         return c
 
     lax.fori_loop(0, NK, one, 0, unroll=8)
@@ -93,8 +101,15 @@
     return lax.dot_general(a, b, (((1,), (0,)), ((), ())), preferred_element_type=jnp.float32)
 
 
-def stats_kernel(order, win, qg_ref, kv_ref, out_ref, k_pos, idx, gap, m_ref, l_ref):
+def fetch(src, dst, sem):
+    copy = pltpu.make_async_copy(src, dst, sem)
+    copy.start()
+    copy.wait()
+
+
+def stats_kernel(win, order_in, q_ref, k_ref, out_ref, order, order_sem, k_pos, idx, gap, m_ref, l_ref):
     window = win[0]
+    fetch(order_in, order, order_sem)
     key_positions(order, k_pos)
 
     def per_query(j, carry):
@@ -103,11 +118,11 @@
         l_ref[...] = jnp.zeros_like(l_ref)
 
         def step(group, first, c):
-            keys = jnp.concatenate([kv_ref[idx[first + i], 0] for i in range(group)], axis=0)
+            keys = jnp.concatenate([k_ref[idx[first + i]] for i in range(group)], axis=0)
             mask = tile_mask([gap[first + i] for i in range(group)], window)
             for b in range(HEADS // 2):
                 cols = pl.ds(b * 256, 256)
-                s = dot_nt(keys, qg_ref[j, 0, cols, :])
+                s = dot_nt(keys, q_ref[j, cols, :])
                 s = jnp.where(mask, s, NEG).reshape(group * 16, 8, 256)
                 m_old = m_ref[:, cols]
                 m_new = jnp.maximum(m_old, jnp.max(s, axis=0))
@@ -128,10 +143,17 @@
 
 
 def grads_kernel(
-    order, win, qg_ref, kv_ref, norm_ref, delta_ref, dq_ref, dkv_ref, k_pos, idx, gap, acc_ref, dq_acc, stat_ref
+    win, order_in, q_ref, k_ref, v_ref, norm_ref, delta_ref, g0, g1, g2, g3, dq_ref, dkv_ref,
+    order, order_sem, k_pos, idx, gap, g_ref, acc_ref, dq_acc, stat_ref,
 ):
     window = win[0]
+    fetch(order_in, order, order_sem)
     key_positions(order, k_pos)
+    for n, block in enumerate((g0, g1, g2, g3)):
+        who = (lax.axis_index("row") // 2 + n) % 4
+        for h in range(HEADS):
+            cols = slice(h * DIM, (h + 1) * DIM)
+            g_ref[who, cols, :] = block[:, cols]
 
     def clear(k, c):
         acc_ref[k] = jnp.zeros((STRIPE, 2 * DIM), jnp.float32)
@@ -148,24 +170,25 @@
 
         def step(group, first, c):
             at = [idx[first + i] for i in range(group)]
-            keys = jnp.concatenate([kv_ref[i, 0] for i in at], axis=0)
-            vals = jnp.concatenate([kv_ref[i, 1] for i in at], axis=0)
+            slots = [slot_of_key(k) for k in at]
+            keys = jnp.concatenate([k_ref[k] for k in at], axis=0)
+            vals = jnp.concatenate([v_ref[k] for k in slots], axis=0)
             keys_t = jnp.transpose(keys)
             mask = tile_mask([gap[first + i] for i in range(group)], window)
             weights, score_grads = [], []
             for b in range(HEADS // 2):
                 cols = pl.ds(b * 256, 256)
-                s = dot_nt(keys, qg_ref[j, 0, cols, :])
+                s = dot_nt(keys, q_ref[j, cols, :])
                 p = jnp.where(mask, jnp.exp2(s * SCALE2 - stat_ref[0:1, cols]), 0.0)
-                w = dot_nt(vals, qg_ref[j, 1, cols, :])
+                w = dot_nt(vals, g_ref[j, cols, :])
                 score_grads.append((p * (w - stat_ref[1:2, cols])).astype(jnp.bfloat16))
                 weights.append(p.astype(jnp.bfloat16))
             weights = jnp.concatenate(weights, axis=1)
             score_grads = jnp.concatenate(score_grads, axis=1)
-            dv = dot_nn(weights, qg_ref[j, 1])
-            dk = dot_nn(score_grads, qg_ref[j, 0])
+            dv = dot_nn(weights, g_ref[j])
+            dk = dot_nn(score_grads, q_ref[j])
             dq_acc[...] += dot_nn(keys_t, score_grads)
-            for i, k in enumerate(at):
+            for i, k in enumerate(slots):
                 rows = slice(i * STRIPE, (i + 1) * STRIPE)
                 acc_ref[k, :, 0:DIM] += dk[rows]
                 acc_ref[k, :, DIM:] += dv[rows]
@@ -207,139 +230,141 @@
 
 
 def gather_kernel(
-    q_in, exp_in, k_in, v_in, o_in, g_in, qg_out, kv_out, delta_out,
-    q_ref, exp_ref, o_ref, g_ref, kv_own, qg_own, delta_own,
-    kv_recv, z_send, y_send, y_pass, sib_send, x_send, x_pass, x_recv, d_send, d_recv, local, load,
+    q_in, exp_in, k_in, v_in, o_in, g_in, q_out, k_out, v_out, delta_out,
+    q_ref, exp_ref, o_ref, g_ref, k_own, v_own, q_own, delta_own,
+    ky_send, ky_recv, kz_send, kz_recv, ks_send, ks_recv,
+    vz_send, vz_recv, vy_send, vy_recv, vy_pass, vs_send, vs_recv,
+    x_send, x_recv, d_send, d_recv, local, load,
 ):
-    loads = [
-        pltpu.make_async_copy(src, dst, load.at[n])
-        for n, (src, dst) in enumerate(
-            ((k_in, kv_own.at[0]), (v_in, kv_own.at[1]), (exp_in, exp_ref), (q_in, q_ref), (g_in, g_ref), (o_in, o_ref))
-        )
-    ]
+    pairs = ((k_in, k_own), (v_in, v_own), (exp_in, exp_ref), (q_in, q_ref), (g_in, g_ref), (o_in, o_ref))
+    loads = [pltpu.make_async_copy(src, dst, load.at[n]) for n, (src, dst) in enumerate(pairs)]
     for copy in loads:
         copy.start()
 
     x, y, z, core = coords()
-    mine = slot_of(y, z, core)
     sibling = device(x, y, z, 1 - core)
-    y_up, y_down = (y + 1) % 4, (y + 3) % 4
     sign = 1 - 2 * core
     x_to, x_from = (x + sign + 4) % 4, (x - sign + 4) % 4
+    y_to, y_from = (y + sign + 4) % 4, (y - sign + 4) % 4
+    y_ways = (device(x, (y + 1) % 4, z, core), device(x, (y + 3) % 4, z, core))
+    z_ways = (device(x, y, (z + 1) % 8, core), device(x, y, (z + 7) % 8, core))
 
     greet(
-        [device(x, y, z, 1 - core)]
+        [sibling]
         + [device((x + d) % 4, y, z, core) for d in (1, 3, 2)]
-        + [device(x, (y + d) % 4, z, core) for d in (1, 3)]
-        + [device(x, y, (z + d) % 8, core) for d in (1, 7)]
+        + list(y_ways)
+        + list(z_ways)
     )
 
-    def slot_copy(s, src, send, to):
-        return remote(src, kv_out.at[s], send, kv_recv.at[s], to)
-
-    def arrived(s):
-        slot_copy(s, kv_own, local.at[0], sibling).wait_recv()
-
-    def z_copy(d, src, up):
-        to = device(x, y, (z + (1 if up else 7)) % 8, core)
-        return slot_copy(slot_of(y, (z + d) % 8, core), src, z_send.at[d, 0 if up else 1], to)
-
-    def y_copy(d, src, up):
-        to = device(x, y_up if up else y_down, z, core)
-        return slot_copy(slot_of(y, (z + d) % 8, core), src, y_send.at[d, 0 if up else 1], to)
-
-    def y_onward(d, up):
-        s = slot_of(y_down if up else y_up, (z + d) % 8, core)
-        return slot_copy(s, kv_out.at[s], y_pass.at[d], device(x, y_up if up else y_down, z, core))
-
-    def sib_copy(s, src):
-        return slot_copy(s, src, sib_send.at[s % 32], sibling)
-
-    def spread(d, src):
-        y_copy(d, src, True).start()
-        y_copy(d, src, False).start()
-        sib_copy(slot_of(y, (z + d) % 8, core), src).start()
+    def ky_copy(yy, src, n, to):
+        return remote(src, k_out.at[key_slot(yy, z, core)], ky_send.at[n], ky_recv.at[yy], to)
+
+    def ky_arrived(yy):
+        ky_copy(yy, k_own, 0, sibling).wait_recv()
+
+    def column(d, c):
+        return k_out.at[pl.ds(key_slot(0, (z + d) % 8, c), 4)]
+
+    def kz_copy(d, way):
+        block = column(d, core)
+        return remote(block, block, kz_send.at[d, way], kz_recv.at[(z + d) % 8], z_ways[way])
+
+    def ks_copy(d, c):
+        block = column(d, c)
+        return remote(block, block, ks_send.at[(z + d) % 8], ks_recv.at[(z + d) % 8], sibling)
+
+    def vz_copy(d, src, way):
+        zz = (z + d) % 8
+        return remote(src, v_out.at[slot_of(y, zz, core)], vz_send.at[d, way], vz_recv.at[zz], z_ways[way])
+
+    def vz_arrived(d):
+        vz_copy(d, v_own, 0).wait_recv()
+
+    def half(yy, n):
+        return v_out.at[pl.ds(slot_of(yy, 4 * n, core), 4)]
+
+    def vy_copy(yy, n, sem, to):
+        return remote(half(yy, n), half(yy, n), sem, vy_recv.at[yy, n], to)
+
+    def vs_copy(yy, c):
+        block = v_out.at[pl.ds(slot_of(yy, 0, c), 8)]
+        return remote(block, block, vs_send.at[yy], vs_recv.at[yy], sibling)
+
+    def q_copy(who, src, n, to):
+        return remote(src, q_out.at[who], x_send.at[n], x_recv.at[who], to)
+
+    def q_arrived(who):
+        q_copy(who, q_own, 0, sibling).wait_recv()
 
     loads[0].wait()
+    for n in range(2):
+        ky_copy(y, k_own, n, y_ways[n]).start()
+    own_k = pltpu.make_async_copy(k_own, k_out.at[key_slot(y, z, core)], local.at[0])
+    own_k.start()
     loads[1].wait()
-    z_copy(0, kv_own, True).start()
-    z_copy(0, kv_own, False).start()
-    spread(0, kv_own)
+    for n in range(2):
+        vz_copy(0, v_own, n).start()
+    own_v = pltpu.make_async_copy(v_own, v_out.at[slot_of(y, z, core)], local.at[1])
+    own_v.start()
 
     loads[2].wait()
     loads[3].wait()
     scale = jnp.transpose(jnp.broadcast_to(jnp.exp2(exp_ref[...].astype(jnp.float32)), (STRIPE, STRIPE)))
-
-    def x_copy(p, n):
-        to = device((x + 1 + 2 * n) % 4, y, z, core)
-        return remote(qg_own.at[p], qg_out.at[x, p], x_send.at[p, n], x_recv.at[x, p], to)
-
     for h in range(HEADS):
         cols = slice(h * DIM, (h + 1) * DIM)
-        qg_own[0, cols, :] = (q_ref[:, cols].astype(jnp.float32) * scale).astype(jnp.bfloat16)
-    x_copy(0, 0).start()
-    x_copy(0, 1).start()
-
-    def x_arrived(who, p):
-        remote(qg_own.at[p], qg_out.at[who, p], local.at[0], x_recv.at[who, p], sibling).wait_recv()
-
-    def x_forward(p):
-        block = qg_out.at[x_from, p]
-        return remote(block, block, x_pass.at[p], x_recv.at[x_from, p], device(x_to, y, z, core))
-
-    def from_z(d, up, onward):
-        s = slot_of(y, (z + d) % 8, core)
-        arrived(s)
-        if onward is True:
-            z_copy(d, kv_out.at[s], up).start()
-        elif onward is not None:
-            @pl.when(onward)
-            def _():
-                z_copy(d, kv_out.at[s], up).start()
-        spread(d, kv_out.at[s])
-
-    def from_y(d):
-        zz = (z + d) % 8
-        below, above = slot_of(y_down, zz, core), slot_of(y_up, zz, core)
-        arrived(below)
-        if d < 4:
-            y_onward(d, True).start()
-        sib_copy(below, kv_out.at[below]).start()
-        arrived(above)
-        if d >= 4:
-            y_onward(d, False).start()
-        sib_copy(above, kv_out.at[above]).start()
+        q_own[cols, :] = (q_ref[:, cols].astype(jnp.float32) * scale).astype(jnp.bfloat16)
+    for n in range(2):
+        q_copy(x, q_own, n, device((x + 1 + 2 * n) % 4, y, z, core)).start()
+    own_q = pltpu.make_async_copy(q_own, q_out.at[x], local.at[2])
+    own_q.start()
+
+    def pass_values(d, way):
+        vz_arrived(d)
+        vz_copy(d, v_out.at[slot_of(y, (z + d) % 8, core)], way).start()
+
+    ky_arrived(y_from)
+    block = k_out.at[key_slot(y_from, z, core)]
+    ky_copy(y_from, block, 2, device(x, y_to, z, core)).start()
+    pass_values(7, 0)
+    pass_values(1, 1)
+    ky_arrived(y_to)
+    ky_arrived((y + 2) % 4)
+    own_k.wait()
+    kz_copy(0, 0).start()
+    kz_copy(0, 1).start()
+    pass_values(6, 0)
+    pass_values(2, 1)
+    ks_copy(0, core).start()
+    vz_arrived(5)
+    vz_arrived(3)
+
+    @pl.when(core == 0)
+    def _():
+        vz_copy(5, v_out.at[slot_of(y, (z + 5) % 8, core)], 0).start()
+
+    @pl.when(core == 1)
+    def _():
+        vz_copy(3, v_out.at[slot_of(y, (z + 3) % 8, core)], 1).start()
+
+    def kz_arrived(d):
+        kz_copy(d, 0).wait_recv()
+
+    def pass_keys(d, way):
+        kz_arrived(d)
+        kz_copy(d, way).start()
+        ks_copy(d, core).start()
+
+    vz_arrived(4)
+    own_v.wait()
+    for n in range(2):
+        vy_copy(y, n, vy_send.at[n, n], y_ways[n]).start()
+    for n in range(2):
+        vy_copy(y, 1 - n, vy_send.at[1 - n, n], y_ways[n]).start()
+    vs_copy(y, core).start()
+    pass_keys(7, 0)
+    pass_keys(1, 1)
 
     loads[4].wait()
-    for h in range(HEADS):
-        cols = slice(h * DIM, (h + 1) * DIM)
-        qg_own[1, cols, :] = g_ref[:, cols]
-
-    from_z(7, True, True)
-    from_z(1, False, True)
-
-    own_kv = pltpu.make_async_copy(kv_own, kv_out.at[mine], local.at[0])
-    own_qg = pltpu.make_async_copy(qg_own, qg_out.at[x], local.at[1])
-    own_kv.start()
-    own_qg.start()
-
-    from_z(6, True, True)
-    from_z(2, False, True)
-    from_y(0)
-
-    x_arrived(x_from, 0)
-    x_forward(0).start()
-    x_copy(1, 0).start()
-    x_copy(1, 1).start()
-
-    from_z(5, True, core == 0)
-    from_z(3, False, core == 1)
-    from_y(1)
-    from_y(7)
-    from_z(4, True, None)
-    from_y(2)
-    from_y(6)
-
     loads[5].wait()
     for h in range(HEADS):
         cols = slice(h * DIM, (h + 1) * DIM)
@@ -352,65 +377,82 @@
 
     for n in range(3):
         d_copy(n).start()
-    own_delta = pltpu.make_async_copy(delta_own, delta_out.at[x], local.at[2])
+    own_delta = pltpu.make_async_copy(delta_own, delta_out.at[x], local.at[3])
     own_delta.start()
 
-    from_y(3)
-    from_y(5)
-    from_y(4)
-    x_arrived(x_from, 1)
-    x_forward(1).start()
-
-    for d in (0, 1, 7, 2, 6, 3, 5, 4):
-        s = slot_of((y + 2) % 4, (z + d) % 8, core)
-        arrived(s)
-        sib_copy(s, kv_out.at[s]).start()
-
-    for p in range(2):
-        x_arrived(x_to, p)
-        x_arrived((x + 2) % 4, p)
+    q_arrived(x_from)
+    q_copy(x_from, q_out.at[x_from], 2, device(x_to, y, z, core)).start()
+
+    pass_keys(6, 0)
+    pass_keys(2, 1)
+
+    def vy_arrived(yy, n):
+        vy_copy(yy, n, local.at[0], sibling).wait_recv()
+
+    beside = ((y + 3) % 4, (y + 1) % 4)
+    for n in range(2):
+        vy_arrived(beside[n], n)
+        vy_copy(beside[n], n, vy_pass.at[n], y_ways[n]).start()
+
+    kz_arrived(5)
+    kz_arrived(3)
+
+    @pl.when(core == 0)
+    def _():
+        kz_copy(5, 0).start()
+
+    @pl.when(core == 1)
+    def _():
+        kz_copy(3, 1).start()
+
+    ks_copy(5, core).start()
+    ks_copy(3, core).start()
+    for n in range(2):
+        vy_arrived(beside[n], 1 - n)
+        vs_copy(beside[n], core).start()
+    kz_arrived(4)
+    ks_copy(4, core).start()
+    for n in range(2):
+        vy_arrived((y + 2) % 4, n)
+    vs_copy((y + 2) % 4, core).start()
+
+    q_arrived(x_to)
+    q_arrived((x + 2) % 4)
     for n in range(1, 4):
         who = (x + n) % 4
         remote(delta_own, delta_out.at[who], local.at[0], d_recv.at[who], sibling).wait_recv()
-
-    def from_sibling(s, c):
-        arrived((1 - core) * 32 + s)
-        return c
-
-    lax.fori_loop(0, 32, from_sibling, 0)
-
-    def sent(d, c):
-        y_copy(d, kv_own, True).wait_send()
-        y_copy(d, kv_own, False).wait_send()
-        slot_copy(mine, kv_own, y_pass.at[d], sibling).wait_send()
-        return c
-
-    lax.fori_loop(0, 8, sent, 0)
-
-    def sib_sent(s, c):
-        sib_copy(s, kv_own).wait_send()
-        return c
-
-    lax.fori_loop(0, 32, sib_sent, 0)
-    for d, up in ((0, True), (0, False), (7, True), (1, False), (6, True), (2, False)):
-        z_copy(d, kv_own, up).wait_send()
+    for d in range(8):
+        ks_copy(d, 1 - core).wait_recv()
+    for yy in range(4):
+        vs_copy(yy, 1 - core).wait_recv()
+
+    for n in range(3):
+        ky_copy(y, k_own, n, sibling).wait_send()
+        q_copy(x, q_own, n, sibling).wait_send()
+        d_copy(n).wait_send()
+    for d, way in ((0, 0), (0, 1), (7, 0), (1, 1), (6, 0), (2, 1)):
+        kz_copy(d, way).wait_send()
+        vz_copy(d, v_own, way).wait_send()
 
     @pl.when(core == 0)
     def _():
-        z_copy(5, kv_own, True).wait_send()
+        kz_copy(5, 0).wait_send()
+        vz_copy(5, v_own, 0).wait_send()
 
     @pl.when(core == 1)
     def _():
-        z_copy(3, kv_own, False).wait_send()
-
-    for p in range(2):
-        x_copy(p, 0).wait_send()
-        x_copy(p, 1).wait_send()
-        x_forward(p).wait_send()
-    for n in range(3):
-        d_copy(n).wait_send()
-    own_kv.wait()
-    own_qg.wait()
+        kz_copy(3, 1).wait_send()
+        vz_copy(3, v_own, 1).wait_send()
+
+    for n in range(2):
+        vy_copy(y, n, vy_send.at[n, 0], sibling).wait_send()
+        vy_copy(y, n, vy_send.at[n, 1], sibling).wait_send()
+        vy_copy(y, n, vy_pass.at[n], sibling).wait_send()
+    for d in range(8):
+        ks_copy(d, core).wait_send()
+    for yy in range(4):
+        vs_copy(yy, core).wait_send()
+    own_q.wait()
     own_delta.wait()
 
 
@@ -609,31 +651,36 @@
 def gather_call(queries, exps, keys, values, outs, grads):
     return pl.pallas_call(
         gather_kernel,
-        out_shape=(bf16(NQ, 2, WIDE, DIM), bf16(NK, 2, STRIPE, DIM), f32(NQ, HEADS, STRIPE)),
+        out_shape=(bf16(NQ, WIDE, DIM), bf16(NK, STRIPE, DIM), bf16(NK, STRIPE, DIM), f32(NQ, HEADS, STRIPE)),
         in_specs=[hbm()] * 6,
-        out_specs=(hbm(), hbm(), hbm()),
+        out_specs=(hbm(),) * 4,
         scratch_shapes=[
             pltpu.VMEM((STRIPE, WIDE), jnp.bfloat16),
             pltpu.VMEM((1, STRIPE), jnp.int32),
             pltpu.VMEM((STRIPE, WIDE), jnp.bfloat16),
             pltpu.VMEM((STRIPE, WIDE), jnp.bfloat16),
-            pltpu.VMEM((2, STRIPE, DIM), jnp.bfloat16),
-            pltpu.VMEM((2, WIDE, DIM), jnp.bfloat16),
+            pltpu.VMEM((STRIPE, DIM), jnp.bfloat16),
+            pltpu.VMEM((STRIPE, DIM), jnp.bfloat16),
+            pltpu.VMEM((WIDE, DIM), jnp.bfloat16),
             pltpu.VMEM((HEADS, STRIPE), jnp.float32),
-            dma(NK), dma(8, 2), dma(8, 2), dma(8), dma(32), dma(2, 2), dma(2), dma(NQ, 2), dma(3), dma(NQ), dma(3), dma(6),
+            dma(3), dma(4), dma(8, 2), dma(8), dma(8), dma(8),
+            dma(8, 2), dma(8), dma(2, 2), dma(4, 2), dma(2), dma(4), dma(4),
+            dma(3), dma(NQ), dma(3), dma(NQ), dma(4), dma(6),
         ],
         compiler_params=params(0, 8),
         name="gather",
     )(queries, exps, keys, values, outs, grads)
 
 
-def stats_call(order, win, qg, kv):
+def stats_call(win, order, q, k):
     return pl.pallas_call(
         stats_kernel,
         out_shape=f32(2, NQ, WIDE),
-        in_specs=[smem()] * 2 + [vmem()] * 2,
+        in_specs=[smem(), hbm()] + [vmem()] * 2,
         out_specs=vmem(),
         scratch_shapes=[
+            pltpu.SMEM((256,), jnp.int32),
+            pltpu.SemaphoreType.DMA,
             pltpu.SMEM((NK,), jnp.int32),
             pltpu.SMEM((NK + 1,), jnp.int32),
             pltpu.SMEM((NK + 1,), jnp.int32),
@@ -642,7 +689,7 @@
         ],
         compiler_params=params(None, 16),
         name="stats",
-    )(order, win, qg, kv)
+    )(win, order, q, k)
 
 
 def norm_call(part):
@@ -657,23 +704,26 @@
     )(part)
 
 
-def grads_call(order, win, qg, kv, norm, delta):
+def grads_call(win, order, q, k, v, norm, delta, *grads):
     return pl.pallas_call(
         grads_kernel,
         out_shape=(bf16(NQ, DIM, WIDE), bf16(NK, STRIPE, 2 * DIM)),
-        in_specs=[smem()] * 2 + [vmem()] * 4,
+        in_specs=[smem(), hbm()] + [vmem()] * 9,
         out_specs=(vmem(), vmem()),
         scratch_shapes=[
+            pltpu.SMEM((256,), jnp.int32),
+            pltpu.SemaphoreType.DMA,
             pltpu.SMEM((NK,), jnp.int32),
             pltpu.SMEM((NK + 1,), jnp.int32),
             pltpu.SMEM((NK + 1,), jnp.int32),
+            pltpu.VMEM((NQ, WIDE, DIM), jnp.bfloat16),
             pltpu.VMEM((NK, STRIPE, 2 * DIM), jnp.float32),
             pltpu.VMEM((DIM, WIDE), jnp.float32),
             pltpu.VMEM((2, WIDE), jnp.float32),
         ],
         compiler_params=params(None, 32),
         name="grads",
-    )(order, win, qg, kv, norm, delta)
+    )(win, order, q, k, v, norm, delta, *grads)
 
 
 def reduce_call(dq, dkv):
@@ -704,12 +754,16 @@
 def per_device(
     queries, query_exps, key_head, value_head, forward_out, output_grad, stripe_order, window_size
 ):
-    qg, kv, delta = gather_call(
-        queries, query_exps.reshape(1, STRIPE), key_head, value_head, forward_out, output_grad
-    )
-    part = stats_call(stripe_order, window_size, qg, kv)
+    held = [pltpu.with_memory_space_constraint(a, pltpu.HBM) for a in (
+        queries, query_exps.reshape(1, STRIPE), key_head, value_head, forward_out, output_grad, stripe_order
+    )]
+    grads = [output_grad] + [
+        lax.ppermute(output_grad, "row", [(r, (r + 8 - 2 * n) % 8) for r in range(8)]) for n in (1, 2, 3)
+    ]
+    q, k, v, delta = gather_call(*held[:6])
+    part = stats_call(window_size, held[6], q, k)
     norm = norm_call(part)
-    dq, dkv = grads_call(stripe_order, window_size, qg, kv, norm, delta)
+    dq, dkv = grads_call(window_size, held[6], q, k, v, norm, delta, *grads)
     return reduce_call(dq, dkv)
 
 

time: 131 us -> 132 us (level)
  the two profiles are of different devices: /device:TPU:6 before, /device:TPU:1 now
where the time goes in v4:
time: 132 us
  Pallas kernels  123 us (93%)
  starting transfers between devices  5.13 us (4%)
  local copies, waits for them, and re-layouts  1.94 us (1%)
  between operations  1.37 us (1%)
    pallas_call x1, Pallas kernels, gather_call(): pl.pallas_call(gather_kernel, out_shape=(bf16(NQ, WIDE, DIM), bf16(NK, ST...  39.5 us
    pallas_call x1, Pallas kernels, reduce_call(): pl.pallas_call(reduce_kernel, out_shape=(bf16(STRIPE, WIDE), bf16(STRIPE,...  39.3 us
    pallas_call x1, Pallas kernels, grads_call(): pl.pallas_call(grads_kernel, out_shape=(bf16(NQ, DIM, WIDE), bf16(NK, STR...  25.6 us
    pallas_call x1, Pallas kernels, stats_call(): pl.pallas_call(stats_kernel, out_shape=f32(2, NQ, WIDE), in_specs=[smem()...  13.9 us
    ppermute x3, starting transfers between devices, per_device(): lax.ppermute(output_grad, 'row', [(r, (r + 8 - 2 * n) % 8) for r in range...  5.13 us
    pallas_call x1, Pallas kernels, norm_call(): pl.pallas_call(norm_kernel, out_shape=f32(NQ, WIDE), in_specs=[vmem()], o...  4.93 us
  transfers between devices with their start and end apart: 3, of which 0 were waited for; matrix products, arithmetic and copies ran while one was open for 0% of the time, Pallas kernels for 44%

profile of v4, /device:TPU:1, one launch (start us, length us, event | category | flops | bytes accessed | tf_op | source)
XLA Modules:
  0.0 131.7 jit_solution(16920561246150181074)
XLA Ops:
  0.6 0.0 copy-start
  0.6 3.7 %collective-permute-start.1 = (bf16[128,1024]{1,0:T(8,128)(2,1)}, bf16[128,1024]{1,0:T(8,128)(2,1)S(1)}, u32[]{:S(2)}, u32[]{:S(2)}) collective-permute-start(bf16[128,1024]{1,0:T(8,128)(2,1)} %g0.1), channel_id=1, source_target_pairs={{0,128},{32,160},{64,192},{96,224},{128,0},{160,32},{192,64},{224,... | collective-permute-start | bytes 786440 | tf_op jit(solution)/shard_map/ppermute | solution.py:761
  4.3 0.9 collective-permute-start
  5.2 0.6 collective-permute-start.2
  6.4 39.5 %gather.1 = (bf16[4,1024,128]{2,1,0:T(8,128)(2,1)S(1)}, bf16[64,128,128]{2,1,0:T(8,128)(2,1)S(1)}, bf16[64,128,128]{2,1,0:T(8,128)(2,1)S(1)}, f32[4,8,128]{2,1,0:T(8,128)S(1)}) custom-call(bf16[128,1024]{1,0:T(8,128)(2,1)} %q_in.1, s32[1,128]{1,0:T(1,128)} %bitcast.1, bf16[128,128]{1,0:T(8,128)(2,1)} %k_in.1, bf16[128,128]{1,0:T(8,128)(2,1)} %v_in.1, ...), custom_call_target="tpu_custom_call" | custom-call | tf_op jit(solution)/shard_map/gather/pallas_call | solution.py:652
  45.9 13.9 %stats.1.part_ref = f32[2,4,1024]{2,1,0:T(4,128)S(1)} custom-call(s32[1]{0:T(128)S(6)} %copy.14.win, s32[256]{0:T(256)} %order_in.3, bf16[4,1024,128]{2,1,0:T(8,128)(2,1)S(1)} %get-tuple-element.9.q_ref, bf16[64,128,128]{2,1,0:T(8,128)(2,1)S(1)} %get-tuple-element.10.k_ref), custom_call_target="tpu_custom_call" | custom-call | tf_op jit(solution)/shard_map/stats/pallas_call | solution.py:676
  59.9 4.9 %norm.1.norm_ref = f32[4,1024]{1,0:T(4,128)S(1)} custom-call(f32[2,4,1024]{2,1,0:T(4,128)S(1)} %stats.1.part_ref), custom_call_target="tpu_custom_call" | custom-call | tf_op jit(solution)/shard_map/norm/pallas_call | solution.py:696
  64.8 0.0 collective-permute-done.1.g2
  64.8 0.0 collective-permute-done.g1
  64.8 0.0 collective-permute-done.2.g3
  64.8 0.0 copy-done
  64.8 25.6 %grads.1 = (bf16[4,128,1024]{2,1,0:T(8,128)(2,1)S(1)}, bf16[64,128,256]{2,1,0:T(8,128)(2,1)S(1)}) custom-call(s32[1]{0:T(128)S(6)} %copy.14.win, s32[256]{0:T(256)} %order_in.3, bf16[4,1024,128]{2,1,0:T(8,128)(2,1)S(1)} %get-tuple-element.9.q_ref, bf16[64,128,128]{2,1,0:T(8,128)(2,1)S(1)} %get-tuple-element.10.k_ref, ...), custom_call_target="tpu_custom_call" | custom-call | tf_op jit(solution)/shard_map/grads/pallas_call | solution.py:708
  90.4 39.3 %reduce.1 = (bf16[128,1024]{1,0:T(8,128)(2,1)S(1)}, bf16[128,128]{1,0:T(8,128)(2,1)S(1)}, bf16[128,128]{1,0:T(8,128)(2,1)S(1)}) custom-call(bf16[4,128,1024]{2,1,0:T(8,128)(2,1)S(1)} %get-tuple-element.13.dq_ref, bf16[64,128,256]{2,1,0:T(8,128)(2,1)S(1)} %get-tuple-element.14.kv_ref), custom_call_target="tpu_custom_call" | custom-call | tf_op jit(solution)/shard_map/reduce/pallas_call | solution.py:731
  129.7 0.7 copy.15
  130.4 0.6 copy.16
  131.0 0.6 copy.17
Async XLA Ops:
  0.6 64.2 %copy-start = (bf16[128,1024]{1,0:T(8,128)(2,1)S(1)}, bf16[128,1024]{1,0:T(8,128)(2,1)}, u32[]{:S(2)}) copy-start(bf16[128,1024]{1,0:T(8,128)(2,1)} %g0.1) | copy-start | bytes 786436
  0.6 64.2 %collective-permute-start.1 = (bf16[128,1024]{1,0:T(8,128)(2,1)}, bf16[128,1024]{1,0:T(8,128)(2,1)S(1)}, u32[]{:S(2)}, u32[]{:S(2)}) collective-permute-start(bf16[128,1024]{1,0:T(8,128)(2,1)} %g0.1), channel_id=1, source_target_pairs={{0,128},{32,160},{64,192},{96,224},{128,0},{160,32},{192,64},{224,... | collective-permute-start | bytes 786440 | tf_op jit(solution)/shard_map/ppermute | solution.py:761
  4.3 60.5 %collective-permute-start = (bf16[128,1024]{1,0:T(8,128)(2,1)}, bf16[128,1024]{1,0:T(8,128)(2,1)S(1)}, u32[]{:S(2)}, u32[]{:S(2)}) collective-permute-start(bf16[128,1024]{1,0:T(8,128)(2,1)} %g0.1), channel_id=1, source_target_pairs={{0,192},{32,224},{64,0},{96,32},{128,64},{160,96},{192,128},{224,1... | collective-permute-start | bytes 786440 | tf_op jit(solution)/shard_map/ppermute | solution.py:761
  5.2 59.7 %collective-permute-start.2 = (bf16[128,1024]{1,0:T(8,128)(2,1)}, bf16[128,1024]{1,0:T(8,128)(2,1)S(1)}, u32[]{:S(2)}, u32[]{:S(2)}) collective-permute-start(bf16[128,1024]{1,0:T(8,128)(2,1)} %g0.1), channel_id=1, source_target_pairs={{0,64},{32,96},{64,128},{96,160},{128,192},{160,224},{192,0},{224,... | collective-permute-start | bytes 786440 | tf_op jit(solution)/shard_map/ppermute | solution.py:761

commit v5 on v3

--- a/solution.py
+++ b/solution.py
@@ -67,10 +67,14 @@
     return n
 
 
-def over_list(n, step):
-    fours = n // 4
-    lax.fori_loop(0, fours, lambda t, c: step(4, 4 * t, c), 0)
-    lax.fori_loop(2 * fours, (n + 1) // 2, lambda t, c: step(2, 2 * t, c), 0)
+def over_list(n, step, most):
+    done = 0
+    while most > 2:
+        full = n // most
+        lax.fori_loop(done * 2 // most, full, lambda t, c, most=most: step(most, most * t, c), 0)
+        done = full * (most // 2)
+        most //= 2
+    lax.fori_loop(done, (n + 1) // 2, lambda t, c: step(2, 2 * t, c), 0)
 
 
 def tile_mask(gaps, window):
@@ -93,8 +97,15 @@
     return lax.dot_general(a, b, (((1,), (0,)), ((), ())), preferred_element_type=jnp.float32)
 
 
-def stats_kernel(order, win, qg_ref, kv_ref, out_ref, k_pos, idx, gap, m_ref, l_ref):
+def fetch(src, dst, sem):
+    copy = pltpu.make_async_copy(src, dst, sem)
+    copy.start()
+    copy.wait()
+
+
+def stats_kernel(win, order_in, qg_ref, kv_ref, out_ref, order, order_sem, k_pos, idx, gap, m_ref, l_ref):
     window = win[0]
+    fetch(order_in, order, order_sem)
     key_positions(order, k_pos)
 
     def per_query(j, carry):
@@ -116,28 +127,31 @@
                 m_ref[:, cols] = m_new
             return c
 
-        over_list(n, step)
+        over_list(n, step, 8)
         m_all = m_ref[...]
         top = jnp.max(m_all, axis=0, keepdims=True)
         total = jnp.sum(l_ref[...] * jnp.exp2((m_all - top) * SCALE2), axis=0, keepdims=True)
-        out_ref[0, pl.ds(j, 1), :] = top
-        out_ref[1, pl.ds(j, 1), :] = total
+        out_ref[pl.ds(j, 1), :] = top * SCALE2 + jnp.log2(jnp.maximum(total, 1e-30))
         return carry
 
     lax.fori_loop(0, NQ, per_query, 0)
 
 
 def grads_kernel(
-    order, win, qg_ref, kv_ref, norm_ref, delta_ref, dq_ref, dkv_ref, k_pos, idx, gap, acc_ref, dq_acc, stat_ref
+    win, order_in, qg_ref, kv_ref, norm_ref, delta_ref, dq_ref, dkv_ref,
+    order, order_sem, k_pos, idx, gap, acc_ref, dq_acc, stat_ref,
 ):
     window = win[0]
-    key_positions(order, k_pos)
+    load = pltpu.make_async_copy(order_in, order, order_sem)
+    load.start()
 
     def clear(k, c):
         acc_ref[k] = jnp.zeros((STRIPE, 2 * DIM), jnp.float32)
         return c
 
     lax.fori_loop(0, NK, clear, 0)
+    load.wait()
+    key_positions(order, k_pos)
 
     def per_query(j, carry):
         n = build_list(query_position(order, j), k_pos, window, idx, gap)
@@ -171,7 +185,7 @@
                 acc_ref[k, :, DIM:] += dv[rows]
             return c
 
-        over_list(n, step)
+        over_list(n, step, 4)
         dq_ref[j] = (dq_acc[...] * SCALE).astype(jnp.bfloat16)
         return carry
 
@@ -240,17 +254,20 @@
     def arrived(s):
         slot_copy(s, kv_own, local.at[0], sibling).wait_recv()
 
-    def z_copy(d, src, up):
+    y_far = (y + 2) % 4
+
+    def z_copy(d, src, up, far=0):
         to = device(x, y, (z + (1 if up else 7)) % 8, core)
-        return slot_copy(slot_of(y, (z + d) % 8, core), src, z_send.at[d, 0 if up else 1], to)
+        s = slot_of(y_far if far else y, (z + d) % 8, core)
+        return slot_copy(s, src, z_send.at[far, d, 0 if up else 1], to)
 
     def y_copy(d, src, up):
         to = device(x, y_up if up else y_down, z, core)
         return slot_copy(slot_of(y, (z + d) % 8, core), src, y_send.at[d, 0 if up else 1], to)
 
-    def y_onward(d, up):
-        s = slot_of(y_down if up else y_up, (z + d) % 8, core)
-        return slot_copy(s, kv_out.at[s], y_pass.at[d], device(x, y_up if up else y_down, z, core))
+    def y_onward():
+        s = slot_of((y - sign + 4) % 4, z, core)
+        return slot_copy(s, kv_out.at[s], y_pass, device(x, (y + sign + 4) % 4, z, core))
 
     def sib_copy(s, src):
         return slot_copy(s, src, sib_send.at[s % 32], sibling)
@@ -279,6 +296,12 @@
         qg_own[0, cols, :] = (q_ref[:, cols].astype(jnp.float32) * scale).astype(jnp.bfloat16)
     x_copy(0, 0).start()
     x_copy(0, 1).start()
+    loads[4].wait()
+    for h in range(HEADS):
+        cols = slice(h * DIM, (h + 1) * DIM)
+        qg_own[1, cols, :] = g_ref[:, cols]
+    x_copy(1, 0).start()
+    x_copy(1, 1).start()
 
     def x_arrived(who, p):
         remote(qg_own.at[p], qg_out.at[who, p], local.at[0], x_recv.at[who, p], sibling).wait_recv()
@@ -300,23 +323,29 @@
 
     def from_y(d):
         zz = (z + d) % 8
-        below, above = slot_of(y_down, zz, core), slot_of(y_up, zz, core)
-        arrived(below)
-        if d < 4:
-            y_onward(d, True).start()
-        sib_copy(below, kv_out.at[below]).start()
-        arrived(above)
-        if d >= 4:
-            y_onward(d, False).start()
-        sib_copy(above, kv_out.at[above]).start()
-
-    loads[4].wait()
-    for h in range(HEADS):
-        cols = slice(h * DIM, (h + 1) * DIM)
-        qg_own[1, cols, :] = g_ref[:, cols]
+        for yy in (y_down, y_up):
+            s = slot_of(yy, zz, core)
+            arrived(s)
+            if d == 0:
+                @pl.when(yy == (y - sign + 4) % 4)
+                def _():
+                    y_onward().start()
+            sib_copy(s, kv_out.at[s]).start()
+
+    def from_far(d, up, onward):
+        s = slot_of(y_far, (z + d) % 8, core)
+        arrived(s)
+        if onward is True:
+            z_copy(d, kv_out.at[s], up, 1).start()
+        elif onward is not None:
+            @pl.when(onward)
+            def _():
+                z_copy(d, kv_out.at[s], up, 1).start()
+        sib_copy(s, kv_out.at[s]).start()
 
     from_z(7, True, True)
     from_z(1, False, True)
+    from_y(0)
 
     own_kv = pltpu.make_async_copy(kv_own, kv_out.at[mine], local.at[0])
     own_qg = pltpu.make_async_copy(qg_own, qg_out.at[x], local.at[1])
@@ -325,20 +354,17 @@
 
     from_z(6, True, True)
     from_z(2, False, True)
-    from_y(0)
-
-    x_arrived(x_from, 0)
-    x_forward(0).start()
-    x_copy(1, 0).start()
-    x_copy(1, 1).start()
-
+    from_far(0, True, True)
+    z_copy(0, kv_out.at[slot_of(y_far, z, core)], False, 1).start()
     from_z(5, True, core == 0)
     from_z(3, False, core == 1)
     from_y(1)
     from_y(7)
+    from_far(7, True, True)
+    from_far(1, False, True)
     from_z(4, True, None)
-    from_y(2)
-    from_y(6)
+    x_arrived(x_from, 0)
+    x_forward(0).start()
 
     loads[5].wait()
     for h in range(HEADS):
@@ -355,16 +381,18 @@
     own_delta = pltpu.make_async_copy(delta_own, delta_out.at[x], local.at[2])
     own_delta.start()
 
+    from_y(2)
+    from_y(6)
+    from_far(6, True, True)
+    from_far(2, False, True)
+    x_arrived(x_from, 1)
+    x_forward(1).start()
     from_y(3)
     from_y(5)
+    from_far(5, True, core == 0)
+    from_far(3, False, core == 1)
     from_y(4)
-    x_arrived(x_from, 1)
-    x_forward(1).start()
-
-    for d in (0, 1, 7, 2, 6, 3, 5, 4):
-        s = slot_of((y + 2) % 4, (z + d) % 8, core)
-        arrived(s)
-        sib_copy(s, kv_out.at[s]).start()
+    from_far(4, True, None)
 
     for p in range(2):
         x_arrived(x_to, p)
@@ -382,7 +410,6 @@
     def sent(d, c):
         y_copy(d, kv_own, True).wait_send()
         y_copy(d, kv_own, False).wait_send()
-        slot_copy(mine, kv_own, y_pass.at[d], sibling).wait_send()
         return c
 
     lax.fori_loop(0, 8, sent, 0)
@@ -392,16 +419,20 @@
         return c
 
     lax.fori_loop(0, 32, sib_sent, 0)
-    for d, up in ((0, True), (0, False), (7, True), (1, False), (6, True), (2, False)):
-        z_copy(d, kv_own, up).wait_send()
+    y_onward().wait_send()
+    for far in range(2):
+        for d, up in ((0, True), (0, False), (7, True), (1, False), (6, True), (2, False)):
+            z_copy(d, kv_own, up, far).wait_send()
 
     @pl.when(core == 0)
     def _():
-        z_copy(5, kv_own, True).wait_send()
+        z_copy(5, kv_own, True, 0).wait_send()
+        z_copy(5, kv_own, True, 1).wait_send()
 
     @pl.when(core == 1)
     def _():
-        z_copy(3, kv_own, False).wait_send()
+        z_copy(3, kv_own, False, 0).wait_send()
+        z_copy(3, kv_own, False, 1).wait_send()
 
     for p in range(2):
         x_copy(p, 0).wait_send()
@@ -427,11 +458,9 @@
     for n in range(1, 4):
         who = (x + n) % 4
         remote(part_ref, got.at[who], send.at[0], recv.at[who], peers[0]).wait_recv()
-    tops = [part_ref[0]] + [got[(x + n) % 4, 0] for n in range(1, 4)]
-    sums = [part_ref[1]] + [got[(x + n) % 4, 1] for n in range(1, 4)]
-    top = functools.reduce(jnp.maximum, tops)
-    total = functools.reduce(jnp.add, [s * jnp.exp2((t - top) * SCALE2) for t, s in zip(tops, sums)])
-    out_ref[...] = top * SCALE2 + jnp.log2(total)
+    logs = [part_ref[...]] + [got[(x + n) % 4] for n in range(1, 4)]
+    top = functools.reduce(jnp.maximum, logs)
+    out_ref[...] = top + jnp.log2(functools.reduce(jnp.add, [jnp.exp2(v - top) for v in logs]))
     for n in range(3):
         copy(n).wait_send()
 
@@ -620,20 +649,22 @@
             pltpu.VMEM((2, STRIPE, DIM), jnp.bfloat16),
             pltpu.VMEM((2, WIDE, DIM), jnp.bfloat16),
             pltpu.VMEM((HEADS, STRIPE), jnp.float32),
-            dma(NK), dma(8, 2), dma(8, 2), dma(8), dma(32), dma(2, 2), dma(2), dma(NQ, 2), dma(3), dma(NQ), dma(3), dma(6),
+            dma(NK), dma(2, 8, 2), dma(8, 2), pltpu.SemaphoreType.DMA, dma(32), dma(2, 2), dma(2), dma(NQ, 2), dma(3), dma(NQ), dma(3), dma(6),
         ],
         compiler_params=params(0, 8),
         name="gather",
     )(queries, exps, keys, values, outs, grads)
 
 
-def stats_call(order, win, qg, kv):
+def stats_call(win, order, qg, kv):
     return pl.pallas_call(
         stats_kernel,
-        out_shape=f32(2, NQ, WIDE),
-        in_specs=[smem()] * 2 + [vmem()] * 2,
+        out_shape=f32(NQ, WIDE),
+        in_specs=[smem(), hbm()] + [vmem()] * 2,
         out_specs=vmem(),
         scratch_shapes=[
+            pltpu.SMEM((256,), jnp.int32),
+            pltpu.SemaphoreType.DMA,
             pltpu.SMEM((NK,), jnp.int32),
             pltpu.SMEM((NK + 1,), jnp.int32),
             pltpu.SMEM((NK + 1,), jnp.int32),
@@ -642,7 +673,7 @@
         ],
         compiler_params=params(None, 16),
         name="stats",
-    )(order, win, qg, kv)
+    )(win, order, qg, kv)
 
 
 def norm_call(part):
@@ -651,19 +682,21 @@
         out_shape=f32(NQ, WIDE),
         in_specs=[vmem()],
         out_specs=vmem(),
-        scratch_shapes=[pltpu.VMEM((NQ, 2, NQ, WIDE), jnp.float32), dma(3), dma(NQ)],
+        scratch_shapes=[pltpu.VMEM((NQ, NQ, WIDE), jnp.float32), dma(3), dma(NQ)],
         compiler_params=params(1, 4),
         name="norm",
     )(part)
 
 
-def grads_call(order, win, qg, kv, norm, delta):
+def grads_call(win, order, qg, kv, norm, delta):
     return pl.pallas_call(
         grads_kernel,
         out_shape=(bf16(NQ, DIM, WIDE), bf16(NK, STRIPE, 2 * DIM)),
-        in_specs=[smem()] * 2 + [vmem()] * 4,
+        in_specs=[smem(), hbm()] + [vmem()] * 4,
         out_specs=(vmem(), vmem()),
         scratch_shapes=[
+            pltpu.SMEM((256,), jnp.int32),
+            pltpu.SemaphoreType.DMA,
             pltpu.SMEM((NK,), jnp.int32),
             pltpu.SMEM((NK + 1,), jnp.int32),
             pltpu.SMEM((NK + 1,), jnp.int32),
@@ -673,7 +706,7 @@
         ],
         compiler_params=params(None, 32),
         name="grads",
-    )(order, win, qg, kv, norm, delta)
+    )(win, order, qg, kv, norm, delta)
 
 
 def reduce_call(dq, dkv):
@@ -704,12 +737,16 @@
 def per_device(
     queries, query_exps, key_head, value_head, forward_out, output_grad, stripe_order, window_size
 ):
-    qg, kv, delta = gather_call(
-        queries, query_exps.reshape(1, STRIPE), key_head, value_head, forward_out, output_grad
-    )
-    part = stats_call(stripe_order, window_size, qg, kv)
+    held = [
+        pltpu.with_memory_space_constraint(a, pltpu.HBM)
+        for a in (
+            queries, query_exps.reshape(1, STRIPE), key_head, value_head, forward_out, output_grad, stripe_order
+        )
+    ]
+    qg, kv, delta = gather_call(*held[:6])
+    part = stats_call(window_size, held[6], qg, kv)
     norm = norm_call(part)
-    dq, dkv = grads_call(stripe_order, window_size, qg, kv, norm, delta)
+    dq, dkv = grads_call(window_size, held[6], qg, kv, norm, delta)
     return reduce_call(dq, dkv)
 
 

time: 131 us -> 115 us (0.88)
  the two profiles are of different devices: /device:TPU:6 before, /device:TPU:4 now
where the time goes in v5:
time: 115 us
  Pallas kernels  112 us (97%)
  local copies, waits for them, and re-layouts  1.93 us (2%)
  between operations  1.32 us (1%)
    pallas_call x1, Pallas kernels, gather_call(): pl.pallas_call(gather_kernel, out_shape=(bf16(NQ, 2, WIDE, DIM), bf16(NK,...  35.2 us
    pallas_call x1, Pallas kernels, reduce_call(): pl.pallas_call(reduce_kernel, out_shape=(bf16(STRIPE, WIDE), bf16(STRIPE,...  32.4 us
    pallas_call x1, Pallas kernels, grads_call(): pl.pallas_call(grads_kernel, out_shape=(bf16(NQ, DIM, WIDE), bf16(NK, STR...  25 us
    pallas_call x1, Pallas kernels, stats_call(): pl.pallas_call(stats_kernel, out_shape=f32(NQ, WIDE), in_specs=[smem(), h...  13.8 us
    pallas_call x1, Pallas kernels, norm_call(): pl.pallas_call(norm_kernel, out_shape=f32(NQ, WIDE), in_specs=[vmem()], o...  5.71 us

profile of v5, /device:TPU:4, one launch (start us, length us, event | category | flops | bytes accessed | tf_op | source)
XLA Modules:
  0.0 115.3 jit_solution(12622448395036768966)
XLA Ops:
  1.3 35.2 %gather.1 = (bf16[4,2,1024,128]{3,2,1,0:T(8,128)(2,1)S(1)}, bf16[64,2,128,128]{3,2,1,0:T(8,128)(2,1)S(1)}, f32[4,8,128]{2,1,0:T(8,128)S(1)}) custom-call(bf16[128,1024]{1,0:T(8,128)(2,1)} %q_in.1, s32[1,128]{1,0:T(1,128)} %bitcast.1, bf16[128,128]{1,0:T(8,128)(2,1)} %k_in.1, bf16[128,128]{1,0:T(8,128)(2,1)} %v_in.1, bf16[128,1024]{1,0:T(8,128)(2,1)} %o_in.1, ...), custom_call_target="tpu_custom_call" | custom-call | tf_op jit(solution)/shard_map/gather/pallas_call | solution.py:639
  36.4 13.8 %stats.1.part_ref = f32[4,1024]{1,0:T(4,128)S(1)} custom-call(s32[1]{0:T(128)S(6)} %copy.14.win, s32[256]{0:T(256)} %order_in.3, bf16[4,2,1024,128]{3,2,1,0:T(8,128)(2,1)S(1)} %get-tuple-element.8.qg_ref, bf16[64,2,128,128]{3,2,1,0:T(8,128)(2,1)S(1)} %get-tuple-element.9.kv_ref), custom_call_target="tpu_custom_call" | custom-call | tf_op jit(solution)/shard_map/stats/pallas_call | solution.py:660
  50.2 5.7 %norm.1.norm_ref = f32[4,1024]{1,0:T(4,128)S(1)} custom-call(f32[4,1024]{1,0:T(4,128)S(1)} %stats.1.part_ref), custom_call_target="tpu_custom_call" | custom-call | tf_op jit(solution)/shard_map/norm/pallas_call | solution.py:680
  55.9 25.0 %grads.1 = (bf16[4,128,1024]{2,1,0:T(8,128)(2,1)S(1)}, bf16[64,128,256]{2,1,0:T(8,128)(2,1)S(1)}) custom-call(s32[1]{0:T(128)S(6)} %copy.14.win, s32[256]{0:T(256)} %order_in.3, bf16[4,2,1024,128]{3,2,1,0:T(8,128)(2,1)S(1)} %get-tuple-element.8.qg_ref, bf16[64,2,128,128]{3,2,1,0:T(8,128)(2,1)S(1)} %get-tuple-element.9.kv_ref, f32[4,1024]{1,0:T(4,128)S(1)} %norm.1.norm_ref, ...), custom_call_target="tpu_custom_call" | custom-call | tf_op jit(solution)/shard_map/grads/pallas_call | solution.py:692
  80.9 32.4 %reduce.1 = (bf16[128,1024]{1,0:T(8,128)(2,1)S(1)}, bf16[128,128]{1,0:T(8,128)(2,1)S(1)}, bf16[128,128]{1,0:T(8,128)(2,1)S(1)}) custom-call(bf16[4,128,1024]{2,1,0:T(8,128)(2,1)S(1)} %get-tuple-element.11.dq_ref, bf16[64,128,256]{2,1,0:T(8,128)(2,1)S(1)} %get-tuple-element.12.kv_ref), custom_call_target="tpu_custom_call" | custom-call | tf_op jit(solution)/shard_map/reduce/pallas_call | solution.py:714
  113.3 0.7 copy.15
  114.1 0.6 copy.16
  114.7 0.6 copy.17

commit v6 on v5

--- a/solution.py
+++ b/solution.py
@@ -16,6 +16,7 @@
 NK = 64
 MESH = pl.DeviceIdType.MESH
 NEG = -1e30
+LIMIT = 2.0**100
 FAR = -(1 << 20)
 SCALE = 1.0 / math.sqrt(DIM)
 SCALE2 = math.log2(math.e) / math.sqrt(DIM)
@@ -110,16 +111,20 @@
 
     def per_query(j, carry):
         n = build_list(query_position(order, j), k_pos, window, idx, gap)
-        m_ref[...] = jnp.full_like(m_ref, NEG)
-        l_ref[...] = jnp.zeros_like(l_ref)
-
-        def step(group, first, c):
+
+        def scores(group, first, b):
             keys = jnp.concatenate([kv_ref[idx[first + i], 0] for i in range(group)], axis=0)
+            return dot_nt(keys, qg_ref[j, 0, pl.ds(b * 256, 256), :])
+
+        def restart():
+            m_ref[...] = jnp.full_like(m_ref, NEG)
+            l_ref[...] = jnp.zeros_like(l_ref)
+
+        def online(group, first, c=0):
             mask = tile_mask([gap[first + i] for i in range(group)], window)
             for b in range(HEADS // 2):
                 cols = pl.ds(b * 256, 256)
-                s = dot_nt(keys, qg_ref[j, 0, cols, :])
-                s = jnp.where(mask, s, NEG).reshape(group * 16, 8, 256)
+                s = jnp.where(mask, scores(group, first, b), NEG).reshape(group * 16, 8, 256)
                 m_old = m_ref[:, cols]
                 m_new = jnp.maximum(m_old, jnp.max(s, axis=0))
                 e = jnp.exp2((s - m_new[None]) * SCALE2)
@@ -127,11 +132,49 @@
                 m_ref[:, cols] = m_new
             return c
 
-        over_list(n, step, 8)
-        m_all = m_ref[...]
-        top = jnp.max(m_all, axis=0, keepdims=True)
-        total = jnp.sum(l_ref[...] * jnp.exp2((m_all - top) * SCALE2), axis=0, keepdims=True)
-        out_ref[pl.ds(j, 1), :] = top * SCALE2 + jnp.log2(jnp.maximum(total, 1e-30))
+        def settle():
+            m_all = m_ref[...]
+            top = jnp.max(m_all, axis=0, keepdims=True)
+            l_ref[...] = l_ref[...] * jnp.exp2((m_all - top) * SCALE2)
+            m_ref[...] = jnp.broadcast_to(top * SCALE2, m_all.shape)
+
+        def shifted(group, first, c=0):
+            gaps = [gap[first + i] for i in range(group)]
+
+            def add(masked):
+                mask = tile_mask(gaps, window) if masked else None
+                for b in range(HEADS // 2):
+                    cols = pl.ds(b * 256, 256)
+                    s = scores(group, first, b)
+                    s = jnp.where(mask, s, NEG) if masked else s
+                    e = jnp.exp2(s.reshape(group * 16, 8, 256) * SCALE2 - m_ref[:, cols][None])
+                    l_ref[:, cols] += jnp.sum(e, axis=0)
+
+            whole = functools.reduce(
+                jnp.logical_and, [(g >= STRIPE) & (g <= window - STRIPE) for g in gaps]
+            )
+            pl.when(whole)(lambda: add(False))
+            pl.when(jnp.logical_not(whole))(lambda: add(True))
+            return c
+
+        restart()
+        pl.when(n >= 8)(lambda: online(8, 0) or None)
+        pl.when((n >= 4) & (n < 8))(lambda: online(4, 0) or None)
+        pl.when((n >= 1) & (n < 4))(lambda: online(2, 0) or None)
+        settle()
+        eights, fours = n // 8, n // 4
+        lax.fori_loop(1, eights, lambda t, c: shifted(8, 8 * t, c), 0)
+        lax.fori_loop(jnp.where(n >= 8, 2 * eights, 1), fours, lambda t, c: shifted(4, 4 * t, c), 0)
+        lax.fori_loop(jnp.where(n >= 4, 2 * fours, 1), (n + 1) // 2, lambda t, c: shifted(2, 2 * t, c), 0)
+
+        @pl.when(jnp.max(l_ref[...]) > LIMIT)
+        def _():
+            restart()
+            over_list(n, online, 8)
+            settle()
+
+        total = jnp.sum(l_ref[...], axis=0, keepdims=True)
+        out_ref[pl.ds(j, 1), :] = m_ref[0:1, :] + jnp.log2(jnp.maximum(total, 1e-30))
         return carry
 
     lax.fori_loop(0, NQ, per_query, 0)
@@ -244,8 +287,8 @@
     greet(
         [device(x, y, z, 1 - core)]
         + [device((x + d) % 4, y, z, core) for d in (1, 3, 2)]
-        + [device(x, (y + d) % 4, z, core) for d in (1, 3)]
-        + [device(x, y, (z + d) % 8, core) for d in (1, 7)]
+        + [device(x, (y + d) % 4, z, core) for d in (1, 3, 2)]
+        + [device(x, y, (z + d) % 8, core) for d in (1, 7, 2, 6)]
     )
 
     def slot_copy(s, src, send, to):
@@ -255,19 +298,19 @@
         slot_copy(s, kv_own, local.at[0], sibling).wait_recv()
 
     y_far = (y + 2) % 4
-
-    def z_copy(d, src, up, far=0):
-        to = device(x, y, (z + (1 if up else 7)) % 8, core)
+    z_steps = (1, 7, 2, 6)
+
+    def z_copy(d, src, n, far=0):
+        to = device(x, y, (z + z_steps[n]) % 8, core)
         s = slot_of(y_far if far else y, (z + d) % 8, core)
-        return slot_copy(s, src, z_send.at[far, d, 0 if up else 1], to)
+        return slot_copy(s, src, z_send.at[far, d, n], to)
 
     def y_copy(d, src, up):
         to = device(x, y_up if up else y_down, z, core)
         return slot_copy(slot_of(y, (z + d) % 8, core), src, y_send.at[d, 0 if up else 1], to)
 
-    def y_onward():
-        s = slot_of((y - sign + 4) % 4, z, core)
-        return slot_copy(s, kv_out.at[s], y_pass, device(x, (y + sign + 4) % 4, z, core))
+    def far_copy():
+        return slot_copy(mine, kv_own, y_pass, device(x, y_far, z, core))
 
     def sib_copy(s, src):
         return slot_copy(s, src, sib_send.at[s % 32], sibling)
@@ -279,8 +322,9 @@
 
     loads[0].wait()
     loads[1].wait()
-    z_copy(0, kv_own, True).start()
-    z_copy(0, kv_own, False).start()
+    for n in range(4):
+        z_copy(0, kv_own, n).start()
+    far_copy().start()
     spread(0, kv_own)
 
     loads[2].wait()
@@ -310,59 +354,56 @@
         block = qg_out.at[x_from, p]
         return remote(block, block, x_pass.at[p], x_recv.at[x_from, p], device(x_to, y, z, core))
 
-    def from_z(d, up, onward):
+    def onward(d, n, far):
+        s = slot_of(y_far if far else y, (z + d) % 8, core)
+        if d in (6, 2):
+            z_copy(d, kv_out.at[s], n, far).start()
+        elif d in (5, 3):
+            @pl.when(core == n)
+            def _():
+                z_copy(d, kv_out.at[s], n, far).start()
+
+    def from_z(d):
         s = slot_of(y, (z + d) % 8, core)
         arrived(s)
-        if onward is True:
-            z_copy(d, kv_out.at[s], up).start()
-        elif onward is not None:
-            @pl.when(onward)
-            def _():
-                z_copy(d, kv_out.at[s], up).start()
+        onward(d, 0 if d > 4 else 1, 0)
         spread(d, kv_out.at[s])
 
-    def from_y(d):
-        zz = (z + d) % 8
-        for yy in (y_down, y_up):
-            s = slot_of(yy, zz, core)
-            arrived(s)
-            if d == 0:
-                @pl.when(yy == (y - sign + 4) % 4)
-                def _():
-                    y_onward().start()
-            sib_copy(s, kv_out.at[s]).start()
-
-    def from_far(d, up, onward):
+    def from_far(d):
         s = slot_of(y_far, (z + d) % 8, core)
         arrived(s)
-        if onward is True:
-            z_copy(d, kv_out.at[s], up, 1).start()
-        elif onward is not None:
-            @pl.when(onward)
-            def _():
-                z_copy(d, kv_out.at[s], up, 1).start()
+        onward(d, 0 if d > 4 else 1, 1)
         sib_copy(s, kv_out.at[s]).start()
 
-    from_z(7, True, True)
-    from_z(1, False, True)
-    from_y(0)
+    def from_y(d):
+        for yy in (y_down, y_up):
+            s = slot_of(yy, (z + d) % 8, core)
+            arrived(s)
+            sib_copy(s, kv_out.at[s]).start()
+
+    from_z(7)
+    from_z(1)
+    from_z(6)
+    from_z(2)
 
     own_kv = pltpu.make_async_copy(kv_own, kv_out.at[mine], local.at[0])
     own_qg = pltpu.make_async_copy(qg_own, qg_out.at[x], local.at[1])
     own_kv.start()
     own_qg.start()
 
-    from_z(6, True, True)
-    from_z(2, False, True)
-    from_far(0, True, True)
-    z_copy(0, kv_out.at[slot_of(y_far, z, core)], False, 1).start()
-    from_z(5, True, core == 0)
-    from_z(3, False, core == 1)
+    from_far(0)
+    for n in range(4):
+        z_copy(0, kv_out.at[slot_of(y_far, z, core)], n, 1).start()
+    from_y(0)
+    from_z(5)
+    from_z(3)
+    from_y(7)
     from_y(1)
-    from_y(7)
-    from_far(7, True, True)
-    from_far(1, False, True)
-    from_z(4, True, None)
+    from_far(7)
+    from_far(1)
+    from_far(6)
+    from_far(2)
+    from_z(4)
     x_arrived(x_from, 0)
     x_forward(0).start()
 
@@ -381,18 +422,16 @@
     own_delta = pltpu.make_async_copy(delta_own, delta_out.at[x], local.at[2])
     own_delta.start()
 
+    from_y(6)
     from_y(2)
-    from_y(6)
-    from_far(6, True, True)
-    from_far(2, False, True)
+    from_far(5)
+    from_far(3)
     x_arrived(x_from, 1)
     x_forward(1).start()
+    from_y(5)
     from_y(3)
-    from_y(5)
-    from_far(5, True, core == 0)
-    from_far(3, False, core == 1)
+    from_far(4)
     from_y(4)
-    from_far(4, True, None)
 
     for p in range(2):
         x_arrived(x_to, p)
@@ -419,20 +458,20 @@
         return c
 
     lax.fori_loop(0, 32, sib_sent, 0)
-    y_onward().wait_send()
+    far_copy().wait_send()
     for far in range(2):
-        for d, up in ((0, True), (0, False), (7, True), (1, False), (6, True), (2, False)):
-            z_copy(d, kv_own, up, far).wait_send()
+        for d, n in ((0, 0), (0, 1), (0, 2), (0, 3), (6, 0), (2, 1)):
+            z_copy(d, kv_own, n, far).wait_send()
 
     @pl.when(core == 0)
     def _():
-        z_copy(5, kv_own, True, 0).wait_send()
-        z_copy(5, kv_own, True, 1).wait_send()
+        z_copy(5, kv_own, 0, 0).wait_send()
+        z_copy(5, kv_own, 0, 1).wait_send()
 
     @pl.when(core == 1)
     def _():
-        z_copy(3, kv_own, False, 0).wait_send()
-        z_copy(3, kv_own, False, 1).wait_send()
+        z_copy(3, kv_own, 1, 0).wait_send()
+        z_copy(3, kv_own, 1, 1).wait_send()
 
     for p in range(2):
         x_copy(p, 0).wait_send()
@@ -555,11 +594,11 @@
     for n in range(11):
         if n < 8:
             step_a(far_first[n])
-            step_b(far_first[n])
-        if 0 <= n - 1 < 8:
-            step_c(far_first[n - 1])
-        if 0 <= n - 3 < 7:
-            step_z(far_first[n - 3])
+        if 0 <= n - 2 < 8:
+            step_b(far_first[n - 2])
+            step_c(far_first[n - 2])
+        if 0 <= n - 4 < 7:
+            step_z(far_first[n - 4])
         if n == 6:
             x_a.wait_recv()
             lax.fori_loop(0, 8, sum_x, 0)
@@ -649,7 +688,7 @@
             pltpu.VMEM((2, STRIPE, DIM), jnp.bfloat16),
             pltpu.VMEM((2, WIDE, DIM), jnp.bfloat16),
             pltpu.VMEM((HEADS, STRIPE), jnp.float32),
-            dma(NK), dma(2, 8, 2), dma(8, 2), pltpu.SemaphoreType.DMA, dma(32), dma(2, 2), dma(2), dma(NQ, 2), dma(3), dma(NQ), dma(3), dma(6),
+            dma(NK), dma(2, 8, 4), dma(8, 2), pltpu.SemaphoreType.DMA, dma(32), dma(2, 2), dma(2), dma(NQ, 2), dma(3), dma(NQ), dma(3), dma(6),
         ],
         compiler_params=params(0, 8),
         name="gather",
@@ -734,6 +773,29 @@
     )(dq, dkv)
 
 
+def finish_kernel(a_in, b_in, c_in, a_out, b_out, c_out, sem):
+    copies = [
+        pltpu.make_async_copy(src, dst, sem.at[n])
+        for n, (src, dst) in enumerate(((a_in, a_out), (b_in, b_out), (c_in, c_out)))
+    ]
+    for copy in copies:
+        copy.start()
+    for copy in copies:
+        copy.wait()
+
+
+def finish_call(dq, dk, dv):
+    return pl.pallas_call(
+        finish_kernel,
+        out_shape=(bf16(STRIPE, WIDE), bf16(STRIPE, DIM), bf16(STRIPE, DIM)),
+        in_specs=[hbm()] * 3,
+        out_specs=(hbm(),) * 3,
+        scratch_shapes=[dma(3)],
+        compiler_params=params(None, 4),
+        name="finish",
+    )(dq, dk, dv)
+
+
 def per_device(
     queries, query_exps, key_head, value_head, forward_out, output_grad, stripe_order, window_size
 ):
@@ -747,7 +809,7 @@
     part = stats_call(window_size, held[6], qg, kv)
     norm = norm_call(part)
     dq, dkv = grads_call(window_size, held[6], qg, kv, norm, delta)
-    return reduce_call(dq, dkv)
+    return finish_call(*reduce_call(dq, dkv))
 
 
 def solution(mesh):

time: 115 us -> 117 us (1.017)
  Pallas kernels: 112 us -> 116 us
  local copies, waits for them, and re-layouts: 1.93 us -> 0 us
    pallas_call x1, Pallas kernels: 32.4 us -> 46.4 us  [reduce_call(): pl.pallas_call(reduce_kernel, out_shape=(bf16(STRIPE, WIDE), bf16(STRIPE,...]
    pallas_call x1, Pallas kernels: 25 us -> 17.5 us  [grads_call(): pl.pallas_call(grads_kernel, out_shape=(bf16(NQ, DIM, WIDE), bf16(NK, STR...]
    pallas_call x1, Pallas kernels: 13.8 us -> 10.1 us  [stats_call(): pl.pallas_call(stats_kernel, out_shape=f32(NQ, WIDE), in_specs=[smem(), h...]
    pallas_call x1, Pallas kernels: 5.71 us -> 8.72 us  [norm_call(): pl.pallas_call(norm_kernel, out_shape=f32(NQ, WIDE), in_specs=[vmem()], o...]
    pallas_call x1, Pallas kernels: 35.2 us -> 32.5 us  [gather_call(): pl.pallas_call(gather_kernel, out_shape=(bf16(NQ, 2, WIDE, DIM), bf16(NK,...]
    unnamed x3 -> x0, local copies, waits for them, and re-layouts: 1.93 us -> none
where the time goes in v6:
time: 117 us
  Pallas kernels  116 us (99%)
  between operations  1.32 us (1%)
    pallas_call x1, Pallas kernels, reduce_call(): pl.pallas_call(reduce_kernel, out_shape=(bf16(STRIPE, WIDE), bf16(STRIPE,...  46.4 us
    pallas_call x1, Pallas kernels, gather_call(): pl.pallas_call(gather_kernel, out_shape=(bf16(NQ, 2, WIDE, DIM), bf16(NK,...  32.5 us
    pallas_call x1, Pallas kernels, grads_call(): pl.pallas_call(grads_kernel, out_shape=(bf16(NQ, DIM, WIDE), bf16(NK, STR...  17.5 us
    pallas_call x1, Pallas kernels, stats_call(): pl.pallas_call(stats_kernel, out_shape=f32(NQ, WIDE), in_specs=[smem(), h...  10.1 us
    pallas_call x1, Pallas kernels, norm_call(): pl.pallas_call(norm_kernel, out_shape=f32(NQ, WIDE), in_specs=[vmem()], o...  8.72 us

profile of v6, /device:TPU:4, one launch (start us, length us, event | category | flops | bytes accessed | tf_op | source)
XLA Modules:
  0.0 117.2 jit_solution(12313934471174781585)
XLA Ops:
  1.3 32.5 %gather.1 = (bf16[4,2,1024,128]{3,2,1,0:T(8,128)(2,1)S(1)}, bf16[64,2,128,128]{3,2,1,0:T(8,128)(2,1)S(1)}, f32[4,8,128]{2,1,0:T(8,128)S(1)}) custom-call(bf16[128,1024]{1,0:T(8,128)(2,1)} %q_in.1, s32[1,128]{1,0:T(1,128)} %bitcast.1, bf16[128,128]{1,0:T(8,128)(2,1)} %k_in.1, bf16[128,128]{1,0:T(8,128)(2,1)} %v_in.1, bf16[128,1024]{1,0:T(8,128)(2,1)} %o_in.1, ...), custom_call_target="tpu_custom_call" | custom-call | tf_op jit(solution)/shard_map/gather/pallas_call | solution.py:678
  33.8 10.1 %stats.1.part_ref = f32[4,1024]{1,0:T(4,128)S(1)} custom-call(s32[1]{0:T(128)S(6)} %copy.11.win, s32[256]{0:T(256)} %order_in.3, bf16[4,2,1024,128]{3,2,1,0:T(8,128)(2,1)S(1)} %get-tuple-element.11.qg_ref, bf16[64,2,128,128]{3,2,1,0:T(8,128)(2,1)S(1)} %get-tuple-element.12.kv_ref), custom_call_target="tpu_custom_call" | custom-call | tf_op jit(solution)/shard_map/stats/pallas_call | solution.py:699
  43.9 8.7 %norm.1.norm_ref = f32[4,1024]{1,0:T(4,128)S(1)} custom-call(f32[4,1024]{1,0:T(4,128)S(1)} %stats.1.part_ref), custom_call_target="tpu_custom_call" | custom-call | tf_op jit(solution)/shard_map/norm/pallas_call | solution.py:719
  52.6 17.5 %grads.1 = (bf16[4,128,1024]{2,1,0:T(8,128)(2,1)S(1)}, bf16[64,128,256]{2,1,0:T(8,128)(2,1)S(1)}) custom-call(s32[1]{0:T(128)S(6)} %copy.11.win, s32[256]{0:T(256)} %order_in.3, bf16[4,2,1024,128]{3,2,1,0:T(8,128)(2,1)S(1)} %get-tuple-element.11.qg_ref, bf16[64,2,128,128]{3,2,1,0:T(8,128)(2,1)S(1)} %get-tuple-element.12.kv_ref, f32[4,1024]{1,0:T(4,128)S(1)} %norm.1.norm_ref, ...), custom_call_target="tpu_custom_call" | custom-call | tf_op jit(solution)/shard_map/grads/pallas_call | solution.py:731
  70.1 46.4 %reduce.1 = (bf16[128,1024]{1,0:T(8,128)(2,1)S(1)}, bf16[128,128]{1,0:T(8,128)(2,1)S(1)}, bf16[128,128]{1,0:T(8,128)(2,1)S(1)}) custom-call(bf16[4,128,1024]{2,1,0:T(8,128)(2,1)S(1)} %get-tuple-element.14.dq_ref, bf16[64,128,256]{2,1,0:T(8,128)(2,1)S(1)} %get-tuple-element.15.kv_ref), custom_call_target="tpu_custom_call" | custom-call | tf_op jit(solution)/shard_map/reduce/pallas_call | solution.py:753
  116.5 0.7 finish.1

commit v7 on v6

--- a/solution.py
+++ b/solution.py
@@ -37,34 +37,48 @@
     return core * 32 + y * 8 + z
 
 
-def key_positions(order, k_pos):
-    row = lax.axis_index("row")
+def positions(order, pos):
+    row, col = lax.axis_index("row"), lax.axis_index("col")
 
     def one(s, c):
         y, z, core = (s // 8) % 4, s % 8, s // 32
         stored = (y * 8 + (z // 2) * 2 + core) * 8 + (row // 2) * 2 + z % 2
-        k_pos[s] = order[stored] * STRIPE
+        pos[s] = order[stored] * STRIPE
         return c
 
     lax.fori_loop(0, NK, one, 0, unroll=8)
-
-
-def query_position(order, j):
-    row, col = lax.axis_index("row"), lax.axis_index("col")
-    return order[(j * 2 + row % 2) * 32 + col] * STRIPE
-
-
-def build_list(q_at, k_pos, window, idx, gap):
+    for j in range(NQ):
+        pos[NK + j] = order[(j * 2 + row % 2) * 32 + col] * STRIPE
+
+
+class Listed:
+    def __init__(self, lists, j):
+        self.lists, self.at, self.count_at = lists, j * (NK + 16), 2 * NQ * (NK + 16) + j
+
+    def index(self, n):
+        return self.lists[self.at + n]
+
+    def gap(self, n):
+        return self.lists[NQ * (NK + 16) + self.at + n]
+
+    def put(self, n, index, gap):
+        self.lists[self.at + n] = index
+        self.lists[NQ * (NK + 16) + self.at + n] = gap
+
+    def count(self):
+        return self.lists[self.count_at]
+
+
+def build_list(listed, q_at, pos, window):
     def one(k, n):
-        distance = q_at - k_pos[k]
+        distance = q_at - pos[k]
         seen = (distance >= 0) & (distance - (STRIPE - 1) < window)
-        idx[n] = k
-        gap[n] = distance
+        listed.put(n, k, distance)
         return n + seen.astype(jnp.int32)
 
     n = lax.fori_loop(0, NK, one, jnp.int32(0), unroll=8)
-    idx[n] = 0
-    gap[n] = FAR
+    listed.put(n, 0, FAR)
+    listed.lists[listed.count_at] = n
     return n
 
 
@@ -98,22 +112,15 @@
     return lax.dot_general(a, b, (((1,), (0,)), ((), ())), preferred_element_type=jnp.float32)
 
 
-def fetch(src, dst, sem):
-    copy = pltpu.make_async_copy(src, dst, sem)
-    copy.start()
-    copy.wait()
-
-
-def stats_kernel(win, order_in, qg_ref, kv_ref, out_ref, order, order_sem, k_pos, idx, gap, m_ref, l_ref):
+def stats_kernel(win, pos, qg_ref, kv_ref, out_ref, lists, m_ref, l_ref):
     window = win[0]
-    fetch(order_in, order, order_sem)
-    key_positions(order, k_pos)
 
     def per_query(j, carry):
-        n = build_list(query_position(order, j), k_pos, window, idx, gap)
+        listed = Listed(lists, j)
+        n = build_list(listed, pos[NK + j], pos, window)
 
         def scores(group, first, b):
-            keys = jnp.concatenate([kv_ref[idx[first + i], 0] for i in range(group)], axis=0)
+            keys = jnp.concatenate([kv_ref[listed.index(first + i), 0] for i in range(group)], axis=0)
             return dot_nt(keys, qg_ref[j, 0, pl.ds(b * 256, 256), :])
 
         def restart():
@@ -121,7 +128,7 @@
             l_ref[...] = jnp.zeros_like(l_ref)
 
         def online(group, first, c=0):
-            mask = tile_mask([gap[first + i] for i in range(group)], window)
+            mask = tile_mask([listed.gap(first + i) for i in range(group)], window)
             for b in range(HEADS // 2):
                 cols = pl.ds(b * 256, 256)
                 s = jnp.where(mask, scores(group, first, b), NEG).reshape(group * 16, 8, 256)
@@ -139,7 +146,7 @@
             m_ref[...] = jnp.broadcast_to(top * SCALE2, m_all.shape)
 
         def shifted(group, first, c=0):
-            gaps = [gap[first + i] for i in range(group)]
+            gaps = [listed.gap(first + i) for i in range(group)]
 
             def add(masked):
                 mask = tile_mask(gaps, window) if masked else None
@@ -181,34 +188,30 @@
 
 
 def grads_kernel(
-    win, order_in, qg_ref, kv_ref, norm_ref, delta_ref, dq_ref, dkv_ref,
-    order, order_sem, k_pos, idx, gap, acc_ref, dq_acc, stat_ref,
+    win, lists, qg_ref, kv_ref, norm_ref, delta_ref, dq_ref, dkv_ref,
+    acc_ref, dq_acc, stat_ref,
 ):
     window = win[0]
-    load = pltpu.make_async_copy(order_in, order, order_sem)
-    load.start()
 
     def clear(k, c):
         acc_ref[k] = jnp.zeros((STRIPE, 2 * DIM), jnp.float32)
         return c
 
     lax.fori_loop(0, NK, clear, 0)
-    load.wait()
-    key_positions(order, k_pos)
 
     def per_query(j, carry):
-        n = build_list(query_position(order, j), k_pos, window, idx, gap)
+        listed = Listed(lists, j)
         dq_acc[...] = jnp.zeros_like(dq_acc)
         stat_ref[0:1, :] = norm_ref[pl.ds(j, 1), :]
         for h in range(HEADS):
             stat_ref[1:2, h * DIM : (h + 1) * DIM] = delta_ref[j, h : h + 1, :]
 
         def step(group, first, c):
-            at = [idx[first + i] for i in range(group)]
+            at = [listed.index(first + i) for i in range(group)]
             keys = jnp.concatenate([kv_ref[i, 0] for i in at], axis=0)
             vals = jnp.concatenate([kv_ref[i, 1] for i in at], axis=0)
             keys_t = jnp.transpose(keys)
-            mask = tile_mask([gap[first + i] for i in range(group)], window)
+            mask = tile_mask([listed.gap(first + i) for i in range(group)], window)
             weights, score_grads = [], []
             for b in range(HEADS // 2):
                 cols = pl.ds(b * 256, 256)
@@ -228,7 +231,7 @@
                 acc_ref[k, :, DIM:] += dv[rows]
             return c
 
-        over_list(n, step, 4)
+        over_list(listed.count(), step, 8)
         dq_ref[j] = (dq_acc[...] * SCALE).astype(jnp.bfloat16)
         return carry
 
@@ -264,14 +267,18 @@
 
 
 def gather_kernel(
-    q_in, exp_in, k_in, v_in, o_in, g_in, qg_out, kv_out, delta_out,
+    q_in, exp_in, k_in, v_in, o_in, g_in, order_in, qg_out, kv_out, delta_out, pos,
+    order,
     q_ref, exp_ref, o_ref, g_ref, kv_own, qg_own, delta_own,
     kv_recv, z_send, y_send, y_pass, sib_send, x_send, x_pass, x_recv, d_send, d_recv, local, load,
 ):
     loads = [
         pltpu.make_async_copy(src, dst, load.at[n])
         for n, (src, dst) in enumerate(
-            ((k_in, kv_own.at[0]), (v_in, kv_own.at[1]), (exp_in, exp_ref), (q_in, q_ref), (g_in, g_ref), (o_in, o_ref))
+            (
+                (k_in, kv_own.at[0]), (v_in, kv_own.at[1]), (exp_in, exp_ref), (q_in, q_ref), (g_in, g_ref), (o_in, o_ref),
+                (order_in, order),
+            )
         )
     ]
     for copy in loads:
@@ -421,6 +428,8 @@
         d_copy(n).start()
     own_delta = pltpu.make_async_copy(delta_own, delta_out.at[x], local.at[2])
     own_delta.start()
+    loads[6].wait()
+    positions(order, pos)
 
     from_y(6)
     from_y(2)
@@ -660,6 +669,10 @@
     return jax.ShapeDtypeStruct(shape, jnp.bfloat16)
 
 
+def i32(*shape):
+    return jax.ShapeDtypeStruct(shape, jnp.int32)
+
+
 def f32(*shape):
     return jax.ShapeDtypeStruct(shape, jnp.float32)
 
@@ -674,13 +687,14 @@
     )
 
 
-def gather_call(queries, exps, keys, values, outs, grads):
+def gather_call(queries, exps, keys, values, outs, grads, order):
     return pl.pallas_call(
         gather_kernel,
-        out_shape=(bf16(NQ, 2, WIDE, DIM), bf16(NK, 2, STRIPE, DIM), f32(NQ, HEADS, STRIPE)),
-        in_specs=[hbm()] * 6,
-        out_specs=(hbm(), hbm(), hbm()),
+        out_shape=(bf16(NQ, 2, WIDE, DIM), bf16(NK, 2, STRIPE, DIM), f32(NQ, HEADS, STRIPE), i32(128)),
+        in_specs=[hbm()] * 7,
+        out_specs=(hbm(), hbm(), hbm(), smem()),
         scratch_shapes=[
+            pltpu.SMEM((256,), jnp.int32),
             pltpu.VMEM((STRIPE, WIDE), jnp.bfloat16),
             pltpu.VMEM((1, STRIPE), jnp.int32),
             pltpu.VMEM((STRIPE, WIDE), jnp.bfloat16),
@@ -688,31 +702,26 @@
             pltpu.VMEM((2, STRIPE, DIM), jnp.bfloat16),
             pltpu.VMEM((2, WIDE, DIM), jnp.bfloat16),
             pltpu.VMEM((HEADS, STRIPE), jnp.float32),
-            dma(NK), dma(2, 8, 4), dma(8, 2), pltpu.SemaphoreType.DMA, dma(32), dma(2, 2), dma(2), dma(NQ, 2), dma(3), dma(NQ), dma(3), dma(6),
+            dma(NK), dma(2, 8, 4), dma(8, 2), pltpu.SemaphoreType.DMA, dma(32), dma(2, 2), dma(2), dma(NQ, 2), dma(3), dma(NQ), dma(3), dma(7),
         ],
         compiler_params=params(0, 8),
         name="gather",
-    )(queries, exps, keys, values, outs, grads)
-
-
-def stats_call(win, order, qg, kv):
+    )(queries, exps, keys, values, outs, grads, order)
+
+
+def stats_call(win, pos, qg, kv):
     return pl.pallas_call(
         stats_kernel,
-        out_shape=f32(NQ, WIDE),
-        in_specs=[smem(), hbm()] + [vmem()] * 2,
-        out_specs=vmem(),
+        out_shape=(f32(NQ, WIDE), i32(1024)),
+        in_specs=[smem()] * 2 + [vmem()] * 2,
+        out_specs=(vmem(), smem()),
         scratch_shapes=[
-            pltpu.SMEM((256,), jnp.int32),
-            pltpu.SemaphoreType.DMA,
-            pltpu.SMEM((NK,), jnp.int32),
-            pltpu.SMEM((NK + 1,), jnp.int32),
-            pltpu.SMEM((NK + 1,), jnp.int32),
             pltpu.VMEM((8, WIDE), jnp.float32),
             pltpu.VMEM((8, WIDE), jnp.float32),
         ],
         compiler_params=params(None, 16),
         name="stats",
-    )(win, order, qg, kv)
+    )(win, pos, qg, kv)
 
 
 def norm_call(part):
@@ -727,25 +736,20 @@
     )(part)
 
 
-def grads_call(win, order, qg, kv, norm, delta):
+def grads_call(win, lists, qg, kv, norm, delta):
     return pl.pallas_call(
         grads_kernel,
         out_shape=(bf16(NQ, DIM, WIDE), bf16(NK, STRIPE, 2 * DIM)),
-        in_specs=[smem(), hbm()] + [vmem()] * 4,
+        in_specs=[smem()] * 2 + [vmem()] * 4,
         out_specs=(vmem(), vmem()),
         scratch_shapes=[
-            pltpu.SMEM((256,), jnp.int32),
-            pltpu.SemaphoreType.DMA,
-            pltpu.SMEM((NK,), jnp.int32),
-            pltpu.SMEM((NK + 1,), jnp.int32),
-            pltpu.SMEM((NK + 1,), jnp.int32),
             pltpu.VMEM((NK, STRIPE, 2 * DIM), jnp.float32),
             pltpu.VMEM((DIM, WIDE), jnp.float32),
             pltpu.VMEM((2, WIDE), jnp.float32),
         ],
-        compiler_params=params(None, 32),
+        compiler_params=params(None, 40),
         name="grads",
-    )(win, order, qg, kv, norm, delta)
+    )(win, lists, qg, kv, norm, delta)
 
 
 def reduce_call(dq, dkv):
@@ -805,10 +809,10 @@
             queries, query_exps.reshape(1, STRIPE), key_head, value_head, forward_out, output_grad, stripe_order
         )
     ]
-    qg, kv, delta = gather_call(*held[:6])
-    part = stats_call(window_size, held[6], qg, kv)
+    qg, kv, delta, pos = gather_call(*held)
+    part, lists = stats_call(window_size, pos, qg, kv)
     norm = norm_call(part)
-    dq, dkv = grads_call(window_size, held[6], qg, kv, norm, delta)
+    dq, dkv = grads_call(window_size, lists, qg, kv, norm, delta)
     return finish_call(*reduce_call(dq, dkv))
 
 

time: 117 us -> 129 us (1.10)
  Pallas kernels: 116 us -> 127 us
    pallas_call x1, Pallas kernels: 46.4 us -> 54.6 us  [reduce_call(): pl.pallas_call(reduce_kernel, out_shape=(bf16(STRIPE, WIDE), bf16(STRIPE,...]
    pallas_call x1, Pallas kernels: 17.5 us -> 21 us  [grads_call(): pl.pallas_call(grads_kernel, out_shape=(bf16(NQ, DIM, WIDE), bf16(NK, STR...]
    pallas_call x1, Pallas kernels: 8.72 us -> 6.83 us  [norm_call(): pl.pallas_call(norm_kernel, out_shape=f32(NQ, WIDE), in_specs=[vmem()], o...]
where the time goes in v7:
time: 129 us; the launch traced here: 128 us
  Pallas kernels  127 us (98%)
  between operations  1.48 us (1%)
    pallas_call x1, Pallas kernels, reduce_call(): pl.pallas_call(reduce_kernel, out_shape=(bf16(STRIPE, WIDE), bf16(STRIPE,...  54.6 us
    pallas_call x1, Pallas kernels, gather_call(): pl.pallas_call(gather_kernel, out_shape=(bf16(NQ, 2, WIDE, DIM), bf16(NK,...  33.1 us
    pallas_call x1, Pallas kernels, grads_call(): pl.pallas_call(grads_kernel, out_shape=(bf16(NQ, DIM, WIDE), bf16(NK, STR...  21 us
    pallas_call x1, Pallas kernels, stats_call(): pl.pallas_call(stats_kernel, out_shape=(f32(NQ, WIDE), i32(1024)), in_spe...  10.7 us
    pallas_call x1, Pallas kernels, norm_call(): pl.pallas_call(norm_kernel, out_shape=f32(NQ, WIDE), in_specs=[vmem()], o...  6.83 us

profile of v7, /device:TPU:4, one launch (start us, length us, event | category | flops | bytes accessed | tf_op | source)
XLA Modules:
  0.0 128.5 jit_solution(9083400333113118218)
XLA Ops:
  1.3 33.1 %gather.1 = (bf16[4,2,1024,128]{3,2,1,0:T(8,128)(2,1)S(1)}, bf16[64,2,128,128]{3,2,1,0:T(8,128)(2,1)S(1)}, f32[4,8,128]{2,1,0:T(8,128)S(1)}, s32[128]{0:T(128)S(1)}) custom-call(bf16[128,1024]{1,0:T(8,128)(2,1)} %q_in.1, s32[1,128]{1,0:T(1,128)} %bitcast.1, bf16[128,128]{1,0:T(8,128)(2,1)} %k_in.1, bf16[128,128]{1,0:T(8,128)(2,1)} %v_in.1, ...), custom_call_target="tpu_custom_call" | custom-call | tf_op jit(solution)/shard_map/gather/pallas_call | solution.py:691
  34.4 10.7 %stats.1 = (f32[4,1024]{1,0:T(4,128)S(1)}, s32[1024]{0:T(1024)S(1)}) custom-call(s32[1]{0:T(128)S(6)} %copy.11.win, s32[128]{0:T(128)S(1)} %get-tuple-element.14.pos, bf16[4,2,1024,128]{3,2,1,0:T(8,128)(2,1)S(1)} %get-tuple-element.15.qg_ref, bf16[64,2,128,128]{3,2,1,0:T(8,128)(2,1)S(1)} %get-tuple-element.16.kv_ref), custom_call_target="tpu_custom_call" | custom-call | tf_op jit(solution)/shard_map/stats/pallas_call | solution.py:713
  45.1 6.8 %norm.1.norm_ref = f32[4,1024]{1,0:T(4,128)S(1)} custom-call(f32[4,1024]{1,0:T(4,128)S(1)} %get-tuple-element.18.part_ref), custom_call_target="tpu_custom_call" | custom-call | tf_op jit(solution)/shard_map/norm/pallas_call | solution.py:728
  52.0 21.0 %grads.1 = (bf16[4,128,1024]{2,1,0:T(8,128)(2,1)S(1)}, bf16[64,128,256]{2,1,0:T(8,128)(2,1)S(1)}) custom-call(s32[1]{0:T(128)S(6)} %copy.11.win, s32[1024]{0:T(1024)S(1)} %get-tuple-element.17.lists, bf16[4,2,1024,128]{3,2,1,0:T(8,128)(2,1)S(1)} %get-tuple-element.15.qg_ref, bf16[64,2,128,128]{3,2,1,0:T(8,128)(2,1)S(1)} %get-tuple-element.16.kv_ref, ...), custom_call_target="tpu_custom_call" | custom-call | tf_op jit(solution)/shard_map/grads/pallas_call | solution.py:740
  73.0 54.6 %reduce.1 = (bf16[128,1024]{1,0:T(8,128)(2,1)S(1)}, bf16[128,128]{1,0:T(8,128)(2,1)S(1)}, bf16[128,128]{1,0:T(8,128)(2,1)S(1)}) custom-call(bf16[4,128,1024]{2,1,0:T(8,128)(2,1)S(1)} %get-tuple-element.20.dq_ref, bf16[64,128,256]{2,1,0:T(8,128)(2,1)S(1)} %get-tuple-element.21.kv_ref), custom_call_target="tpu_custom_call" | custom-call | tf_op jit(solution)/shard_map/reduce/pallas_call | solution.py:757
  127.6 0.7 finish.1
